TPU v7x, 32 devices: a whole 2x2x4 slice. The times are simulated.
32 devices in a mesh: edge: 8 (over z, y), grp: 4 (over x, core).
Axes of the slice: x: 2, y: 2, z: 4, core: 2. Of those that a mesh axis runs over, the one named last changes fastest.
Arguments:
- edge_lat: bfloat16 [4, 8192, 512], P('grp', 'edge'), may hold values from -6 to 6
- node_lat: bfloat16 [4, 512, 512], P('grp', 'edge'), may hold values from -6 to 6
- edge_cot: bfloat16 [4, 8192, 512], P('grp', 'edge'), may hold values from -3 to 3
- node_cot: bfloat16 [4, 512, 512], P('grp', 'edge'), may hold values from -9 to 9
- senders: int32 [4, 8192], P('grp', 'edge'), may hold values from 0 to 511
- receivers: int32 [4, 8192], P('grp', 'edge'), may hold values from 0 to 511
- edge_count: int32 [4, 8], P('grp', 'edge'), may hold values from 512 to 1024, as said below
- w_edge_in: float32 [1536, 512], P(('edge', 'grp')), may hold values from -0.15625 to 0.15625
- w_edge_out: float32 [512, 512], P(('edge', 'grp')), may hold values from -0.25 to 0.25
- w_node_in: float32 [1024, 512], P(('edge', 'grp'))
- w_node_out: float32 [512, 512], P(('edge', 'grp')), may hold values from -0.25 to 0.25
- small_params: float32 [8, 512], P(None, ('edge', 'grp'))
- first_edge_in: float32 [1536, 512], P(('edge', 'grp'))
- first_edge_out: float32 [512, 512], P(('edge', 'grp'))
- first_node_in: float32 [1024, 512], P(('edge', 'grp'))
- first_node_out: float32 [512, 512], P(('edge', 'grp'))
- first_small: float32 [8, 512], P(None, ('edge', 'grp'))
- second_edge_in: float32 [1536, 512], P(('edge', 'grp')), as said below
- second_edge_out: float32 [512, 512], P(('edge', 'grp'))
- second_node_in: float32 [1024, 512], P(('edge', 'grp'))
- second_node_out: float32 [512, 512], P(('edge', 'grp'))
- second_small: float32 [8, 512], P(None, ('edge', 'grp'))
Outputs:
- edge_new: bfloat16 [4, 8192, 512], P('grp', 'edge')
- node_new: bfloat16 [4, 512, 512], P('grp', 'edge')
- edge_grad: bfloat16 [4, 8192, 512], P('grp', 'edge')
- node_grad: bfloat16 [4, 512, 512], P('grp', 'edge')
- grad_edge_in: float32 [1536, 512], P(('edge', 'grp'))
- grad_edge_out: float32 [512, 512], P(('edge', 'grp'))
- grad_node_in: float32 [1024, 512], P(('edge', 'grp'))
- grad_node_out: float32 [512, 512], P(('edge', 'grp'))
- grad_small: float32 [8, 512], P(None, ('edge', 'grp'))
- second_edge_in_new: float32 [1536, 512], P(('edge', 'grp'))
- second_edge_out_new: float32 [512, 512], P(('edge', 'grp'))
- second_node_in_new: float32 [1024, 512], P(('edge', 'grp'))
- second_node_out_new: float32 [512, 512], P(('edge', 'grp'))
- second_small_new: float32 [8, 512], P(None, ('edge', 'grp'))
- w_edge_in_new: float32 [1536, 512], P(('edge', 'grp'))
- w_edge_out_new: float32 [512, 512], P(('edge', 'grp'))
- w_node_in_new: float32 [1024, 512], P(('edge', 'grp'))
- w_node_out_new: float32 [512, 512], P(('edge', 'grp'))
- small_new: float32 [8, 512], P(None, ('edge', 'grp'))
Inputs may be any that keep to these rules, and one draw needn't show every extreme that they name: `edge_count`: in each sample one shard has all 1024 slots live; live slots come first in a shard. `senders`: node index within the sample's multimesh, also in padded slots. `receivers`: node index within the sample's multimesh, also in padded slots. `second_edge_in`: Positive.
All inputs are finite; a program needn't handle non-finite values.
Results may differ from a plain program's by a relative error of at most 0.011.
Values may be sent and summed in bfloat16 or wider, within the bound.
A program may use at most 128 MiB of HBM per device.

v0:
```python
import jax
import jax.numpy as jnp
from jax import lax
from jax.sharding import PartitionSpec as P

step_count = 10.0


def inner(left, right):
    return lax.dot_general(
        left, right, (((0,), (0,)), ((), ())), preferred_element_type=jnp.float32
    )


def times_t(left, right):
    return lax.dot_general(
        left, right, (((1,), (1,)), ((), ())), preferred_element_type=jnp.float32
    )


def norm_stats(values):
    mean = jnp.mean(values, axis=-1, keepdims=True)
    centred = values - mean
    var = jnp.mean(centred * centred, axis=-1, keepdims=True)
    rstd = lax.rsqrt(var + 1e-05)
    return (centred * rstd, rstd)


def norm_back(grad_out, normed, rstd, gain):
    scaled = grad_out * gain
    return rstd * (
        scaled
        - jnp.mean(scaled, axis=-1, keepdims=True)
        - normed * jnp.mean(scaled * normed, axis=-1, keepdims=True)
    )


def silu_slope(values):
    sig = jax.nn.sigmoid(values)
    return sig * (1.0 + values * (1.0 - sig))


def adamw(weight, grad, first, second, rate):
    first_new = 0.9 * first + 0.1 * grad
    second_new = 0.999 * second + 0.001 * grad * grad
    mhat = first_new / (1.0 - 0.9**step_count)
    vhat = second_new / (1.0 - 0.999**step_count)
    return (weight - rate * (mhat / (jnp.sqrt(vhat) + 1e-08) + 0.1 * weight), second_new)


def on_device(
    edge_lat,
    node_lat,
    edge_cot,
    node_cot,
    senders,
    receivers,
    edge_count,
    w_edge_in,
    w_edge_out,
    w_node_in,
    w_node_out,
    small_params,
    first_edge_in,
    first_edge_out,
    first_node_in,
    first_node_out,
    first_small,
    second_edge_in,
    second_edge_out,
    second_node_in,
    second_node_out,
    second_small,
):
    bf = jnp.bfloat16
    edges = edge_lat[0]
    nodes = node_lat[0]
    send = senders[0]
    recv = receivers[0]
    rows = edges.shape[0]
    width = edges.shape[1]
    maskf = (jnp.arange(rows, dtype=jnp.int32) < edge_count[0, 0]).astype(jnp.float32)[:, None]
    w1e, w2e, w1n, w2n, small = (
        lax.all_gather(w_edge_in.astype(bf), ("edge", "grp"), axis=0, tiled=True),
        lax.all_gather(w_edge_out.astype(bf), ("edge", "grp"), axis=0, tiled=True),
        lax.all_gather(w_node_in.astype(bf), ("edge", "grp"), axis=0, tiled=True),
        lax.all_gather(w_node_out.astype(bf), ("edge", "grp"), axis=0, tiled=True),
        lax.all_gather(small_params.astype(bf), ("edge", "grp"), axis=1, tiled=True),
    )
    params = small.astype(jnp.float32)
    whole = lax.all_gather(nodes, "edge", axis=0, tiled=True)
    node_total = whole.shape[0]
    joined = jnp.concatenate([edges, whole[send], whole[recv]], axis=1)
    pre = jnp.dot(joined, w1e, preferred_element_type=jnp.float32) + params[0]
    hidden = jax.nn.silu(pre).astype(bf)
    out = jnp.dot(hidden, w2e, preferred_element_type=jnp.float32) + params[1]
    normed, rstd = norm_stats(out)
    edge_new = edges.astype(jnp.float32) + maskf * (normed * params[2] + params[3])
    dense = jnp.zeros((node_total, width), jnp.float32).at[recv].add(maskf * edge_new)
    agg = lax.psum_scatter(dense, "edge", scatter_dimension=0, tiled=True)
    node_in = jnp.concatenate([nodes, agg.astype(bf)], axis=1)
    pre_n = jnp.dot(node_in, w1n, preferred_element_type=jnp.float32) + params[4]
    hidden_n = jax.nn.silu(pre_n).astype(bf)
    out_n = jnp.dot(hidden_n, w2n, preferred_element_type=jnp.float32) + params[5]
    normed_n, rstd_n = norm_stats(out_n)
    node_new = nodes.astype(jnp.float32) + normed_n * params[6] + params[7]
    grad_node_out_f = node_cot[0].astype(jnp.float32)
    d_out_n = norm_back(grad_node_out_f, normed_n, rstd_n, params[6]).astype(bf)
    gain_n = jnp.sum(grad_node_out_f * normed_n, axis=0)
    shift_n = jnp.sum(grad_node_out_f, axis=0)
    g_w2n = inner(hidden_n, d_out_n)
    g_b2n = jnp.sum(d_out_n.astype(jnp.float32), axis=0)
    d_pre_n = (times_t(d_out_n, w2n) * silu_slope(pre_n)).astype(bf)
    g_w1n = inner(node_in, d_pre_n)
    g_b1n = jnp.sum(d_pre_n.astype(jnp.float32), axis=0)
    d_node_in = times_t(d_pre_n, w1n)
    node_part = grad_node_out_f + d_node_in[:, :width]
    d_agg = d_node_in[:, width:].astype(bf)
    agg_rows = lax.all_gather(d_agg, "edge", axis=0, tiled=True)
    d_edge = edge_cot[0].astype(jnp.float32) + maskf * agg_rows[recv].astype(jnp.float32)
    masked = maskf * d_edge
    d_out = norm_back(masked, normed, rstd, params[2]).astype(bf)
    gain_e = jnp.sum(masked * normed, axis=0)
    shift_e = jnp.sum(masked, axis=0)
    g_w2e = inner(hidden, d_out)
    g_b2e = jnp.sum(d_out.astype(jnp.float32), axis=0)
    d_pre = (times_t(d_out, w2e) * silu_slope(pre)).astype(bf)
    g_w1e = inner(joined, d_pre)
    g_b1e = jnp.sum(d_pre.astype(jnp.float32), axis=0)
    d_joined = times_t(d_pre, w1e)
    edge_grad = (d_edge + d_joined[:, :width]).astype(bf)
    dense_grad = jnp.zeros((node_total, width), jnp.float32)
    dense_grad = (
        dense_grad.at[send]
        .add(d_joined[:, width : 2 * width])
        .at[recv]
        .add(d_joined[:, 2 * width :])
    )
    node_sum = lax.psum_scatter(dense_grad, "edge", scatter_dimension=0, tiled=True)
    node_grad = (node_part + node_sum).astype(bf)
    g_small = jnp.stack([g_b1e, g_b2e, gain_e, shift_e, g_b1n, g_b2n, gain_n, shift_n])
    grads = (
        lax.psum_scatter(g_w1e, ("edge", "grp"), scatter_dimension=0, tiled=True),
        lax.psum_scatter(g_w2e, ("edge", "grp"), scatter_dimension=0, tiled=True),
        lax.psum_scatter(g_w1n, ("edge", "grp"), scatter_dimension=0, tiled=True),
        lax.psum_scatter(g_w2n, ("edge", "grp"), scatter_dimension=0, tiled=True),
        lax.psum_scatter(g_small, ("edge", "grp"), scatter_dimension=1, tiled=True),
    )
    weights = (w_edge_in, w_edge_out, w_node_in, w_node_out, small_params)
    firsts = (first_edge_in, first_edge_out, first_node_in, first_node_out, first_small)
    seconds = (second_edge_in, second_edge_out, second_node_in, second_node_out, second_small)
    rates = (0.03, 0.03, 0.03, 0.03, 0.2)
    updated = [
        adamw(w, g, m, v, r) for w, g, m, v, r in zip(weights, grads, firsts, seconds, rates)
    ]
    return (
        edge_new.astype(bf)[None],
        node_new.astype(bf)[None],
        edge_grad[None],
        node_grad[None],
        grads[0],
        grads[1],
        grads[2],
        grads[3],
        grads[4],
        updated[0][1],
        updated[1][1],
        updated[2][1],
        updated[3][1],
        updated[4][1],
        updated[0][0],
        updated[1][0],
        updated[2][0],
        updated[3][0],
        updated[4][0],
    )


def solution(mesh):
    in_specs = (
        P("grp", "edge", None),
        P("grp", "edge", None),
        P("grp", "edge", None),
        P("grp", "edge", None),
        P("grp", "edge"),
        P("grp", "edge"),
        P("grp", "edge"),
        P(("edge", "grp"), None),
        P(("edge", "grp"), None),
        P(("edge", "grp"), None),
        P(("edge", "grp"), None),
        P(None, ("edge", "grp")),
        P(("edge", "grp"), None),
        P(("edge", "grp"), None),
        P(("edge", "grp"), None),
        P(("edge", "grp"), None),
        P(None, ("edge", "grp")),
        P(("edge", "grp"), None),
        P(("edge", "grp"), None),
        P(("edge", "grp"), None),
        P(("edge", "grp"), None),
        P(None, ("edge", "grp")),
    )
    out_specs = (
        P("grp", "edge", None),
        P("grp", "edge", None),
        P("grp", "edge", None),
        P("grp", "edge", None),
        P(("edge", "grp"), None),
        P(("edge", "grp"), None),
        P(("edge", "grp"), None),
        P(("edge", "grp"), None),
        P(None, ("edge", "grp")),
        P(("edge", "grp"), None),
        P(("edge", "grp"), None),
        P(("edge", "grp"), None),
        P(("edge", "grp"), None),
        P(None, ("edge", "grp")),
        P(("edge", "grp"), None),
        P(("edge", "grp"), None),
        P(("edge", "grp"), None),
        P(("edge", "grp"), None),
        P(None, ("edge", "grp")),
    )
    return jax.shard_map(
        on_device, mesh=mesh, in_specs=in_specs, out_specs=out_specs, check_vma=False
    )
```

profile of v0, /device:TPU:0, one launch (start us, length us, event | category | flops | bytes accessed | tf_op | source)
XLA Modules:
  0.0 1047.8 jit_solution(5538673776109677973)
XLA Ops:
  10.9 43.4 %all-gather.1 = bf16[32,16,8]{1,2,0:T(8,128)(2,1)S(1)} all-gather(bf16[1,16,8]{1,2,0:T(8,128)(2,1)S(1)} %convert_bitcast_fusion.1), channel_id=1, replica_groups=mesh['edge'=8,'grp'=4] {'edge','grp'}, dimensions={0}, use_global_device_ids=true | all-gather | bytes 8448 | tf_op jit(solution)/shard_map/all_gather | solution.py:88
  55.4 32.0 %all-gather = bf16[1,512,512]{2,1,0:T(8,128)(2,1)S(1)} all-gather(bf16[1,64,512]{2,1,0:T(8,128)(2,1)} %param.23), channel_id=2, replica_groups=mesh['edge'=8,'grp'=4] {'edge'}, dimensions={1}, use_global_device_ids=true | all-gather | bytes 589824 | tf_op jit(solution)/shard_map/all_gather | solution.py:91
  87.3 4.0 gather_fusion
  93.3 4.0 gather_fusion.1
  99.2 40.4 %all_gather.24 = bf16[512,512]{1,0:T(8,128)(2,1)} all-gather(bf16[16,512]{1,0:T(8,128)(2,1)S(1)} %convert_element_type.98), channel_id=1, replica_groups=mesh['edge'=8,'grp'=4] {'edge','grp'}, dimensions={0}, use_global_device_ids=true | all-gather | bytes 540672 | tf_op jit(solution)/shard_map/all_gather | solution.py:85
  139.6 5.5 multiply_convert_fusion.2
  151.6 8.3 scatter_custom_fusion
  162.8 40.0 %all_gather.26 = bf16[512,512]{1,0:T(8,128)(2,1)S(1)} all-gather(bf16[16,512]{1,0:T(8,128)(2,1)S(1)} %convert_element_type.104), channel_id=1, replica_groups=mesh['edge'=8,'grp'=4] {'edge','grp'}, dimensions={0}, use_global_device_ids=true | all-gather | bytes 540672 | tf_op jit(solution)/shard_map/all_gather | solution.py:87
  202.7 18.8 %reduce-scatter.10.cloned.1.call-done = f32[64,512]{1,0:T(8,128)} async-done(((f32[512,512]{1,0:T(8,128)}), f32[64,512]{1,0:T(8,128)}) %reduce-scatter.10.cloned.1.call-update) | async-done | bytes 131088 | tf_op jit(solution)/shard_map/reduce_scatter | solution.py:100
  222.4 55.6 %all-gather.7.cloned.1.call-done = bf16[1024,512]{1,0:T(8,128)(2,1)} async-done(((bf16[32,512]{1,0:T(8,128)(2,1)}), bf16[1024,512]{1,0:T(8,128)(2,1)}) %all-gather.7.cloned.1.call-update) | async-done | bytes 1048592 | tf_op jit(solution)/shard_map/all_gather | solution.py:86
  283.6 31.7 %all_gather.27 = bf16[512,512]{1,0:T(8,128)(2,1)S(1)} all-gather(bf16[64,512]{1,0:T(8,128)(2,1)S(1)} %slice.82), channel_id=1, replica_groups=mesh['edge'=8,'grp'=4] {'edge'}, dimensions={0}, use_global_device_ids=true | all-gather | bytes 589824 | tf_op jit(solution)/shard_map/all_gather | solution.py:119
  315.2 5.1 gather_fusion.2
  322.7 3.2 multiply_reduce_fusion
  335.8 5.7 fusion.52
  341.5 7.6 scatter_custom_fusion.1
  349.1 8.0 scatter_custom_fusion.2
  358.3 5.4 fusion.5
  367.7 3.2 slice.70
  377.5 86.3 %reduce-scatter.22.cloned.1.call-done = f32[16,8]{1,0:T(8,128)} async-done(((f32[512,8]{1,0:T(8,128)}), f32[16,8]{1,0:T(8,128)}) %reduce-scatter.22.cloned.1.call-update) | async-done | bytes 528
  465.2 132.0 %reduce-scatter.16.cloned.1.call-done = f32[16,512]{1,0:T(8,128)} async-done(((f32[512,512]{1,0:T(8,128)}), f32[16,512]{1,0:T(8,128)}) %reduce-scatter.16.cloned.1.call-update) | async-done | bytes 32784 | tf_op jit(solution)/shard_map/reduce_scatter | solution.py:144
  598.6 132.1 %reduce-scatter.20.cloned.1.call-done = f32[16,512]{1,0:T(8,128)} async-done(((f32[512,512]{1,0:T(8,128)}), f32[16,512]{1,0:T(8,128)}) %reduce-scatter.20.cloned.1.call-update) | async-done | bytes 32784 | tf_op jit(solution)/shard_map/reduce_scatter | solution.py:146
  732.1 61.5 %reduce-scatter.12.cloned.1.call-done = f32[64,512]{1,0:T(8,128)} async-done(((f32[512,512]{1,0:T(8,128)}), f32[64,512]{1,0:T(8,128)}) %reduce-scatter.12.cloned.1.call-update) | async-done | bytes 131088 | tf_op jit(solution)/shard_map/reduce_scatter | solution.py:139
  795.2 105.9 %reduce-scatter.14.cloned.1.call-done = f32[48,512]{1,0:T(8,128)} async-done(((f32[1536,512]{1,0:T(8,128)}), f32[48,512]{1,0:T(8,128)}) %reduce-scatter.14.cloned.1.call-update) | async-done | bytes 98320 | tf_op jit(solution)/shard_map/reduce_scatter | solution.py:143
  902.7 137.0 %reduce-scatter.18.cloned.1.call-done = f32[32,512]{1,0:T(8,128)} async-done(((f32[1024,512]{1,0:T(8,128)}), f32[32,512]{1,0:T(8,128)}) %reduce-scatter.18.cloned.1.call-update) | async-done | bytes 65552 | tf_op jit(solution)/shard_map/reduce_scatter | solution.py:145
  (199 shorter events, 56.0 us)
Async XLA Ops:
  7.2 132.4 %all-gather.5.cloned.1.call-start = ((), (), s32[]{:S(2)}) async-start(), calls=%async_computation.7 | async-start | bytes 1622016 | tf_op jit(solution)/shard_map/all_gather | solution.py:84
  8.8 212.7 %reduce-scatter.10.cloned.1.call-start = ((), (), s32[]{:S(2)}) async-start(), calls=%async_computation.8 | async-start | bytes 1179648 | tf_op jit(solution)/shard_map/reduce_scatter | solution.py:100
  160.0 118.1 %copy-start.9 = (bf16[1,64,512]{2,1,0:T(8,128)(2,1)S(1)}, bf16[1,64,512]{2,1,0:T(8,128)(2,1)}, u32[]{:S(2)}) copy-start(bf16[1,64,512]{2,1,0:T(8,128)(2,1)} %param.23) | copy-start | bytes 196612
  160.0 118.0 %all-gather.7.cloned.1.call-start = ((), (), s32[]{:S(2)}) async-start(), calls=%async_computation.9 | async-start | bytes 1081344 | tf_op jit(solution)/shard_map/all_gather | solution.py:86
  160.7 303.1 %reduce-scatter.22.cloned.1.call-start = ((), (), s32[]{:S(2)}) async-start(), calls=%async_computation.15 | async-start | bytes 270336
  331.2 266.0 %reduce-scatter.16.cloned.1.call-start = ((), (), s32[]{:S(2)}) async-start(), calls=%async_computation.12 | async-start | bytes 1081344 | tf_op jit(solution)/shard_map/reduce_scatter | solution.py:144
  334.3 396.4 %reduce-scatter.20.cloned.1.call-start = ((), (), s32[]{:S(2)}) async-start(), calls=%async_computation.14 | async-start | bytes 1081344 | tf_op jit(solution)/shard_map/reduce_scatter | solution.py:146
  335.7 457.9 %reduce-scatter.12.cloned.1.call-start = ((), (), s32[]{:S(2)}) async-start(), calls=%async_computation.10 | async-start | bytes 1179648 | tf_op jit(solution)/shard_map/reduce_scatter | solution.py:139
  358.2 542.9 %reduce-scatter.14.cloned.1.call-start = ((), (), s32[]{:S(2)}) async-start(), calls=%async_computation.11 | async-start | bytes 3244032 | tf_op jit(solution)/shard_map/reduce_scatter | solution.py:143
  363.7 676.0 %reduce-scatter.18.cloned.1.call-start = ((), (), s32[]{:S(2)}) async-start(), calls=%async_computation.13 | async-start | bytes 2162688 | tf_op jit(solution)/shard_map/reduce_scatter | solution.py:145
  376.0 88.6 %copy-start.44 = (f32[8,16]{1,0:T(8,128)S(1)}, f32[8,16]{1,0:T(8,128)}, u32[]{:S(2)}) copy-start(f32[8,16]{1,0:T(8,128)} %param.33) | copy-start | bytes 1540
  376.0 221.2 %copy-start.26 = (f32[16,512]{1,0:T(8,128)S(1)}, f32[16,512]{1,0:T(8,128)}, u32[]{:S(2)}) copy-start(f32[16,512]{1,0:T(8,128)} %param.30) | copy-start | bytes 98308
  376.0 221.2 %copy-start.37 = (f32[16,512]{1,0:T(8,128)S(1)}, f32[16,512]{1,0:T(8,128)}, u32[]{:S(2)}) copy-start(f32[16,512]{1,0:T(8,128)} %param.35) | copy-start | bytes 98308
  376.0 221.1 %copy-start.38 = (f32[16,512]{1,0:T(8,128)S(1)}, f32[16,512]{1,0:T(8,128)}, u32[]{:S(2)}) copy-start(f32[16,512]{1,0:T(8,128)} %param.40) | copy-start | bytes 98308
  376.1 354.7 %copy-start.28 = (f32[16,512]{1,0:T(8,128)S(1)}, f32[16,512]{1,0:T(8,128)}, u32[]{:S(2)}) copy-start(f32[16,512]{1,0:T(8,128)} %param.32) | copy-start | bytes 98308
  376.1 354.7 %copy-start.39 = (f32[16,512]{1,0:T(8,128)S(1)}, f32[16,512]{1,0:T(8,128)}, u32[]{:S(2)}) copy-start(f32[16,512]{1,0:T(8,128)} %param.37) | copy-start | bytes 98308
  376.1 354.7 %copy-start.40 = (f32[16,512]{1,0:T(8,128)S(1)}, f32[16,512]{1,0:T(8,128)}, u32[]{:S(2)}) copy-start(f32[16,512]{1,0:T(8,128)} %param.42) | copy-start | bytes 98308
  376.1 525.0 %copy-start.19 = (f32[48,512]{1,0:T(8,128)S(1)}, f32[48,512]{1,0:T(8,128)}, u32[]{:S(2)}) copy-start(f32[48,512]{1,0:T(8,128)} %param.29) | copy-start | bytes 294916
  376.1 525.0 %copy-start.29 = (f32[48,512]{1,0:T(8,128)S(1)}, f32[48,512]{1,0:T(8,128)}, u32[]{:S(2)}) copy-start(f32[48,512]{1,0:T(8,128)} %param.34) | copy-start | bytes 294916
  376.1 525.0 %copy-start.30 = (f32[48,512]{1,0:T(8,128)S(1)}, f32[48,512]{1,0:T(8,128)}, u32[]{:S(2)}) copy-start(f32[48,512]{1,0:T(8,128)} %param.39) | copy-start | bytes 294916
  376.1 663.6 %copy-start.23 = (f32[32,512]{1,0:T(8,128)S(1)}, f32[32,512]{1,0:T(8,128)}, u32[]{:S(2)}) copy-start(f32[32,512]{1,0:T(8,128)} %param.31) | copy-start | bytes 196612
  376.1 663.6 %copy-start.31 = (f32[32,512]{1,0:T(8,128)S(1)}, f32[32,512]{1,0:T(8,128)}, u32[]{:S(2)}) copy-start(f32[32,512]{1,0:T(8,128)} %param.36) | copy-start | bytes 196612
  376.2 663.6 %copy-start.32 = (f32[32,512]{1,0:T(8,128)S(1)}, f32[32,512]{1,0:T(8,128)}, u32[]{:S(2)}) copy-start(f32[32,512]{1,0:T(8,128)} %param.41) | copy-start | bytes 196612
  464.6 576.7 %copy-start.43 = (f32[8,16]{1,0:T(8,128)}, f32[8,16]{1,0:T(8,128)S(1)}, u32[]{:S(2)}) copy-start(f32[8,16]{1,0:T(8,128)S(1)} %copy.81) | copy-start | bytes 1540
  (46 other events, 692.3 us)
Sparse Core Ops, SparseCore 0:
  11.5 58.8 all-gather.4
  160.1 61.3 reduce-scatter.9
  225.4 52.6 all-gather.6
  331.3 132.4 reduce-scatter.21
  466.5 130.6 reduce-scatter.15
  599.9 130.7 reduce-scatter.19
  734.1 59.4 reduce-scatter.11
  800.5 100.5 reduce-scatter.13
  904.0 135.6 reduce-scatter.17
where the time goes:
time: 1050 us
  waiting for transfers between devices  729 us (69%)
  blocking collectives  187 us (18%)
  other arithmetic  50.2 us (5%)
  local copies, waits for them, and re-layouts  36.2 us (3%)
  matrix products  29 us (3%)
  between operations  15.3 us (1%)
    reduce_scatter x1, waiting for transfers between devices, on_device(): lax.psum_scatter(g_w1n, ('edge', 'grp'), scatter_dimension=0, tiled=True)  137 us
    reduce_scatter x1, waiting for transfers between devices, on_device(): lax.psum_scatter(g_w2n, ('edge', 'grp'), scatter_dimension=0, tiled=True)  132 us
    reduce_scatter x1, waiting for transfers between devices, on_device(): lax.psum_scatter(g_w2e, ('edge', 'grp'), scatter_dimension=0, tiled=True)  132 us
    reduce_scatter x1, waiting for transfers between devices, on_device(): lax.psum_scatter(g_w1e, ('edge', 'grp'), scatter_dimension=0, tiled=True)  106 us
    unnamed x10, waiting for transfers between devices  86.5 us
    reduce_scatter x1, waiting for transfers between devices, on_device(): lax.psum_scatter(dense_grad, 'edge', scatter_dimension=0, tiled=True)  61.5 us
    all_gather x1, waiting for transfers between devices, on_device(): lax.all_gather(w_node_in.astype(bf), ('edge', 'grp'), axis=0, tiled=True)  55.6 us
    all_gather x1, blocking collectives, on_device(): lax.all_gather(small_params.astype(bf), ('edge', 'grp'), axis=1, tiled=True)  43.4 us
  transfers between devices with their start and end apart: 9, of which 8 were waited for; matrix products, arithmetic and copies ran while one was open for 7% of the time, Pallas kernels for 0%

commit v1 on v0

--- a/solution.py
+++ b/solution.py
@@ -1,6 +1,10 @@
+import functools
+
 import jax
 import jax.numpy as jnp
 from jax import lax
+from jax.experimental import pallas as pl
+from jax.experimental.pallas import tpu as pltpu
 from jax.sharding import PartitionSpec as P
 
 step_count = 10.0
@@ -48,7 +52,7 @@
     return (weight - rate * (mhat / (jnp.sqrt(vhat) + 1e-08) + 0.1 * weight), second_new)
 
 
-def on_device(
+def native(
     edge_lat,
     node_lat,
     edge_cot,
@@ -176,6 +180,667 @@
     )
 
 
+bf16 = jnp.bfloat16
+f32 = jnp.float32
+MESH = pl.DeviceIdType.MESH
+
+
+def mm(left, right):
+    return jnp.dot(left, right, preferred_element_type=f32)
+
+
+def fold_rows(values):
+    count, width = values.shape
+    return jnp.sum(values.reshape(count // 8, 8, width), axis=0)
+
+
+def layer_kernel(geo, *refs):
+    Z, Y, X, C = geo["dims"]
+    n_sem = geo["n_sem"]
+    (
+        edges_hbm,
+        cot_hbm,
+        nodes_in,
+        ncot_in,
+        send_in,
+        recv_in,
+        count_in,
+        w1_in,
+        w2_in,
+        w3_in,
+        w4_in,
+        small_in,
+        enew_out,
+        egrad_out,
+        nnew_out,
+        ngrad_out,
+        g1_out,
+        g2_out,
+        g3_out,
+        g4_out,
+        gs_out,
+        edges,
+        cot,
+        nbuf,
+        dbuf,
+        w1,
+        w2,
+        w3,
+        w4,
+        w2v,
+        w3v,
+        w4v,
+        pick,
+        spread,
+        proj,
+        slope,
+        hidden,
+        normed,
+        rstd,
+        term,
+        enew,
+        dedge,
+        dout,
+        dpre,
+        egrad,
+        sums,
+        pf,
+        pb_a,
+        pb_n,
+        yr_a,
+        yr_n,
+        zs_a,
+        zs_n,
+        zr_a,
+        zr_n,
+        seg,
+        sm_src,
+        sm_rcv,
+        gm_src,
+        gm_rcv,
+        gsm,
+        *grad_refs,
+    ) = refs
+    local_sem, ssem, rsem = grad_refs[-3:]
+    grad_refs = grad_refs[:-3]
+    rows, D = edges.shape
+    n = nodes_in.shape[0]
+    N = Z * Y * n
+    R = geo["chunk"]
+
+    e_id = lax.axis_index("edge")
+    g_id = lax.axis_index("grp")
+    z = e_id // Y
+    y = e_id % Y
+    x = g_id // C
+    c = g_id % C
+    yp, xp, cp = 1 - y, 1 - x, 1 - c
+    me = e_id * (X * C) + g_id
+    y_dev = (z * Y + yp, g_id)
+    x_dev = (e_id, xp * C + c)
+    c_dev = (e_id, x * C + cp)
+
+    def z_at(o):
+        return lax.rem(z + o, Z)
+
+    def z_dev(o):
+        return (z_at(o) * Y + y, g_id)
+
+    started = []
+
+    def push(src, dst, dev):
+        k = len(started)
+        assert k < n_sem
+        copy = pltpu.make_async_remote_copy(
+            src_ref=src,
+            dst_ref=dst,
+            send_sem=ssem.at[k],
+            recv_sem=rsem.at[k],
+            device_id=dev,
+            device_id_type=MESH,
+        )
+        copy.start()
+        started.append(copy)
+        return copy
+
+    edges_copy = pltpu.make_async_copy(edges_hbm, edges, local_sem.at[0])
+    cot_copy = pltpu.make_async_copy(cot_hbm, cot, local_sem.at[1])
+    edges_copy.start()
+    cot_copy.start()
+    barrier = pltpu.get_barrier_semaphore()
+    peers = [z_dev(o) for o in range(1, Z)] + [y_dev, x_dev, c_dev]
+    for dev in peers:
+        pl.semaphore_signal(barrier, inc=1, device_id=dev, device_id_type=MESH)
+
+    nbuf[z, y] = nodes_in[...]
+    r1 = w1_in.shape[0]
+    w1[pl.ds(pl.multiple_of(me * r1, 16), r1), :] = w1_in[...].astype(bf16)
+    for v, own in ((w2v, w2_in), (w3v, w3_in), (w4v, w4_in)):
+        v[z, y, x, c] = own[...].astype(bf16)
+    ws = small_in.shape[1]
+    place = (
+        lax.broadcasted_iota(jnp.int32, (ws, D), 1)
+        == lax.broadcasted_iota(jnp.int32, (ws, D), 0) + me * ws
+    )
+    sm_src[0] = mm(small_in[...].astype(bf16), jnp.where(place, 1.0, 0.0).astype(bf16))
+    pl.semaphore_wait(barrier, len(peers))
+
+    own_n = nbuf.at[z, y]
+    n_z = [push(own_n, own_n, z_dev(o)) for o in range(1, Z)]
+    n_y = [push(own_n, own_n, y_dev)]
+
+    def slot(zz, yy, xx):
+        at = (((zz * Y + yy) * X + xx) * C + c) * r1
+        return w1.at[pl.ds(pl.multiple_of(at, 16), r1), :]
+
+    s = slot(z, y, x)
+    w1_z = [push(s, s, z_dev(o)) for o in range(1, Z)]
+    w1_y = [push(s, s, y_dev)]
+    w1_x = [push(s, s, x_dev)]
+    w1_c = [push(s, s, c_dev)]
+    sm_z = [push(sm_src.at[0], sm_rcv.at[o - 1], z_dev(o)) for o in range(1, Z)]
+
+    class Lines:
+        def __init__(self, v):
+            self.v = v
+            s = v.at[z, y, x, c]
+            self.z = [push(s, s, z_dev(o)) for o in range(1, Z)]
+
+        def line(self):
+            for copy in self.z:
+                copy.wait_recv()
+            s = self.v.at[:, y, x, c]
+            self.y = push(s, s, y_dev)
+            self.x = [push(s, s, x_dev)]
+
+        def cross(self):
+            self.y.wait_recv()
+            s = self.v.at[:, yp, x, c]
+            self.x.append(push(s, s, x_dev))
+
+        def pair(self):
+            for copy in self.x:
+                copy.wait_recv()
+            s = self.v.at[:, :, :, c]
+            self.c = push(s, s, c_dev)
+
+        def done(self, whole):
+            self.c.wait_recv()
+            whole[...] = self.v[...].reshape(whole.shape)
+
+    w2_lines = Lines(w2v)
+    w3_lines = Lines(w3v)
+    w4_lines = Lines(w4v)
+
+    lane = lax.broadcasted_iota(jnp.int32, (128, N), 1)
+    sub = lax.broadcasted_iota(jnp.int32, (N, 128), 0)
+
+    @pl.loop(0, rows // 128)
+    def _(k):
+        at = pl.ds(pl.multiple_of(k * 128, 128), 128)
+        for half, ids in enumerate((send_in, recv_in)):
+            row = jnp.broadcast_to(ids[0:1, at], (128, 128))
+            col = jnp.tile(row.T, (1, N // 128))
+            pick[at, half * N : (half + 1) * N] = jnp.where(lane == col, 1.0, 0.0).astype(bf16)
+            wide = jnp.broadcast_to(ids[0:1, at], (N, 128))
+            spread[half * N : (half + 1) * N, at] = jnp.where(sub == wide, 1.0, 0.0).astype(bf16)
+
+    for o in range(1, Z):
+        n_z[o - 1].wait_recv()
+        s = nbuf.at[z_at(Z - o), y]
+        n_y.append(push(s, s, y_dev))
+    for o in range(1, Z):
+        w1_z[o - 1].wait_recv()
+        s = slot(z_at(Z - o), y, x)
+        w1_y.append(push(s, s, y_dev))
+        w1_x.append(push(s, s, x_dev))
+        w1_c.append(push(s, s, c_dev))
+    w2_lines.line()
+
+    def small_sum(src, rcv, stage, copies):
+        total = src[stage]
+        for copy, k in copies:
+            copy.wait_recv()
+            total = total + rcv[k]
+        src[stage + 1] = total
+
+    small_sum(sm_src, sm_rcv, 0, [(copy, k) for k, copy in enumerate(sm_z)])
+    sm_y = push(sm_src.at[1], sm_rcv.at[Z - 1], y_dev)
+    for o in range(Z):
+        w1_y[o].wait_recv()
+        s = slot(z_at(Z - o), yp, x)
+        w1_x.append(push(s, s, x_dev))
+        w1_c.append(push(s, s, c_dev))
+    w2_lines.cross()
+    small_sum(sm_src, sm_rcv, 1, [(sm_y, Z - 1)])
+    sm_x = push(sm_src.at[2], sm_rcv.at[Z], x_dev)
+    for k in range(Y * Z):
+        w1_x[k].wait_recv()
+        s = slot(z_at(Z - k % Z), y if k < Z else yp, xp)
+        w1_c.append(push(s, s, c_dev))
+    w2_lines.pair()
+    small_sum(sm_src, sm_rcv, 2, [(sm_x, Z)])
+    sm_c = push(sm_src.at[3], sm_rcv.at[Z + 1], c_dev)
+    w3_lines.line()
+    w4_lines.line()
+    for copy in n_y:
+        copy.wait_recv()
+    edges_copy.wait()
+    for copy in w1_c:
+        copy.wait_recv()
+    w2_lines.done(w2)
+    small_sum(sm_src, sm_rcv, 3, [(sm_c, Z + 1)])
+
+    nodes_all = nbuf[...].reshape(N, D)
+    proj[0:N, :] = mm(nodes_all, w1[D : 2 * D, :]).astype(bf16)
+    proj[N : 2 * N, :] = mm(nodes_all, w1[2 * D : 3 * D, :]).astype(bf16)
+    count = count_in[0, 0]
+    row_id = lax.broadcasted_iota(jnp.int32, (R, D), 0)
+
+    @pl.loop(0, rows // R)
+    def _(i):
+        at = pl.ds(pl.multiple_of(i * R, R), R)
+        live = row_id < count - i * R
+        own = edges[at, :]
+        pre = mm(own, w1[0:D, :]) + mm(pick[at, :], proj[...]) + sm_src[4, 0:1, :]
+        sig = jax.nn.sigmoid(pre)
+        act = (pre * sig).astype(bf16)
+        hidden[at, :] = act
+        slope[at, :] = sig * (1.0 + pre * (1.0 - sig))
+        out = mm(act, w2[...]) + sm_src[4, 1:2, :]
+        norm, inv = norm_stats(out)
+        normed[at, :] = norm
+        rstd[at, :] = jnp.broadcast_to(inv, (R, 128))
+        new = own.astype(f32) + jnp.where(live, norm * sm_src[4, 2:3, :] + sm_src[4, 3:4, :], 0.0)
+        enew[at, :] = new.astype(bf16)
+        term[at, :] = jnp.where(live, new, 0.0).astype(bf16)
+
+    enew_copy = pltpu.make_async_copy(enew, enew_out, local_sem.at[2])
+    enew_copy.start()
+    w3_lines.cross()
+    w4_lines.cross()
+
+    class NodeSum:
+        def __init__(self, total, pb, yr, zs, zr):
+            self.zs, self.zr = zs, zr
+            pf[...] = total.reshape(Z, Y, n, D)
+            pb[...] = total.astype(bf16).reshape(Z, Y, n, D)
+            self.yr = yr
+            self.y = [push(pb.at[z_at(o), yp], yr.at[o], y_dev) for o in (*range(1, Z), 0)]
+
+        def turn(self):
+            self.z = []
+            for k, o in enumerate((*range(1, Z), 0)):
+                self.y[k].wait_recv()
+                part = pf[z_at(o), y] + self.yr[o].astype(f32)
+                if o == 0:
+                    self.kept = part
+                else:
+                    self.zs[o - 1] = part.astype(bf16)
+                    self.z.append(push(self.zs.at[o - 1], self.zr.at[o - 1], z_dev(o)))
+
+        def total(self):
+            result = self.kept
+            for o in range(1, Z):
+                self.z[o - 1].wait_recv()
+                result = result + self.zr[o - 1].astype(f32)
+            return result
+
+    agg_sum = NodeSum(mm(spread[N : 2 * N, :], term[...]), pb_a, yr_a, zs_a, zr_a)
+    w3_lines.pair()
+    w4_lines.pair()
+    agg_sum.turn()
+    w3_lines.done(w3)
+    w4_lines.done(w4)
+    agg = agg_sum.total()
+
+    def par(k):
+        return sm_src[4, k : k + 1, :]
+
+    own_nodes = nodes_in[...]
+    agg_low = agg.astype(bf16)
+    pre_n = mm(own_nodes, w3[0:D, :]) + mm(agg_low, w3[D : 2 * D, :]) + par(4)
+    sig_n = jax.nn.sigmoid(pre_n)
+    hidden_n = (pre_n * sig_n).astype(bf16)
+    out_n = mm(hidden_n, w4[...]) + par(5)
+    normed_n, rstd_n = norm_stats(out_n)
+    ncot = ncot_in[...].astype(f32)
+    d_out_n = norm_back(ncot, normed_n, rstd_n, par(6)).astype(bf16)
+    slope_n = sig_n * (1.0 + pre_n * (1.0 - sig_n))
+    d_pre_n = (times_t(d_out_n, w4[...]) * slope_n).astype(bf16)
+    dbuf[z, y] = times_t(d_pre_n, w3[D : 2 * D, :]).astype(bf16)
+    own_d = dbuf.at[z, y]
+    d_z = [push(own_d, own_d, z_dev(o)) for o in range(1, Z)]
+    d_y = [push(own_d, own_d, y_dev)]
+
+    class WeightSum:
+        def __init__(self, grad, crecv, xs, xrecv, ks, ys, yrecv, zs, zrecv):
+            self.grad, self.crecv, self.xs, self.xrecv, self.ks = grad, crecv, xs, xrecv, ks
+            self.ys, self.yrecv, self.zs, self.zrecv = ys, yrecv, zs, zrecv
+
+        def put(self, first, values):
+            low, r = values.astype(bf16), self.grad.shape[4]
+            row = 0
+            while row < values.shape[0]:
+                k, off = divmod(first + row, r)
+                size = min(r - off, values.shape[0] - row)
+                at = (k // (Y * X * C), k // (X * C) % Y, k // C % X, k % C)
+                self.grad[(*at, slice(off, off + size))] = low[row : row + size]
+                row += size
+
+        def rows_of(self, zz, yy, xx):
+            return self.grad[zz, yy, xx, c].astype(f32)
+
+        def start(self):
+            self.c = [
+                push(self.grad.at[:, :, xx, cp], self.crecv.at[h], c_dev)
+                for h, xx in enumerate((xp, x))
+            ]
+
+        def cross_x(self):
+            self.c[0].wait_recv()
+            self.x = []
+            for h, yy in enumerate((yp, y)):
+                for zz in range(Z):
+                    part = self.rows_of(zz, yy, xp) + self.crecv[0, zz, yy].astype(f32)
+                    self.xs[h, zz] = part.astype(bf16)
+                self.x.append(push(self.xs.at[h], self.xrecv.at[h], x_dev))
+            self.c[1].wait_recv()
+            for h, yy in enumerate((yp, y)):
+                for zz in range(Z):
+                    self.ks[h, zz] = self.rows_of(zz, yy, x) + self.crecv[1, zz, yy].astype(f32)
+
+        def cross_y(self):
+            self.x[0].wait_recv()
+            self.ys[...] = (self.ks[0] + self.xrecv[0].astype(f32)).astype(bf16)
+            self.y = push(self.ys, self.yrecv, y_dev)
+            self.x[1].wait_recv()
+            self.ks[1] = self.ks[1] + self.xrecv[1].astype(f32)
+
+        def cross_z(self):
+            self.y.wait_recv()
+            self.z = []
+            for o in range(1, Z):
+                zz = z_at(o)
+                self.zs[o - 1] = (self.ks[1, zz] + self.yrecv[zz].astype(f32)).astype(bf16)
+                self.z.append(push(self.zs.at[o - 1], self.zrecv.at[o - 1], z_dev(o)))
+
+        def total(self):
+            result = self.ks[1, z] + self.yrecv[z].astype(f32)
+            for o in range(1, Z):
+                self.z[o - 1].wait_recv()
+                result = result + self.zrecv[o - 1].astype(f32)
+            return result
+
+    per = len(grad_refs) // 4
+    sum1, sum2, sum3, sum4 = [WeightSum(*grad_refs[k * per : (k + 1) * per]) for k in range(4)]
+
+    sum3.put(0, inner(own_nodes, d_pre_n))
+    sum3.put(D, inner(agg_low, d_pre_n))
+    sum4.put(0, inner(hidden_n, d_out_n))
+    sum3.start()
+    sum4.start()
+    nnew_out[...] = (own_nodes.astype(f32) + normed_n * par(6) + par(7)).astype(bf16)
+    node_part = ncot + times_t(d_pre_n, w3[0:D, :])
+    gsm[4:5, :] = jnp.sum(d_pre_n.astype(f32), axis=0, keepdims=True)
+    gsm[5:6, :] = jnp.sum(d_out_n.astype(f32), axis=0, keepdims=True)
+    gsm[6:7, :] = jnp.sum(ncot * normed_n, axis=0, keepdims=True)
+    gsm[7:8, :] = jnp.sum(ncot, axis=0, keepdims=True)
+    for o in range(1, Z):
+        d_z[o - 1].wait_recv()
+        s = dbuf.at[z_at(Z - o), y]
+        d_y.append(push(s, s, y_dev))
+    sum3.cross_x()
+    sum4.cross_x()
+    cot_copy.wait()
+    for copy in d_y:
+        copy.wait_recv()
+
+    sums[...] = jnp.zeros_like(sums)
+    d_all = dbuf[...].reshape(N, D)
+
+    @pl.loop(0, rows // R)
+    def _(i):
+        at = pl.ds(pl.multiple_of(i * R, R), R)
+        live = row_id < count - i * R
+        d_edge = cot[at, :].astype(f32) + jnp.where(live, mm(pick[at, N : 2 * N], d_all), 0.0)
+        dedge[at, :] = d_edge
+        masked = jnp.where(live, d_edge, 0.0)
+        norm = normed[at, :]
+        inv = rstd[at, 0:1]
+        weighted = masked * norm
+        sums[2] += fold_rows(weighted)
+        sums[3] += fold_rows(masked)
+        d_out = norm_back(masked, norm, inv, par(2)).astype(bf16)
+        dout[at, :] = d_out
+        sums[1] += fold_rows(d_out.astype(f32))
+        d_pre = (times_t(d_out, w2[...]) * slope[at, :]).astype(bf16)
+        dpre[at, :] = d_pre
+        sums[0] += fold_rows(d_pre.astype(f32))
+
+    sum3.cross_y()
+    sum4.cross_y()
+    d_pre = dpre[...]
+    seg[0:N, :] = mm(spread[0:N, :], d_pre).astype(bf16)
+    seg[N : 2 * N, :] = mm(spread[N : 2 * N, :], d_pre).astype(bf16)
+    node_sum = NodeSum(
+        times_t(seg[0:N, :], w1[D : 2 * D, :]) + times_t(seg[N : 2 * N, :], w1[2 * D : 3 * D, :]),
+        pb_n,
+        yr_n,
+        zs_n,
+        zr_n,
+    )
+    sum2.put(0, inner(hidden[...], dout[...]))
+    sum2.start()
+    sum1.put(D, inner(nodes_all, seg[0:N, :]))
+    sum1.put(2 * D, inner(nodes_all, seg[N : 2 * N, :]))
+    sum1.put(0, inner(edges[...], d_pre))
+    sum1.start()
+    for k in range(4):
+        gsm[k : k + 1, :] = jnp.sum(sums[k], axis=0, keepdims=True)
+    gm_src[0] = gsm[...]
+    gm_c = push(gm_src.at[0], gm_rcv.at[0], c_dev)
+    node_sum.turn()
+    sum3.cross_z()
+    sum4.cross_z()
+    sum2.cross_x()
+    sum1.cross_x()
+    small_sum(gm_src, gm_rcv, 0, [(gm_c, 0)])
+    gm_x = push(gm_src.at[1], gm_rcv.at[1], x_dev)
+
+    @pl.loop(0, rows // R)
+    def _(i):
+        at = pl.ds(pl.multiple_of(i * R, R), R)
+        egrad[at, :] = (dedge[at, :] + times_t(dpre[at, :], w1[0:D, :])).astype(bf16)
+
+    egrad_copy = pltpu.make_async_copy(egrad, egrad_out, local_sem.at[3])
+    egrad_copy.start()
+    sum2.cross_y()
+    sum1.cross_y()
+    small_sum(gm_src, gm_rcv, 1, [(gm_x, 1)])
+    gm_y = push(gm_src.at[2], gm_rcv.at[2], y_dev)
+    ngrad_out[...] = (node_part + node_sum.total()).astype(bf16)
+    g3_out[...] = sum3.total()
+    g4_out[...] = sum4.total()
+    sum2.cross_z()
+    sum1.cross_z()
+    small_sum(gm_src, gm_rcv, 2, [(gm_y, 2)])
+    gm_z = [push(gm_src.at[3], gm_rcv.at[2 + o], z_dev(o)) for o in range(1, Z)]
+    g2_out[...] = sum2.total()
+    g1_out[...] = sum1.total()
+    small_sum(gm_src, gm_rcv, 3, [(copy, 3 + k) for k, copy in enumerate(gm_z)])
+    take = (
+        lax.broadcasted_iota(jnp.int32, (D, ws), 0)
+        == lax.broadcasted_iota(jnp.int32, (D, ws), 1) + me * ws
+    )
+    gs_out[...] = jnp.dot(
+        gm_src[4],
+        jnp.where(take, 1.0, 0.0),
+        preferred_element_type=f32,
+        precision=lax.Precision.HIGHEST,
+    )
+    for copy in started:
+        copy.wait_send()
+    enew_copy.wait()
+    egrad_copy.wait()
+
+
+def update_kernel(*refs):
+    (
+        enew,
+        egrad,
+        nnew,
+        ngrad,
+        *rest,
+    ) = refs[:24]
+    outs = refs[24:]
+    for src, dst in zip((enew, nnew, egrad, ngrad), outs[:4]):
+        dst[0] = src[...]
+    grads, weights, firsts, seconds = rest[0:5], rest[5:10], rest[10:15], rest[15:20]
+    rates = (0.03, 0.03, 0.03, 0.03, 0.2)
+    for k in range(5):
+        grad = grads[k][...]
+        new_w, new_v = adamw(weights[k][...], grad, firsts[k][...], seconds[k][...], rates[k])
+        outs[4 + k][...] = grad
+        outs[9 + k][...] = new_v
+        outs[14 + k][...] = new_w
+
+
+def on_device(n_edge, n_grp, *args):
+    (
+        edge_lat,
+        node_lat,
+        edge_cot,
+        node_cot,
+        senders,
+        receivers,
+        edge_count,
+        *state,
+    ) = args
+    weights, firsts, seconds = state[0:5], state[5:10], state[10:15]
+    rows, D = edge_lat.shape[1:]
+    n = node_lat.shape[1]
+    N = n * n_edge
+    n_dev = n_edge * n_grp
+    shards = [w.shape[0] for w in weights[:4]]
+    fits = (
+        n_edge % 2 == 0
+        and n_grp == 4
+        and all(r % 16 == 0 for r in shards)
+        and D % 128 == 0
+        and N % 128 == 0
+        and rows % 256 == 0
+        and rows * N <= 1024 * 1024
+    )
+    if not fits:
+        return native(*args)
+    Z, Y, X, C = n_edge // 2, 2, 2, 2
+    n_sem = 160
+
+    def vm(shape, dtype=bf16):
+        return pltpu.VMEM(shape, dtype)
+
+    scratch = [
+        vm((rows, D)),
+        vm((rows, D)),
+        vm((Z, Y, n, D)),
+        vm((Z, Y, n, D)),
+        *[vm((r * n_dev, D)) for r in shards],
+        *[vm((Z, Y, X, C, r, D)) for r in shards[1:]],
+        vm((rows, 2 * N)),
+        vm((2 * N, rows)),
+        vm((2 * N, D)),
+        vm((rows, D), f32),
+        vm((rows, D)),
+        vm((rows, D), f32),
+        vm((rows, 128), f32),
+        vm((rows, D)),
+        vm((rows, D)),
+        vm((rows, D), f32),
+        vm((rows, D)),
+        vm((rows, D)),
+        vm((rows, D)),
+        vm((4, 8, D), f32),
+        vm((Z, Y, n, D), f32),
+        vm((Z, Y, n, D)),
+        vm((Z, Y, n, D)),
+        vm((Z, n, D)),
+        vm((Z, n, D)),
+        vm((Z - 1, n, D)),
+        vm((Z - 1, n, D)),
+        vm((Z - 1, n, D)),
+        vm((Z - 1, n, D)),
+        vm((2 * N, D)),
+        vm((5, 8, D), f32),
+        vm((Z + 2, 8, D), f32),
+        vm((5, 8, D), f32),
+        vm((Z + 2, 8, D), f32),
+        vm((8, D), f32),
+    ]
+    for r in shards:
+        scratch += [
+            vm((Z, Y, X, C, r, D)),
+            vm((2, Z, Y, r, D)),
+            vm((2, Z, r, D)),
+            vm((2, Z, r, D)),
+            vm((2, Z, r, D), f32),
+            vm((Z, r, D)),
+            vm((Z, r, D)),
+            vm((Z - 1, r, D)),
+            vm((Z - 1, r, D)),
+        ]
+    scratch += [
+        pltpu.SemaphoreType.DMA((4,)),
+        pltpu.SemaphoreType.DMA((n_sem,)),
+        pltpu.SemaphoreType.DMA((n_sem,)),
+    ]
+    sds = jax.ShapeDtypeStruct
+    anyspace = pl.BlockSpec(memory_space=pl.ANY)
+    vmem = pl.BlockSpec(memory_space=pltpu.VMEM)
+    smem = pl.BlockSpec(memory_space=pltpu.SMEM)
+    big = [sds((rows, D), bf16)] * 2 + [sds((n, D), bf16)] * 2
+    grads = [sds(w.shape, f32) for w in weights]
+    results = pl.pallas_call(
+        functools.partial(layer_kernel, {"dims": (Z, Y, X, C), "n_sem": n_sem, "chunk": 256}),
+        out_shape=big + grads,
+        in_specs=[anyspace, anyspace] + [vmem] * 4 + [smem] + [vmem] * 5,
+        out_specs=[anyspace, anyspace] + [vmem] * 7,
+        scratch_shapes=scratch,
+        compiler_params=pltpu.CompilerParams(
+            collective_id=0, has_side_effects=True, vmem_limit_bytes=56 * 1024 * 1024
+        ),
+        name="layer",
+    )(
+        edge_lat[0],
+        edge_cot[0],
+        node_lat[0],
+        node_cot[0],
+        senders,
+        receivers,
+        edge_count,
+        *weights,
+    )
+    state_out = [sds(w.shape, f32) for w in weights]
+    return tuple(
+        pl.pallas_call(
+            update_kernel,
+            out_shape=[
+                sds((1, rows, D), bf16),
+                sds((1, n, D), bf16),
+                sds((1, rows, D), bf16),
+                sds((1, n, D), bf16),
+                *state_out,
+                *state_out,
+                *state_out,
+            ],
+            in_specs=[vmem] * 24,
+            out_specs=[vmem] * 19,
+            compiler_params=pltpu.CompilerParams(vmem_limit_bytes=32 * 1024 * 1024),
+            name="update",
+        )(*results, *weights, *firsts, *seconds)
+    )
+
+
 def solution(mesh):
     in_specs = (
         P("grp", "edge", None),
@@ -223,5 +888,6 @@
         P(None, ("edge", "grp")),
     )
     return jax.shard_map(
-        on_device, mesh=mesh, in_specs=in_specs, out_specs=out_specs, check_vma=False
-    )
+        functools.partial(on_device, mesh.shape["edge"], mesh.shape["grp"]),
+        mesh=mesh, in_specs=in_specs, out_specs=out_specs, check_vma=False
+    )

time: 1050 us -> 116 us (0.11)
  waiting for transfers between devices: 729 us -> 0 us
  blocking collectives: 187 us -> 0 us
  Pallas kernels: 0 us -> 106 us
  other arithmetic: 50.2 us -> 0 us
  matrix products: 29 us -> 0 us
  local copies, waits for them, and re-layouts: 36.2 us -> 8 us
  between operations: 15.3 us -> 1.55 us
    reduce_scatter x6 -> x0, waiting for transfers between devices: 587 us -> none  [the longest x1 137 us: on_device(): lax.psum_scatter(g_w1n, ('edge', 'grp'), scatter_dimension=0, tiled=True)]
    all_gather x5 -> x0, blocking collectives: 187 us -> none  [the longest x1 43.4 us: on_device(): lax.all_gather(small_params.astype(bf), ('edge', 'grp'), axis=1, tiled=True)]
    pallas_call x0 -> x2, Pallas kernels: none -> 106 us  [the longest x1 104 us: on_device(): pl.pallas_call(functools.partial(layer_kernel, {'dims': (Z, Y, X, C), 'n_...]
    unnamed x10 -> x0, waiting for transfers between devices: 86.5 us -> none
    all_gather x2 -> x0, waiting for transfers between devices: 55.6 us -> none  [the longest x1 55.6 us: on_device(): lax.all_gather(w_node_in.astype(bf), ('edge', 'grp'), axis=0, tiled=True)]
    dot_general x12 -> x0, matrix products: 29 us -> none  [the longest x4 11.5 us: inner(): lax.dot_general(left, right, (((0,), (0,)), ((), ())), preferred_element_...]
    scatter-add x3 -> x0, other arithmetic: 24 us -> none  [the longest x2 15.7 us: on_device(): dense_grad = dense_grad.at[send].add(d_joined[:, width:2 * width]).at[rec...]
    gather x6 -> x0, local copies, waits for them, and re-layouts: 18 us -> none  [the longest x4 10.5 us: on_device(): joined = jnp.concatenate([edges, whole[send], whole[recv]], axis=1)]
  transfers between devices with their start and end apart: 9 -> 0, of which waited for: 8 -> 0; matrix products, arithmetic and copies ran while one was open for 7% -> 0% of each run, Pallas kernels for 0% -> 0%
where the time goes in v1:
time: 116 us; the launch traced here: 115 us
  Pallas kernels  106 us (91%)
  local copies, waits for them, and re-layouts  8 us (7%)
  between operations  1.55 us (1%)
    pallas_call x1, Pallas kernels, on_device(): pl.pallas_call(functools.partial(layer_kernel, {'dims': (Z, Y, X, C), 'n_...  104 us
    unnamed x48, local copies, waits for them, and re-layouts  8 us

profile of v1, /device:TPU:0, one launch (start us, length us, event | category | flops | bytes accessed | tf_op | source)
XLA Modules:
  0.0 115.1 jit_solution(6572122621841572363)
XLA Ops:
  1.3 0.0 copy-start.2
  1.3 0.0 copy-start.3
  1.3 0.0 copy-start.4
  1.3 0.0 copy-start.5
  1.3 0.0 copy-start.6
  1.4 0.0 copy-start.7
  1.4 0.0 copy-start.9
  1.4 103.7 %layer.1 = (bf16[1024,512]{1,0:T(8,128)(2,1)}, bf16[1024,512]{1,0:T(8,128)(2,1)}, bf16[64,512]{1,0:T(8,128)(2,1)}, bf16[64,512]{1,0:T(8,128)(2,1)}, f32[48,512]{...) custom-call(bf16[1024,512]{1,0:T(8,128)(2,1)} %bitcast.4, ...), custom_call_target="tpu_custom_call" | custom-call | tf_op jit(solution)/shard_map/layer/pallas_call | solution.py:803
  105.1 0.0 copy-start.22
  105.1 0.0 copy-start.21
  105.1 0.0 copy-start.20
  105.3 0.5 copy-done.23
  105.8 0.0 copy-done.22
  105.8 0.0 copy-done.21
  105.8 0.0 copy-done.20
  105.8 1.2 %copy-done = bf16[1024,512]{1,0:T(8,128)(2,1)S(1)} copy-done((bf16[1024,512]{1,0:T(8,128)(2,1)S(1)}, bf16[1024,512]{1,0:T(8,128)(2,1)}, u32[]{:S(2)}) %copy-start) | copy-done | bytes 1048600
  107.1 1.2 %copy-done.1 = bf16[1024,512]{1,0:T(8,128)(2,1)S(1)} copy-done((bf16[1024,512]{1,0:T(8,128)(2,1)S(1)}, bf16[1024,512]{1,0:T(8,128)(2,1)}, u32[]{:S(2)}) %copy-start.1) | copy-done | bytes 1048600
  108.3 0.9 copy-done.8
  109.2 0.8 copy-done.11
  110.0 0.8 copy-done.12
  110.9 0.8 copy-done.13
  111.7 0.8 copy-done.18
  112.5 0.8 copy-done.19
  113.2 1.9 %update.1 = (bf16[1,1024,512]{2,1,0:T(8,128)(2,1)}, bf16[1,64,512]{2,1,0:T(8,128)(2,1)}, bf16[1,1024,512]{2,1,0:T(8,128)(2,1)}, bf16[1,64,512]{2,1,0:T(8,128)(2,...) custom-call(bf16[1024,512]{1,0:T(8,128)(2,1)S(1)} %copy-done, ...), custom_call_target="tpu_custom_call" | custom-call | tf_op jit(solution)/shard_map/update/pallas_call | solution.py:825
  (26 shorter events, 0.1 us)
Async XLA Ops:
  1.3 103.8 %copy-start.2 = (f32[48,512]{1,0:T(8,128)S(1)}, f32[48,512]{1,0:T(8,128)}, u32[]{:S(2)}) copy-start(f32[48,512]{1,0:T(8,128)} %refs_9_.3) | copy-start | bytes 294916
  1.3 103.8 %copy-start.3 = (f32[32,512]{1,0:T(8,128)S(1)}, f32[32,512]{1,0:T(8,128)}, u32[]{:S(2)}) copy-start(f32[32,512]{1,0:T(8,128)} %refs_11_.3) | copy-start | bytes 196612
  1.3 103.8 %copy-start.4 = (f32[16,512]{1,0:T(8,128)S(1)}, f32[16,512]{1,0:T(8,128)}, u32[]{:S(2)}) copy-start(f32[16,512]{1,0:T(8,128)} %refs_10_.3) | copy-start | bytes 98308
  1.3 103.8 %copy-start.5 = (f32[16,512]{1,0:T(8,128)S(1)}, f32[16,512]{1,0:T(8,128)}, u32[]{:S(2)}) copy-start(f32[16,512]{1,0:T(8,128)} %refs_12_.1) | copy-start | bytes 98308
  1.3 103.8 %copy-start.6 = (f32[48,512]{1,0:T(8,128)S(1)}, f32[48,512]{1,0:T(8,128)}, u32[]{:S(2)}) copy-start(f32[48,512]{1,0:T(8,128)} %refs_14_.1) | copy-start | bytes 294916
  1.4 103.8 %copy-start.7 = (f32[48,512]{1,0:T(8,128)S(1)}, f32[48,512]{1,0:T(8,128)}, u32[]{:S(2)}) copy-start(f32[48,512]{1,0:T(8,128)} %refs_19_.1) | copy-start | bytes 294916
  1.4 103.8 %copy-start.9 = (f32[32,512]{1,0:T(8,128)S(1)}, f32[32,512]{1,0:T(8,128)}, u32[]{:S(2)}) copy-start(f32[32,512]{1,0:T(8,128)} %refs_16_.1) | copy-start | bytes 196612
  1.4 103.8 %copy-start.10 = (f32[32,512]{1,0:T(8,128)S(1)}, f32[32,512]{1,0:T(8,128)}, u32[]{:S(2)}) copy-start(f32[32,512]{1,0:T(8,128)} %refs_21_.1) | copy-start | bytes 196612
  1.4 103.8 %copy-start.14 = (f32[16,512]{1,0:T(8,128)S(1)}, f32[16,512]{1,0:T(8,128)}, u32[]{:S(2)}) copy-start(f32[16,512]{1,0:T(8,128)} %refs_15_.1) | copy-start | bytes 98308
  1.4 103.8 %copy-start.15 = (f32[16,512]{1,0:T(8,128)S(1)}, f32[16,512]{1,0:T(8,128)}, u32[]{:S(2)}) copy-start(f32[16,512]{1,0:T(8,128)} %refs_17_.1) | copy-start | bytes 98308
  1.4 103.8 %copy-start.16 = (f32[16,512]{1,0:T(8,128)S(1)}, f32[16,512]{1,0:T(8,128)}, u32[]{:S(2)}) copy-start(f32[16,512]{1,0:T(8,128)} %refs_20_.1) | copy-start | bytes 98308
  1.4 103.8 %copy-start.17 = (f32[16,512]{1,0:T(8,128)S(1)}, f32[16,512]{1,0:T(8,128)}, u32[]{:S(2)}) copy-start(f32[16,512]{1,0:T(8,128)} %refs_22_.1) | copy-start | bytes 98308
  105.1 0.7 copy-start.23
  105.1 0.7 copy-start.22
  105.1 0.7 copy-start.21
  105.1 0.7 copy-start.20
  105.8 1.2 %copy-start = (bf16[1024,512]{1,0:T(8,128)(2,1)S(1)}, bf16[1024,512]{1,0:T(8,128)(2,1)}, u32[]{:S(2)}) copy-start(bf16[1024,512]{1,0:T(8,128)(2,1)} %get-tuple-element.28.refs_0_) | copy-start | bytes 3145732
  107.1 1.2 %copy-start.1 = (bf16[1024,512]{1,0:T(8,128)(2,1)S(1)}, bf16[1024,512]{1,0:T(8,128)(2,1)}, u32[]{:S(2)}) copy-start(bf16[1024,512]{1,0:T(8,128)(2,1)} %get-tuple-element.29.refs_1_) | copy-start | bytes 3145732
  108.3 0.9 copy-start.8
  109.2 0.8 copy-start.11
  110.0 0.8 copy-start.12
  110.9 0.8 copy-start.13
  111.7 0.8 copy-start.18
  112.5 0.8 copy-start.19

commit v2 on v1

--- a/solution.py
+++ b/solution.py
@@ -227,9 +227,8 @@
         w2,
         w3,
         w4,
-        w2v,
-        w3v,
-        w4v,
+        wa,
+        wb,
         pick,
         spread,
         proj,
@@ -313,10 +312,11 @@
         pl.semaphore_signal(barrier, inc=1, device_id=dev, device_id_type=MESH)
 
     nbuf[z, y] = nodes_in[...]
-    r1 = w1_in.shape[0]
-    w1[pl.ds(pl.multiple_of(me * r1, 16), r1), :] = w1_in[...].astype(bf16)
-    for v, own in ((w2v, w2_in), (w3v, w3_in), (w4v, w4_in)):
-        v[z, y, x, c] = own[...].astype(bf16)
+    r1, r2, r3, r4 = (own.shape[0] for own in (w1_in, w2_in, w3_in, w4_in))
+    wa[z, y, x, c, 0:r1, :] = w1_in[...].astype(bf16)
+    wa[z, y, x, c, r1 : r1 + r2, :] = w2_in[...].astype(bf16)
+    wb[z, y, x, c, 0:r3, :] = w3_in[...].astype(bf16)
+    wb[z, y, x, c, r3 : r3 + r4, :] = w4_in[...].astype(bf16)
     ws = small_in.shape[1]
     place = (
         lax.broadcasted_iota(jnp.int32, (ws, D), 1)
@@ -325,52 +325,17 @@
     sm_src[0] = mm(small_in[...].astype(bf16), jnp.where(place, 1.0, 0.0).astype(bf16))
     pl.semaphore_wait(barrier, len(peers))
 
+    sm_z = [push(sm_src.at[0], sm_rcv.at[o - 1], z_dev(o)) for o in range(1, Z)]
+    s = wa.at[z, y, x, c]
+    a_z = [push(s, s, z_dev(o)) for o in range(1, Z)]
+    a_y = [push(s, s, y_dev)]
+    a_x = [push(s, s, x_dev)]
+    a_c = [push(s, s, c_dev)]
     own_n = nbuf.at[z, y]
+    n_y = [push(own_n, own_n, y_dev)]
     n_z = [push(own_n, own_n, z_dev(o)) for o in range(1, Z)]
-    n_y = [push(own_n, own_n, y_dev)]
-
-    def slot(zz, yy, xx):
-        at = (((zz * Y + yy) * X + xx) * C + c) * r1
-        return w1.at[pl.ds(pl.multiple_of(at, 16), r1), :]
-
-    s = slot(z, y, x)
-    w1_z = [push(s, s, z_dev(o)) for o in range(1, Z)]
-    w1_y = [push(s, s, y_dev)]
-    w1_x = [push(s, s, x_dev)]
-    w1_c = [push(s, s, c_dev)]
-    sm_z = [push(sm_src.at[0], sm_rcv.at[o - 1], z_dev(o)) for o in range(1, Z)]
-
-    class Lines:
-        def __init__(self, v):
-            self.v = v
-            s = v.at[z, y, x, c]
-            self.z = [push(s, s, z_dev(o)) for o in range(1, Z)]
-
-        def line(self):
-            for copy in self.z:
-                copy.wait_recv()
-            s = self.v.at[:, y, x, c]
-            self.y = push(s, s, y_dev)
-            self.x = [push(s, s, x_dev)]
-
-        def cross(self):
-            self.y.wait_recv()
-            s = self.v.at[:, yp, x, c]
-            self.x.append(push(s, s, x_dev))
-
-        def pair(self):
-            for copy in self.x:
-                copy.wait_recv()
-            s = self.v.at[:, :, :, c]
-            self.c = push(s, s, c_dev)
-
-        def done(self, whole):
-            self.c.wait_recv()
-            whole[...] = self.v[...].reshape(whole.shape)
-
-    w2_lines = Lines(w2v)
-    w3_lines = Lines(w3v)
-    w4_lines = Lines(w4v)
+    s = wb.at[z, y, x, c]
+    b_z = [push(s, s, z_dev(o)) for o in range(1, Z)]
 
     lane = lax.broadcasted_iota(jnp.int32, (128, N), 1)
     sub = lax.broadcasted_iota(jnp.int32, (N, 128), 0)
@@ -385,17 +350,10 @@
             wide = jnp.broadcast_to(ids[0:1, at], (N, 128))
             spread[half * N : (half + 1) * N, at] = jnp.where(sub == wide, 1.0, 0.0).astype(bf16)
 
-    for o in range(1, Z):
-        n_z[o - 1].wait_recv()
-        s = nbuf.at[z_at(Z - o), y]
-        n_y.append(push(s, s, y_dev))
-    for o in range(1, Z):
-        w1_z[o - 1].wait_recv()
-        s = slot(z_at(Z - o), y, x)
-        w1_y.append(push(s, s, y_dev))
-        w1_x.append(push(s, s, x_dev))
-        w1_c.append(push(s, s, c_dev))
-    w2_lines.line()
+    def settle(zz, yy, xx, cc):
+        k = ((zz * Y + yy) * X + xx) * C + cc
+        w1[pl.ds(pl.multiple_of(k * r1, 16), r1), :] = wa[zz, yy, xx, cc, 0:r1, :]
+        w2[pl.ds(pl.multiple_of(k * r2, 16), r2), :] = wa[zz, yy, xx, cc, r1 : r1 + r2, :]
 
     def small_sum(src, rcv, stage, copies):
         total = src[stage]
@@ -404,31 +362,65 @@
             total = total + rcv[k]
         src[stage + 1] = total
 
+    def on_z(o):
+        a_z[o - 1].wait_recv()
+        s = wa.at[z_at(Z - o), y, x, c]
+        a_y.append(push(s, s, y_dev))
+        a_x.append(push(s, s, x_dev))
+        a_c.append(push(s, s, c_dev))
+        settle(z_at(Z - o), y, x, c)
+
+    def on_y(o):
+        a_y[o].wait_recv()
+        s = wa.at[z_at(Z - o), yp, x, c]
+        a_x.append(push(s, s, x_dev))
+        a_c.append(push(s, s, c_dev))
+        settle(z_at(Z - o), yp, x, c)
+
+    x_order = [(0, 0)]
+    settle(z, y, x, c)
+    for o in range(1, Z):
+        on_z(o)
+        x_order.append((o, 0))
+        on_y(o - 1)
+        x_order.append((o - 1, 1))
     small_sum(sm_src, sm_rcv, 0, [(copy, k) for k, copy in enumerate(sm_z)])
     sm_y = push(sm_src.at[1], sm_rcv.at[Z - 1], y_dev)
-    for o in range(Z):
-        w1_y[o].wait_recv()
-        s = slot(z_at(Z - o), yp, x)
-        w1_x.append(push(s, s, x_dev))
-        w1_c.append(push(s, s, c_dev))
-    w2_lines.cross()
+
+    def on_n(o):
+        n_z[o - 1].wait_recv()
+        s = nbuf.at[z_at(Z - o), y]
+        n_y.append(push(s, s, y_dev))
+
+    on_n(1)
+    on_y(Z - 1)
+    x_order.append((Z - 1, 1))
+    for o in range(2, Z):
+        on_n(o)
     small_sum(sm_src, sm_rcv, 1, [(sm_y, Z - 1)])
     sm_x = push(sm_src.at[2], sm_rcv.at[Z], x_dev)
-    for k in range(Y * Z):
-        w1_x[k].wait_recv()
-        s = slot(z_at(Z - k % Z), y if k < Z else yp, xp)
-        w1_c.append(push(s, s, c_dev))
-    w2_lines.pair()
+    for copy, (o, flip) in zip(list(a_x), x_order):
+        copy.wait_recv()
+        yy = yp if flip else y
+        s = wa.at[z_at(Z - o), yy, xp, c]
+        a_c.append(push(s, s, c_dev))
+        settle(z_at(Z - o), yy, xp, c)
     small_sum(sm_src, sm_rcv, 2, [(sm_x, Z)])
     sm_c = push(sm_src.at[3], sm_rcv.at[Z + 1], c_dev)
-    w3_lines.line()
-    w4_lines.line()
+    for copy in b_z:
+        copy.wait_recv()
+    s = wb.at[:, y, x, c]
+    b_y = push(s, s, y_dev)
+    b_x = [push(s, s, x_dev)]
     for copy in n_y:
         copy.wait_recv()
     edges_copy.wait()
-    for copy in w1_c:
+    for copy in a_c:
         copy.wait_recv()
-    w2_lines.done(w2)
+    for zz in range(Z):
+        for yy in range(Y):
+            for xx in range(X):
+                settle(zz, yy, xx, cp)
     small_sum(sm_src, sm_rcv, 3, [(sm_c, Z + 1)])
 
     nodes_all = nbuf[...].reshape(N, D)
@@ -457,8 +449,11 @@
 
     enew_copy = pltpu.make_async_copy(enew, enew_out, local_sem.at[2])
     enew_copy.start()
-    w3_lines.cross()
-    w4_lines.cross()
+    b_y.wait_recv()
+    s = wb.at[:, yp, x, c]
+    b_x.append(push(s, s, x_dev))
+
+    order = (*range(1, Z), 0)
 
     class NodeSum:
         def __init__(self, total, pb, yr, zs, zr):
@@ -466,11 +461,11 @@
             pf[...] = total.reshape(Z, Y, n, D)
             pb[...] = total.astype(bf16).reshape(Z, Y, n, D)
             self.yr = yr
-            self.y = [push(pb.at[z_at(o), yp], yr.at[o], y_dev) for o in (*range(1, Z), 0)]
+            self.y = [push(pb.at[z_at(o), yp], yr.at[o], y_dev) for o in order]
 
         def turn(self):
             self.z = []
-            for k, o in enumerate((*range(1, Z), 0)):
+            for k, o in enumerate(order):
                 self.y[k].wait_recv()
                 part = pf[z_at(o), y] + self.yr[o].astype(f32)
                 if o == 0:
@@ -487,19 +482,23 @@
             return result
 
     agg_sum = NodeSum(mm(spread[N : 2 * N, :], term[...]), pb_a, yr_a, zs_a, zr_a)
-    w3_lines.pair()
-    w4_lines.pair()
+    for copy in b_x:
+        copy.wait_recv()
+    s = wb.at[:, :, :, c]
+    b_c = push(s, s, c_dev)
     agg_sum.turn()
-    w3_lines.done(w3)
-    w4_lines.done(w4)
+    b_c.wait_recv()
+    w3[...] = wb[:, :, :, :, 0:r3, :].reshape(w3.shape)
+    w4[...] = wb[:, :, :, :, r3 : r3 + r4, :].reshape(w4.shape)
+    own_nodes = nodes_in[...]
+    pre_own = mm(own_nodes, w3[0:D, :])
     agg = agg_sum.total()
 
     def par(k):
         return sm_src[4, k : k + 1, :]
 
-    own_nodes = nodes_in[...]
     agg_low = agg.astype(bf16)
-    pre_n = mm(own_nodes, w3[0:D, :]) + mm(agg_low, w3[D : 2 * D, :]) + par(4)
+    pre_n = pre_own + mm(agg_low, w3[D : 2 * D, :]) + par(4)
     sig_n = jax.nn.sigmoid(pre_n)
     hidden_n = (pre_n * sig_n).astype(bf16)
     out_n = mm(hidden_n, w4[...]) + par(5)
@@ -518,68 +517,70 @@
             self.grad, self.crecv, self.xs, self.xrecv, self.ks = grad, crecv, xs, xrecv, ks
             self.ys, self.yrecv, self.zs, self.zrecv = ys, yrecv, zs, zrecv
 
-        def put(self, first, values):
-            low, r = values.astype(bf16), self.grad.shape[4]
+        def put(self, first, values, lane_rows=None, base=0):
+            low, r = values.astype(bf16), lane_rows or self.grad.shape[4]
             row = 0
             while row < values.shape[0]:
                 k, off = divmod(first + row, r)
                 size = min(r - off, values.shape[0] - row)
                 at = (k // (Y * X * C), k // (X * C) % Y, k // C % X, k % C)
-                self.grad[(*at, slice(off, off + size))] = low[row : row + size]
+                self.grad[(*at, slice(base + off, base + off + size))] = low[row : row + size]
                 row += size
-
-        def rows_of(self, zz, yy, xx):
-            return self.grad[zz, yy, xx, c].astype(f32)
 
         def start(self):
             self.c = [
-                push(self.grad.at[:, :, xx, cp], self.crecv.at[h], c_dev)
-                for h, xx in enumerate((xp, x))
+                push(self.grad.at[:, yy, xx, cp], self.crecv.at[k], c_dev)
+                for k, (yy, xx) in enumerate(((yp, xp), (y, xp), (yp, x), (y, x)))
             ]
 
         def cross_x(self):
-            self.c[0].wait_recv()
             self.x = []
-            for h, yy in enumerate((yp, y)):
-                for zz in range(Z):
-                    part = self.rows_of(zz, yy, xp) + self.crecv[0, zz, yy].astype(f32)
-                    self.xs[h, zz] = part.astype(bf16)
-                self.x.append(push(self.xs.at[h], self.xrecv.at[h], x_dev))
-            self.c[1].wait_recv()
-            for h, yy in enumerate((yp, y)):
-                for zz in range(Z):
-                    self.ks[h, zz] = self.rows_of(zz, yy, x) + self.crecv[1, zz, yy].astype(f32)
+            for k, yy in enumerate((yp, y)):
+                self.c[k].wait_recv()
+                for o in order:
+                    zz = z_at(o)
+                    part = self.grad[zz, yy, xp, c].astype(f32) + self.crecv[k, zz].astype(f32)
+                    self.xs[k, o] = part.astype(bf16)
+                    self.x.append(push(self.xs.at[k, o], self.xrecv.at[k, o], x_dev))
+            for k, yy in enumerate((yp, y)):
+                self.c[2 + k].wait_recv()
+                for o in order:
+                    zz = z_at(o)
+                    self.ks[k, o] = self.grad[zz, yy, x, c].astype(f32) + self.crecv[2 + k, zz].astype(f32)
 
         def cross_y(self):
-            self.x[0].wait_recv()
-            self.ys[...] = (self.ks[0] + self.xrecv[0].astype(f32)).astype(bf16)
-            self.y = push(self.ys, self.yrecv, y_dev)
-            self.x[1].wait_recv()
-            self.ks[1] = self.ks[1] + self.xrecv[1].astype(f32)
+            self.y = []
+            for k, o in enumerate(order):
+                self.x[k].wait_recv()
+                self.ys[o] = (self.ks[0, o] + self.xrecv[0, o].astype(f32)).astype(bf16)
+                self.y.append(push(self.ys.at[o], self.yrecv.at[o], y_dev))
+
+        def gather(self, k, o):
+            self.x[Z + k].wait_recv()
+            self.y[k].wait_recv()
+            return self.ks[1, o] + self.xrecv[1, o].astype(f32) + self.yrecv[o].astype(f32)
 
         def cross_z(self):
-            self.y.wait_recv()
             self.z = []
-            for o in range(1, Z):
-                zz = z_at(o)
-                self.zs[o - 1] = (self.ks[1, zz] + self.yrecv[zz].astype(f32)).astype(bf16)
+            for k, o in enumerate(order[:-1]):
+                self.zs[o - 1] = self.gather(k, o).astype(bf16)
                 self.z.append(push(self.zs.at[o - 1], self.zrecv.at[o - 1], z_dev(o)))
+            self.kept = self.gather(Z - 1, 0)
 
         def total(self):
-            result = self.ks[1, z] + self.yrecv[z].astype(f32)
+            result = self.kept
             for o in range(1, Z):
                 self.z[o - 1].wait_recv()
                 result = result + self.zrecv[o - 1].astype(f32)
             return result
 
-    per = len(grad_refs) // 4
-    sum1, sum2, sum3, sum4 = [WeightSum(*grad_refs[k * per : (k + 1) * per]) for k in range(4)]
-
-    sum3.put(0, inner(own_nodes, d_pre_n))
-    sum3.put(D, inner(agg_low, d_pre_n))
-    sum4.put(0, inner(hidden_n, d_out_n))
-    sum3.start()
-    sum4.start()
+    per = len(grad_refs) // 3
+    sum1, sum2, sum_n = [WeightSum(*grad_refs[k * per : (k + 1) * per]) for k in range(3)]
+
+    sum_n.put(0, inner(own_nodes, d_pre_n), r3)
+    sum_n.put(D, inner(agg_low, d_pre_n), r3)
+    sum_n.put(0, inner(hidden_n, d_out_n), r4, r3)
+    sum_n.start()
     nnew_out[...] = (own_nodes.astype(f32) + normed_n * par(6) + par(7)).astype(bf16)
     node_part = ncot + times_t(d_pre_n, w3[0:D, :])
     gsm[4:5, :] = jnp.sum(d_pre_n.astype(f32), axis=0, keepdims=True)
@@ -590,8 +591,7 @@
         d_z[o - 1].wait_recv()
         s = dbuf.at[z_at(Z - o), y]
         d_y.append(push(s, s, y_dev))
-    sum3.cross_x()
-    sum4.cross_x()
+    sum_n.cross_x()
     cot_copy.wait()
     for copy in d_y:
         copy.wait_recv()
@@ -599,8 +599,7 @@
     sums[...] = jnp.zeros_like(sums)
     d_all = dbuf[...].reshape(N, D)
 
-    @pl.loop(0, rows // R)
-    def _(i):
+    def edge_back(i):
         at = pl.ds(pl.multiple_of(i * R, R), R)
         live = row_id < count - i * R
         d_edge = cot[at, :].astype(f32) + jnp.where(live, mm(pick[at, N : 2 * N], d_all), 0.0)
@@ -618,11 +617,27 @@
         dpre[at, :] = d_pre
         sums[0] += fold_rows(d_pre.astype(f32))
 
-    sum3.cross_y()
-    sum4.cross_y()
+    half = rows // R // 2
+    pl.loop(0, half)(edge_back)
+    sum_n.cross_y()
+    pl.loop(half, rows // R)(edge_back)
+    sum2.put(0, inner(hidden[...], dout[...]))
+    sum2.start()
+    for k in range(4):
+        gsm[k : k + 1, :] = jnp.sum(sums[k], axis=0, keepdims=True)
+    gm_src[0] = gsm[...]
+    gm_c = push(gm_src.at[0], gm_rcv.at[0], c_dev)
+    sum_n.cross_z()
     d_pre = dpre[...]
+    sum1.put(0, inner(edges[...], d_pre))
+    sum2.cross_x()
+    small_sum(gm_src, gm_rcv, 0, [(gm_c, 0)])
+    gm_x = push(gm_src.at[1], gm_rcv.at[1], x_dev)
     seg[0:N, :] = mm(spread[0:N, :], d_pre).astype(bf16)
     seg[N : 2 * N, :] = mm(spread[N : 2 * N, :], d_pre).astype(bf16)
+    sum1.put(D, inner(nodes_all, seg[0:N, :]))
+    sum1.put(2 * D, inner(nodes_all, seg[N : 2 * N, :]))
+    sum1.start()
     node_sum = NodeSum(
         times_t(seg[0:N, :], w1[D : 2 * D, :]) + times_t(seg[N : 2 * N, :], w1[2 * D : 3 * D, :]),
         pb_n,
@@ -630,23 +645,14 @@
         zs_n,
         zr_n,
     )
-    sum2.put(0, inner(hidden[...], dout[...]))
-    sum2.start()
-    sum1.put(D, inner(nodes_all, seg[0:N, :]))
-    sum1.put(2 * D, inner(nodes_all, seg[N : 2 * N, :]))
-    sum1.put(0, inner(edges[...], d_pre))
-    sum1.start()
-    for k in range(4):
-        gsm[k : k + 1, :] = jnp.sum(sums[k], axis=0, keepdims=True)
-    gm_src[0] = gsm[...]
-    gm_c = push(gm_src.at[0], gm_rcv.at[0], c_dev)
+    sum1.cross_x()
+    small_sum(gm_src, gm_rcv, 1, [(gm_x, 1)])
+    gm_y = push(gm_src.at[2], gm_rcv.at[2], y_dev)
+    sum2.cross_y()
     node_sum.turn()
-    sum3.cross_z()
-    sum4.cross_z()
-    sum2.cross_x()
-    sum1.cross_x()
-    small_sum(gm_src, gm_rcv, 0, [(gm_c, 0)])
-    gm_x = push(gm_src.at[1], gm_rcv.at[1], x_dev)
+    sum2.cross_z()
+    small_sum(gm_src, gm_rcv, 2, [(gm_y, 2)])
+    gm_z = [push(gm_src.at[3], gm_rcv.at[2 + o], z_dev(o)) for o in range(1, Z)]
 
     @pl.loop(0, rows // R)
     def _(i):
@@ -655,19 +661,12 @@
 
     egrad_copy = pltpu.make_async_copy(egrad, egrad_out, local_sem.at[3])
     egrad_copy.start()
-    sum2.cross_y()
     sum1.cross_y()
-    small_sum(gm_src, gm_rcv, 1, [(gm_x, 1)])
-    gm_y = push(gm_src.at[2], gm_rcv.at[2], y_dev)
     ngrad_out[...] = (node_part + node_sum.total()).astype(bf16)
-    g3_out[...] = sum3.total()
-    g4_out[...] = sum4.total()
-    sum2.cross_z()
-    sum1.cross_z()
-    small_sum(gm_src, gm_rcv, 2, [(gm_y, 2)])
-    gm_z = [push(gm_src.at[3], gm_rcv.at[2 + o], z_dev(o)) for o in range(1, Z)]
+    total_n = sum_n.total()
+    g3_out[...] = total_n[0:r3]
+    g4_out[...] = total_n[r3 : r3 + r4]
     g2_out[...] = sum2.total()
-    g1_out[...] = sum1.total()
     small_sum(gm_src, gm_rcv, 3, [(copy, 3 + k) for k, copy in enumerate(gm_z)])
     take = (
         lax.broadcasted_iota(jnp.int32, (D, ws), 0)
@@ -679,6 +678,8 @@
         preferred_element_type=f32,
         precision=lax.Precision.HIGHEST,
     )
+    sum1.cross_z()
+    g1_out[...] = sum1.total()
     for copy in started:
         copy.wait_send()
     enew_copy.wait()
@@ -735,7 +736,7 @@
     if not fits:
         return native(*args)
     Z, Y, X, C = n_edge // 2, 2, 2, 2
-    n_sem = 160
+    n_sem = 200
 
     def vm(shape, dtype=bf16):
         return pltpu.VMEM(shape, dtype)
@@ -746,7 +747,8 @@
         vm((Z, Y, n, D)),
         vm((Z, Y, n, D)),
         *[vm((r * n_dev, D)) for r in shards],
-        *[vm((Z, Y, X, C, r, D)) for r in shards[1:]],
+        vm((Z, Y, X, C, shards[0] + shards[1], D)),
+        vm((Z, Y, X, C, shards[2] + shards[3], D)),
         vm((rows, 2 * N)),
         vm((2 * N, rows)),
         vm((2 * N, D)),
@@ -777,10 +779,10 @@
         vm((Z + 2, 8, D), f32),
         vm((8, D), f32),
     ]
-    for r in shards:
+    for r in (shards[0], shards[1], shards[2] + shards[3]):
         scratch += [
             vm((Z, Y, X, C, r, D)),
-            vm((2, Z, Y, r, D)),
+            vm((4, Z, r, D)),
             vm((2, Z, r, D)),
             vm((2, Z, r, D)),
             vm((2, Z, r, D), f32),
@@ -835,7 +837,7 @@
             ],
             in_specs=[vmem] * 24,
             out_specs=[vmem] * 19,
-            compiler_params=pltpu.CompilerParams(vmem_limit_bytes=32 * 1024 * 1024),
+            compiler_params=pltpu.CompilerParams(vmem_limit_bytes=60 * 1024 * 1024),
             name="update",
         )(*results, *weights, *firsts, *seconds)
     )

time: 116 us -> 97.2 us (0.84)
  Pallas kernels: 106 us -> 95.7 us
  local copies, waits for them, and re-layouts: 8 us -> 0 us
    pallas_call x1, Pallas kernels: 104 us -> 92.1 us  [on_device(): pl.pallas_call(functools.partial(layer_kernel, {'dims': (Z, Y, X, C), 'n_...]
    unnamed x48 -> x0, local copies, waits for them, and re-layouts: 8 us -> none
    pallas_call x1, Pallas kernels: 1.85 us -> 3.61 us  [on_device(): pl.pallas_call(update_kernel, out_shape=[sds((1, rows, D), bf16), sds((1,...]
where the time goes in v2:
time: 97.2 us; the launch traced here: 97 us
  Pallas kernels  95.7 us (98%)
  between operations  1.31 us (1%)
    pallas_call x1, Pallas kernels, on_device(): pl.pallas_call(functools.partial(layer_kernel, {'dims': (Z, Y, X, C), 'n_...  92.1 us
    pallas_call x1, Pallas kernels, on_device(): pl.pallas_call(update_kernel, out_shape=[sds((1, rows, D), bf16), sds((1,...  3.61 us

profile of v2, /device:TPU:0, one launch (start us, length us, event | category | flops | bytes accessed | tf_op | source)
XLA Modules:
  0.0 97.0 jit_solution(12518038466774743190)
XLA Ops:
  1.3 92.1 %layer.1 = (bf16[1024,512]{1,0:T(8,128)(2,1)}, bf16[1024,512]{1,0:T(8,128)(2,1)}, bf16[64,512]{1,0:T(8,128)(2,1)}, bf16[64,512]{1,0:T(8,128)(2,1)}, f32[48,512]{...) custom-call(bf16[1024,512]{1,0:T(8,128)(2,1)} %bitcast.4, ...), custom_call_target="tpu_custom_call" | custom-call | tf_op jit(solution)/shard_map/layer/pallas_call | solution.py:805
  93.4 3.6 %update.1 = (bf16[1,1024,512]{2,1,0:T(8,128)(2,1)}, bf16[1,64,512]{2,1,0:T(8,128)(2,1)}, bf16[1,1024,512]{2,1,0:T(8,128)(2,1)}, bf16[1,64,512]{2,1,0:T(8,128)(2,...) custom-call(bf16[1024,512]{1,0:T(8,128)(2,1)} %get-tuple-element.28., ...), custom_call_target="tpu_custom_call" | custom-call | tf_op jit(solution)/shard_map/update/pallas_call | solution.py:827

commit v3 on v2

--- a/solution.py
+++ b/solution.py
@@ -194,24 +194,46 @@
     return jnp.sum(values.reshape(count // 8, 8, width), axis=0)
 
 
+GEO = {
+    "chunk": 256,
+    "gather": (
+        "n0", "y0.0", "y0.1", "z1.0", "z2.0", "z1.1", "z2.1", "y1.0", "y2.0", "s0", "z3.0", "s1",
+        "y2.1", "z3.1", "y1.1", "n1", "n2", "b0", "y3.0", "n3", "s2", "y3.1"
+    ),
+    "late": (
+        "b1", "b2", "l0", "l1", "l2"
+    ),
+    "mid": (
+        "b3", "l3"
+    ),
+    "tail": (
+        "wa", "zn3", "wb", "xa0", "zn2", "ns", "xb0", "g_0", "xb1", "zn1", "xb3", "wc", "ng3",
+        "xa2", "xa1", "ng2", "ya3", "nh2", "nh3", "xa3", "ng1", "ya2", "xb2", "g_1", "ya1", "nh1",
+        "xc0", "ng0", "yb3", "xc1", "za3", "ya0", "zn0", "yb1", "za2", "yb2", "xc3", "g_2", "za1",
+        "yb0", "xc2", "yc3", "zb3", "e", "yc1", "zb1", "yc2", "zb2", "zb0", "za0", "nh0", "tn",
+        "g_3", "zc3", "zc1", "g_4", "zc2", "yc0", "zc0", "tb", "ta", "tN", "tc"
+    ),
+}
+
+
 def layer_kernel(geo, *refs):
     Z, Y, X, C = geo["dims"]
     n_sem = geo["n_sem"]
     (
         edges_hbm,
         cot_hbm,
-        nodes_in,
-        ncot_in,
-        send_in,
-        recv_in,
+        nodes_hbm,
+        ncot_hbm,
+        send_hbm,
+        recv_hbm,
         count_in,
-        w1_in,
-        w2_in,
-        w3_in,
-        w4_in,
-        small_in,
-        enew_out,
-        egrad_out,
+        w1_hbm,
+        w2_hbm,
+        w3_hbm,
+        w4_hbm,
+        small_hbm,
+        enew,
+        egrad,
         nnew_out,
         ngrad_out,
         g1_out,
@@ -221,6 +243,15 @@
         gs_out,
         edges,
         cot,
+        nodes_in,
+        ncot_in,
+        send_in,
+        recv_in,
+        w1_in,
+        w2_in,
+        w3_in,
+        w4_in,
+        small_in,
         nbuf,
         dbuf,
         w1,
@@ -237,11 +268,9 @@
         normed,
         rstd,
         term,
-        enew,
         dedge,
         dout,
         dpre,
-        egrad,
         sums,
         pf,
         pb_a,
@@ -255,8 +284,11 @@
         seg,
         sm_src,
         sm_rcv,
+        sm_tile,
+        par_all,
         gm_src,
         gm_rcv,
+        gm_tile,
         gsm,
         *grad_refs,
     ) = refs
@@ -279,11 +311,15 @@
     x_dev = (e_id, xp * C + c)
     c_dev = (e_id, x * C + cp)
 
-    def z_at(o):
-        return lax.rem(z + o, Z)
-
-    def z_dev(o):
-        return (z_at(o) * Y + y, g_id)
+    def zx(m):
+        place = z
+        for j in range(m.bit_length()):
+            if m >> j & 1:
+                place = place + (1 << j) - (2 << j) * (z // (1 << j) % 2)
+        return place
+
+    def z_dev(m):
+        return (zx(m) * Y + y, g_id)
 
     started = []
 
@@ -302,41 +338,46 @@
         started.append(copy)
         return copy
 
-    edges_copy = pltpu.make_async_copy(edges_hbm, edges, local_sem.at[0])
-    cot_copy = pltpu.make_async_copy(cot_hbm, cot, local_sem.at[1])
-    edges_copy.start()
-    cot_copy.start()
     barrier = pltpu.get_barrier_semaphore()
-    peers = [z_dev(o) for o in range(1, Z)] + [y_dev, x_dev, c_dev]
+    peers = [z_dev(m) for m in range(1, Z)] + [y_dev, x_dev, c_dev]
     for dev in peers:
         pl.semaphore_signal(barrier, inc=1, device_id=dev, device_id_type=MESH)
-
-    nbuf[z, y] = nodes_in[...]
+    loads = [
+        (w1_hbm, w1_in),
+        (w2_hbm, w2_in),
+        (w3_hbm, w3_in),
+        (w4_hbm, w4_in),
+        (small_hbm, small_in),
+        (nodes_hbm, nodes_in),
+        (send_hbm, send_in),
+        (recv_hbm, recv_in),
+        (ncot_hbm, ncot_in),
+        (edges_hbm, edges),
+        (cot_hbm, cot),
+    ]
+    loads = [pltpu.make_async_copy(*pair, local_sem.at[k]) for k, pair in enumerate(loads)]
+    for load in loads:
+        load.start()
+    for load in loads[0:6]:
+        load.wait()
     r1, r2, r3, r4 = (own.shape[0] for own in (w1_in, w2_in, w3_in, w4_in))
+    ra = r1 + r2
     wa[z, y, x, c, 0:r1, :] = w1_in[...].astype(bf16)
-    wa[z, y, x, c, r1 : r1 + r2, :] = w2_in[...].astype(bf16)
+    wa[z, y, x, c, r1:ra, :] = w2_in[...].astype(bf16)
     wb[z, y, x, c, 0:r3, :] = w3_in[...].astype(bf16)
     wb[z, y, x, c, r3 : r3 + r4, :] = w4_in[...].astype(bf16)
+    nbuf[z, y] = nodes_in[...]
     ws = small_in.shape[1]
+    wide = ws * Y * X * C
+    first = me % (Y * X * C) * ws
     place = (
-        lax.broadcasted_iota(jnp.int32, (ws, D), 1)
-        == lax.broadcasted_iota(jnp.int32, (ws, D), 0) + me * ws
+        lax.broadcasted_iota(jnp.int32, (ws, wide), 1)
+        == lax.broadcasted_iota(jnp.int32, (ws, wide), 0) + first
     )
     sm_src[0] = mm(small_in[...].astype(bf16), jnp.where(place, 1.0, 0.0).astype(bf16))
-    pl.semaphore_wait(barrier, len(peers))
-
-    sm_z = [push(sm_src.at[0], sm_rcv.at[o - 1], z_dev(o)) for o in range(1, Z)]
-    s = wa.at[z, y, x, c]
-    a_z = [push(s, s, z_dev(o)) for o in range(1, Z)]
-    a_y = [push(s, s, y_dev)]
-    a_x = [push(s, s, x_dev)]
-    a_c = [push(s, s, c_dev)]
-    own_n = nbuf.at[z, y]
-    n_y = [push(own_n, own_n, y_dev)]
-    n_z = [push(own_n, own_n, z_dev(o)) for o in range(1, Z)]
-    s = wb.at[z, y, x, c]
-    b_z = [push(s, s, z_dev(o)) for o in range(1, Z)]
-
+
+    for load in loads[6:9]:
+        load.wait()
     lane = lax.broadcasted_iota(jnp.int32, (128, N), 1)
     sub = lax.broadcasted_iota(jnp.int32, (N, 128), 0)
 
@@ -347,81 +388,128 @@
             row = jnp.broadcast_to(ids[0:1, at], (128, 128))
             col = jnp.tile(row.T, (1, N // 128))
             pick[at, half * N : (half + 1) * N] = jnp.where(lane == col, 1.0, 0.0).astype(bf16)
-            wide = jnp.broadcast_to(ids[0:1, at], (N, 128))
-            spread[half * N : (half + 1) * N, at] = jnp.where(sub == wide, 1.0, 0.0).astype(bf16)
+            flat = jnp.broadcast_to(ids[0:1, at], (N, 128))
+            spread[half * N : (half + 1) * N, at] = jnp.where(sub == flat, 1.0, 0.0).astype(bf16)
+
+    pl.semaphore_wait(barrier, len(peers))
+
+    def along_z(own):
+        return {1 << j: push(own, own, z_dev(1 << j)) for j in reversed(range((Z - 1).bit_length()))}
+
+    def arrive_z(copies, m, block):
+        copies[m].wait_recv()
+        j = 0
+        while not m >> j & 1:
+            copies[m | 1 << j] = push(block, block, z_dev(1 << j))
+            j += 1
+
+    halves = ra // 2
+
+    def part(zz, yy, xx, h):
+        return wa.at[zz, yy, xx, c, h * halves : (h + 1) * halves, :]
+
+    def send(block, dev):
+        return push(block, block, dev)
 
     def settle(zz, yy, xx, cc):
         k = ((zz * Y + yy) * X + xx) * C + cc
         w1[pl.ds(pl.multiple_of(k * r1, 16), r1), :] = wa[zz, yy, xx, cc, 0:r1, :]
-        w2[pl.ds(pl.multiple_of(k * r2, 16), r2), :] = wa[zz, yy, xx, cc, r1 : r1 + r2, :]
-
-    def small_sum(src, rcv, stage, copies):
-        total = src[stage]
-        for copy, k in copies:
-            copy.wait_recv()
-            total = total + rcv[k]
-        src[stage + 1] = total
-
-    def on_z(o):
-        a_z[o - 1].wait_recv()
-        s = wa.at[z_at(Z - o), y, x, c]
-        a_y.append(push(s, s, y_dev))
-        a_x.append(push(s, s, x_dev))
-        a_c.append(push(s, s, c_dev))
-        settle(z_at(Z - o), y, x, c)
-
-    def on_y(o):
-        a_y[o].wait_recv()
-        s = wa.at[z_at(Z - o), yp, x, c]
-        a_x.append(push(s, s, x_dev))
-        a_c.append(push(s, s, c_dev))
-        settle(z_at(Z - o), yp, x, c)
-
-    x_order = [(0, 0)]
+        w2[pl.ds(pl.multiple_of(k * r2, 16), r2), :] = wa[zz, yy, xx, cc, r1:ra, :]
+
+    def small_sum(src, rcv, stage, copy):
+        copy.wait_recv()
+        src[stage + 1] = src[stage] + rcv[stage]
+
+    small = [push(sm_src.at[0], sm_rcv.at[0], c_dev)]
+    a_z, a_y, a_x, a_c, x_order = ({}, {}), {}, [], [], []
+    n_z, n_y, b_z, b_y, b_x = {}, [], {}, [], []
+    for h in range(2):
+        own = part(z, y, x, h)
+        a_z[h].update(along_z(own))
+        a_y[0, h] = send(own, y_dev)
+        a_x.append(send(own, x_dev))
+        x_order.append((0, 0, h))
+    a_c.append(send(wa.at[z, y, x, c], c_dev))
+
+    def across(m, flip, h):
+        yy = yp if flip else y
+        a_x.append(send(part(zx(m), yy, x, h), x_dev))
+        x_order.append((m, flip, h))
+        if h == 1:
+            a_c.append(send(wa.at[zx(m), yy, x, c], c_dev))
+            settle(zx(m), yy, x, c)
+
+    def on_z(m, h):
+        block = part(zx(m), y, x, h)
+        arrive_z(a_z[h], m, block)
+        a_y[m, h] = send(block, y_dev)
+        across(m, 0, h)
+
+    def on_y(m, h):
+        a_y[m, h].wait_recv()
+        across(m, 1, h)
+
+    def on_n(m, _):
+        block = nbuf.at[zx(m), y]
+        if m == 0:
+            n_z.update(along_z(block))
+        else:
+            arrive_z(n_z, m, block)
+        n_y.append(send(block, y_dev))
+
+    def on_b(m, _):
+        block = wb.at[zx(m), y, x, c]
+        if m == 0:
+            b_z.update(along_z(block))
+        else:
+            arrive_z(b_z, m, block)
+
+    def line_b(m, _):
+        block = wb.at[zx(m), y, x, c]
+        b_y.append(send(block, y_dev))
+        b_x.append(send(block, x_dev))
+
+    def on_x(first, last):
+        for k in range(first, last):
+            m, flip, h = x_order[k]
+            a_x[k].wait_recv()
+            if h == 1:
+                yy = yp if flip else y
+                a_c.append(send(wa.at[zx(m), yy, xp, c], c_dev))
+                settle(zx(m), yy, xp, c)
+
+    def on_small(k, _):
+        small_sum(sm_src, sm_rcv, k, small[k])
+        if k < 2:
+            small.append(push(sm_src.at[k + 1], sm_rcv.at[k + 1], (y_dev, x_dev)[k]))
+        else:
+            sm_tile[z] = sm_src[3]
+            small.extend(push(sm_src.at[3], sm_tile.at[z], z_dev(m)) for m in range(1, Z))
+
     settle(z, y, x, c)
-    for o in range(1, Z):
-        on_z(o)
-        x_order.append((o, 0))
-        on_y(o - 1)
-        x_order.append((o - 1, 1))
-    small_sum(sm_src, sm_rcv, 0, [(copy, k) for k, copy in enumerate(sm_z)])
-    sm_y = push(sm_src.at[1], sm_rcv.at[Z - 1], y_dev)
-
-    def on_n(o):
-        n_z[o - 1].wait_recv()
-        s = nbuf.at[z_at(Z - o), y]
-        n_y.append(push(s, s, y_dev))
-
-    on_n(1)
-    on_y(Z - 1)
-    x_order.append((Z - 1, 1))
-    for o in range(2, Z):
-        on_n(o)
-    small_sum(sm_src, sm_rcv, 1, [(sm_y, Z - 1)])
-    sm_x = push(sm_src.at[2], sm_rcv.at[Z], x_dev)
-    for copy, (o, flip) in zip(list(a_x), x_order):
-        copy.wait_recv()
-        yy = yp if flip else y
-        s = wa.at[z_at(Z - o), yy, xp, c]
-        a_c.append(push(s, s, c_dev))
-        settle(z_at(Z - o), yy, xp, c)
-    small_sum(sm_src, sm_rcv, 2, [(sm_x, Z)])
-    sm_c = push(sm_src.at[3], sm_rcv.at[Z + 1], c_dev)
-    for copy in b_z:
-        copy.wait_recv()
-    s = wb.at[:, y, x, c]
-    b_y = push(s, s, y_dev)
-    b_x = [push(s, s, x_dev)]
+    steps = {"z": on_z, "y": on_y, "n": on_n, "b": on_b, "l": line_b, "x": on_x, "s": on_small}
+    for step in geo["gather"]:
+        kind, (m, h) = step[0], ([int(v) for v in step[1:].split(".")] + [0])[:2]
+        if kind in "xs" or m < Z:
+            steps[kind](m, h)
+    on_x(0, len(x_order))
     for copy in n_y:
         copy.wait_recv()
-    edges_copy.wait()
+    loads[9].wait()
     for copy in a_c:
         copy.wait_recv()
+    for step in geo["late"]:
+        kind, m = step[0], int(step[1:])
+        if m < Z:
+            steps[kind](m, 0)
     for zz in range(Z):
         for yy in range(Y):
             for xx in range(X):
                 settle(zz, yy, xx, cp)
-    small_sum(sm_src, sm_rcv, 3, [(sm_c, Z + 1)])
+    for copy in small[3:]:
+        copy.wait_recv()
+    for zz in range(Z):
+        par_all[:, zz * wide : (zz + 1) * wide] = sm_tile[zz]
 
     nodes_all = nbuf[...].reshape(N, D)
     proj[0:N, :] = mm(nodes_all, w1[D : 2 * D, :]).astype(bf16)
@@ -429,65 +517,78 @@
     count = count_in[0, 0]
     row_id = lax.broadcasted_iota(jnp.int32, (R, D), 0)
 
-    @pl.loop(0, rows // R)
-    def _(i):
+    def edge_forward(i):
         at = pl.ds(pl.multiple_of(i * R, R), R)
         live = row_id < count - i * R
         own = edges[at, :]
-        pre = mm(own, w1[0:D, :]) + mm(pick[at, :], proj[...]) + sm_src[4, 0:1, :]
+        pre = mm(own, w1[0:D, :]) + mm(pick[at, :], proj[...]) + par_all[0:1, :]
         sig = jax.nn.sigmoid(pre)
         act = (pre * sig).astype(bf16)
         hidden[at, :] = act
         slope[at, :] = sig * (1.0 + pre * (1.0 - sig))
-        out = mm(act, w2[...]) + sm_src[4, 1:2, :]
+        out = mm(act, w2[...]) + par_all[1:2, :]
         norm, inv = norm_stats(out)
         normed[at, :] = norm
         rstd[at, :] = jnp.broadcast_to(inv, (R, 128))
-        new = own.astype(f32) + jnp.where(live, norm * sm_src[4, 2:3, :] + sm_src[4, 3:4, :], 0.0)
+        new = own.astype(f32) + jnp.where(live, norm * par_all[2:3, :] + par_all[3:4, :], 0.0)
         enew[at, :] = new.astype(bf16)
         term[at, :] = jnp.where(live, new, 0.0).astype(bf16)
 
-    enew_copy = pltpu.make_async_copy(enew, enew_out, local_sem.at[2])
-    enew_copy.start()
-    b_y.wait_recv()
-    s = wb.at[:, yp, x, c]
-    b_x.append(push(s, s, x_dev))
-
-    order = (*range(1, Z), 0)
+    half = rows // R // 2
+    pl.loop(0, half)(edge_forward)
+    for step in geo["mid"]:
+        kind, m = step[0], int(step[1:])
+        if m < Z:
+            steps[kind](m, 0)
+    pl.loop(half, rows // R)(edge_forward)
+
+    order = tuple(reversed(range(Z)))
 
     class NodeSum:
         def __init__(self, total, pb, yr, zs, zr):
-            self.zs, self.zr = zs, zr
-            pf[...] = total.reshape(Z, Y, n, D)
-            pb[...] = total.astype(bf16).reshape(Z, Y, n, D)
-            self.yr = yr
-            self.y = [push(pb.at[z_at(o), yp], yr.at[o], y_dev) for o in order]
-
-        def turn(self):
-            self.z = []
-            for k, o in enumerate(order):
-                self.y[k].wait_recv()
-                part = pf[z_at(o), y] + self.yr[o].astype(f32)
-                if o == 0:
-                    self.kept = part
-                else:
-                    self.zs[o - 1] = part.astype(bf16)
-                    self.z.append(push(self.zs.at[o - 1], self.zr.at[o - 1], z_dev(o)))
+            self.yr, self.zs, self.zr = yr, zs, zr
+            pf[...] = total.reshape(Z, Y, 2, n // 2, D)
+            pb[...] = total.astype(bf16).reshape(Z, Y, 2, n // 2, D)
+            self.y = {
+                (m, h): push(pb.at[zx(m), yp, h], yr.at[m, h], y_dev) for m in order for h in range(2)
+            }
+
+            self.z = {}
+
+        def turn(self, m, h):
+            self.y[m, h].wait_recv()
+            part = pf[zx(m), y, h] + self.yr[m, h].astype(f32)
+            if m == 0:
+                pf[z, y, h] = part
+            else:
+                self.zs[m - 1, h] = part.astype(bf16)
+                self.z[m, h] = push(self.zs.at[m - 1, h], self.zr.at[m - 1, h], z_dev(m))
 
         def total(self):
-            result = self.kept
-            for o in range(1, Z):
-                self.z[o - 1].wait_recv()
-                result = result + self.zr[o - 1].astype(f32)
-            return result
+            sums = []
+            for h in range(2):
+                part = pf[z, y, h]
+                for m in range(1, Z):
+                    self.z[m, h].wait_recv()
+                    part = part + self.zr[m - 1, h].astype(f32)
+                sums.append(part)
+            return jnp.concatenate(sums, axis=0)
 
     agg_sum = NodeSum(mm(spread[N : 2 * N, :], term[...]), pb_a, yr_a, zs_a, zr_a)
-    for copy in b_x:
+    for copy in b_y:
         copy.wait_recv()
-    s = wb.at[:, :, :, c]
-    b_c = push(s, s, c_dev)
-    agg_sum.turn()
-    b_c.wait_recv()
+    b_x.append(send(wb.at[:, yp, x, c], x_dev))
+    b_c = [send(wb.at[:, yy, x, c], c_dev) for yy in (y, yp)]
+    for m in order:
+        for h in range(2):
+            agg_sum.turn(m, h)
+    for copy in b_x[:-1]:
+        copy.wait_recv()
+    b_c.append(send(wb.at[:, y, xp, c], c_dev))
+    b_x[-1].wait_recv()
+    b_c.append(send(wb.at[:, yp, xp, c], c_dev))
+    for copy in b_c:
+        copy.wait_recv()
     w3[...] = wb[:, :, :, :, 0:r3, :].reshape(w3.shape)
     w4[...] = wb[:, :, :, :, r3 : r3 + r4, :].reshape(w4.shape)
     own_nodes = nodes_in[...]
@@ -495,7 +596,7 @@
     agg = agg_sum.total()
 
     def par(k):
-        return sm_src[4, k : k + 1, :]
+        return par_all[k : k + 1, :]
 
     agg_low = agg.astype(bf16)
     pre_n = pre_own + mm(agg_low, w3[D : 2 * D, :]) + par(4)
@@ -508,9 +609,15 @@
     slope_n = sig_n * (1.0 + pre_n * (1.0 - sig_n))
     d_pre_n = (times_t(d_out_n, w4[...]) * slope_n).astype(bf16)
     dbuf[z, y] = times_t(d_pre_n, w3[D : 2 * D, :]).astype(bf16)
-    own_d = dbuf.at[z, y]
-    d_z = [push(own_d, own_d, z_dev(o)) for o in range(1, Z)]
-    d_y = [push(own_d, own_d, y_dev)]
+    d_z, d_y = {}, []
+
+    def d_part(m, h):
+        return dbuf.at[zx(m), y, h * (n // 2) : (h + 1) * (n // 2), :]
+
+    for h in range(2):
+        for m in order[:-1]:
+            d_z[m, h] = send(d_part(0, h), z_dev(m))
+        d_y.append(send(d_part(0, h), y_dev))
 
     class WeightSum:
         def __init__(self, grad, crecv, xs, xrecv, ks, ys, yrecv, zs, zrecv):
@@ -533,49 +640,43 @@
                 for k, (yy, xx) in enumerate(((yp, xp), (y, xp), (yp, x), (y, x)))
             ]
 
-        def cross_x(self):
-            self.x = []
-            for k, yy in enumerate((yp, y)):
-                self.c[k].wait_recv()
-                for o in order:
-                    zz = z_at(o)
-                    part = self.grad[zz, yy, xp, c].astype(f32) + self.crecv[k, zz].astype(f32)
-                    self.xs[k, o] = part.astype(bf16)
-                    self.x.append(push(self.xs.at[k, o], self.xrecv.at[k, o], x_dev))
-            for k, yy in enumerate((yp, y)):
-                self.c[2 + k].wait_recv()
-                for o in order:
-                    zz = z_at(o)
-                    self.ks[k, o] = self.grad[zz, yy, x, c].astype(f32) + self.crecv[2 + k, zz].astype(f32)
-
-        def cross_y(self):
-            self.y = []
-            for k, o in enumerate(order):
-                self.x[k].wait_recv()
-                self.ys[o] = (self.ks[0, o] + self.xrecv[0, o].astype(f32)).astype(bf16)
-                self.y.append(push(self.ys.at[o], self.yrecv.at[o], y_dev))
-
-        def gather(self, k, o):
-            self.x[Z + k].wait_recv()
-            self.y[k].wait_recv()
-            return self.ks[1, o] + self.xrecv[1, o].astype(f32) + self.yrecv[o].astype(f32)
-
-        def cross_z(self):
-            self.z = []
-            for k, o in enumerate(order[:-1]):
-                self.zs[o - 1] = self.gather(k, o).astype(bf16)
-                self.z.append(push(self.zs.at[o - 1], self.zrecv.at[o - 1], z_dev(o)))
-            self.kept = self.gather(Z - 1, 0)
+            self.x, self.y, self.z = {}, {}, {}
+
+        def cross_x(self, k):
+            self.c[k].wait_recv()
+            for m in order:
+                part = self.grad[zx(m), (yp, y)[k % 2], (xp, x)[k // 2], c].astype(f32)
+                part = part + self.crecv[k, zx(m)].astype(f32)
+                if k < 2:
+                    self.xs[k, m] = part.astype(bf16)
+                    self.x[k, m] = push(self.xs.at[k, m], self.xrecv.at[k, m], x_dev)
+                else:
+                    self.ks[k - 2, m] = part
+
+        def cross_y(self, m):
+            self.x[0, m].wait_recv()
+            self.ys[m] = (self.ks[0, m] + self.xrecv[0, m].astype(f32)).astype(bf16)
+            self.y[m] = push(self.ys.at[m], self.yrecv.at[m], y_dev)
+
+        def cross_z(self, m):
+            self.x[1, m].wait_recv()
+            self.y[m].wait_recv()
+            part = self.ks[1, m] + self.xrecv[1, m].astype(f32) + self.yrecv[m].astype(f32)
+            if m == 0:
+                self.ks[1, 0] = part
+            else:
+                self.zs[m - 1] = part.astype(bf16)
+                self.z[m] = push(self.zs.at[m - 1], self.zrecv.at[m - 1], z_dev(m))
 
         def total(self):
-            result = self.kept
+            result = self.ks[1, 0]
             for o in range(1, Z):
-                self.z[o - 1].wait_recv()
+                self.z[o].wait_recv()
                 result = result + self.zrecv[o - 1].astype(f32)
             return result
 
-    per = len(grad_refs) // 3
-    sum1, sum2, sum_n = [WeightSum(*grad_refs[k * per : (k + 1) * per]) for k in range(3)]
+    per = len(grad_refs) // 4
+    sum1a, sum1b, sum2, sum_n = [WeightSum(*grad_refs[k * per : (k + 1) * per]) for k in range(4)]
 
     sum_n.put(0, inner(own_nodes, d_pre_n), r3)
     sum_n.put(D, inner(agg_low, d_pre_n), r3)
@@ -587,12 +688,13 @@
     gsm[5:6, :] = jnp.sum(d_out_n.astype(f32), axis=0, keepdims=True)
     gsm[6:7, :] = jnp.sum(ncot * normed_n, axis=0, keepdims=True)
     gsm[7:8, :] = jnp.sum(ncot, axis=0, keepdims=True)
-    for o in range(1, Z):
-        d_z[o - 1].wait_recv()
-        s = dbuf.at[z_at(Z - o), y]
-        d_y.append(push(s, s, y_dev))
-    sum_n.cross_x()
-    cot_copy.wait()
+    for h in range(2):
+        for m in range(1, Z):
+            d_z[m, h].wait_recv()
+            d_y.append(send(d_part(m, h), y_dev))
+    for k in range(4):
+        sum_n.cross_x(k)
+    loads[10].wait()
     for copy in d_y:
         copy.wait_recv()
 
@@ -617,94 +719,145 @@
         dpre[at, :] = d_pre
         sums[0] += fold_rows(d_pre.astype(f32))
 
-    half = rows // R // 2
     pl.loop(0, half)(edge_back)
-    sum_n.cross_y()
+    for m in order:
+        sum_n.cross_y(m)
     pl.loop(half, rows // R)(edge_back)
-    sum2.put(0, inner(hidden[...], dout[...]))
-    sum2.start()
-    for k in range(4):
-        gsm[k : k + 1, :] = jnp.sum(sums[k], axis=0, keepdims=True)
-    gm_src[0] = gsm[...]
-    gm_c = push(gm_src.at[0], gm_rcv.at[0], c_dev)
-    sum_n.cross_z()
-    d_pre = dpre[...]
-    sum1.put(0, inner(edges[...], d_pre))
-    sum2.cross_x()
-    small_sum(gm_src, gm_rcv, 0, [(gm_c, 0)])
-    gm_x = push(gm_src.at[1], gm_rcv.at[1], x_dev)
-    seg[0:N, :] = mm(spread[0:N, :], d_pre).astype(bf16)
-    seg[N : 2 * N, :] = mm(spread[N : 2 * N, :], d_pre).astype(bf16)
-    sum1.put(D, inner(nodes_all, seg[0:N, :]))
-    sum1.put(2 * D, inner(nodes_all, seg[N : 2 * N, :]))
-    sum1.start()
-    node_sum = NodeSum(
-        times_t(seg[0:N, :], w1[D : 2 * D, :]) + times_t(seg[N : 2 * N, :], w1[2 * D : 3 * D, :]),
-        pb_n,
-        yr_n,
-        zs_n,
-        zr_n,
-    )
-    sum1.cross_x()
-    small_sum(gm_src, gm_rcv, 1, [(gm_x, 1)])
-    gm_y = push(gm_src.at[2], gm_rcv.at[2], y_dev)
-    sum2.cross_y()
-    node_sum.turn()
-    sum2.cross_z()
-    small_sum(gm_src, gm_rcv, 2, [(gm_y, 2)])
-    gm_z = [push(gm_src.at[3], gm_rcv.at[2 + o], z_dev(o)) for o in range(1, Z)]
-
-    @pl.loop(0, rows // R)
-    def _(i):
-        at = pl.ds(pl.multiple_of(i * R, R), R)
-        egrad[at, :] = (dedge[at, :] + times_t(dpre[at, :], w1[0:D, :])).astype(bf16)
-
-    egrad_copy = pltpu.make_async_copy(egrad, egrad_out, local_sem.at[3])
-    egrad_copy.start()
-    sum1.cross_y()
-    ngrad_out[...] = (node_part + node_sum.total()).astype(bf16)
-    total_n = sum_n.total()
-    g3_out[...] = total_n[0:r3]
-    g4_out[...] = total_n[r3 : r3 + r4]
-    g2_out[...] = sum2.total()
-    small_sum(gm_src, gm_rcv, 3, [(copy, 3 + k) for k, copy in enumerate(gm_z)])
-    take = (
-        lax.broadcasted_iota(jnp.int32, (D, ws), 0)
-        == lax.broadcasted_iota(jnp.int32, (D, ws), 1) + me * ws
-    )
-    gs_out[...] = jnp.dot(
-        gm_src[4],
-        jnp.where(take, 1.0, 0.0),
-        preferred_element_type=f32,
-        precision=lax.Precision.HIGHEST,
-    )
-    sum1.cross_z()
-    g1_out[...] = sum1.total()
+    edges_all = edges[...]
+
+    def edge_grads(k, into):
+        at = slice(k * (D // 2), (k + 1) * (D // 2))
+        d_pre = dpre[:, at]
+        into.put(0, inner(edges_all, d_pre))
+        for half in range(2):
+            nodes_at = slice(half * N, (half + 1) * N)
+            seg[nodes_at, at] = mm(spread[nodes_at, :], d_pre).astype(bf16)
+            into.put((1 + half) * D, inner(nodes_all, seg[nodes_at, at]))
+        into.start()
+
+    sums_w = {"a": sum1a, "b": sum1b, "c": sum2, "n": sum_n}
+    gm = []
+    later = {}
+
+    def step_w(which, _):
+        if which == "c":
+            sum2.put(0, inner(hidden[...], dout[...]))
+            sum2.start()
+        else:
+            edge_grads("ab".index(which), sums_w[which])
+
+    def step_t(which, _):
+        if which == "N":
+            ngrad_out[...] = (node_part + later["N"].total()).astype(bf16)
+            return
+        result = sums_w[which].total()
+        if which == "n":
+            g3_out[...] = result[0:r3]
+            g4_out[...] = result[r3 : r3 + r4]
+        elif which == "c":
+            g2_out[...] = result
+        else:
+            k = "ab".index(which)
+            g1_out[:, k * (D // 2) : (k + 1) * (D // 2)] = result
+
+    def step_n(which, k):
+        if which == "s":
+            later["N"] = NodeSum(
+                times_t(seg[0:N, :], w1[D : 2 * D, :])
+                + times_t(seg[N : 2 * N, :], w1[2 * D : 3 * D, :]),
+                pb_n,
+                yr_n,
+                zs_n,
+                zr_n,
+            )
+        else:
+            later["N"].turn(k, "gh".index(which))
+
+    def step_e(*_):
+        @pl.loop(0, rows // R)
+        def _(i):
+            at = pl.ds(pl.multiple_of(i * R, R), R)
+            egrad[at, :] = (dedge[at, :] + times_t(dpre[at, :], w1[0:D, :])).astype(bf16)
+
+    def step_g(_, k):
+        if k == 0:
+            for row in range(4):
+                gsm[row : row + 1, :] = jnp.sum(sums[row], axis=0, keepdims=True)
+            for zz in range(Z):
+                gm_tile[zz] = gsm[:, zz * wide : (zz + 1) * wide]
+            gm.extend(
+                push(gm_tile.at[zx(m)], gm_tile.at[Z + m - 1], z_dev(m)) for m in range(1, Z)
+            )
+        elif k == 1:
+            tile = gm_tile[z]
+            for m in range(1, Z):
+                gm[m - 1].wait_recv()
+                tile = tile + gm_tile[Z + m - 1]
+            gm_src[0] = tile
+            gm.append(push(gm_src.at[0], gm_rcv.at[0], y_dev))
+        else:
+            small_sum(gm_src, gm_rcv, k - 2, gm[-1])
+            if k < 4:
+                gm.append(push(gm_src.at[k - 1], gm_rcv.at[k - 1], (x_dev, c_dev)[k - 2]))
+                return
+            take = (
+                lax.broadcasted_iota(jnp.int32, (wide, ws), 0)
+                == lax.broadcasted_iota(jnp.int32, (wide, ws), 1) + first
+            )
+            gs_out[...] = jnp.dot(
+                gm_src[3],
+                jnp.where(take, 1.0, 0.0),
+                preferred_element_type=f32,
+                precision=lax.Precision.HIGHEST,
+            )
+
+    tail = {
+        "w": step_w,
+        "x": lambda which, k: sums_w[which].cross_x(k),
+        "y": lambda which, m: sums_w[which].cross_y(m),
+        "z": lambda which, m: sums_w[which].cross_z(m),
+        "t": step_t,
+        "n": step_n,
+        "e": step_e,
+        "g": step_g,
+    }
+    for step in geo["tail"]:
+        kind, which, k = step[0], step[1:2], int(step[2:] or 0)
+        if kind not in "yzn" or k < Z:
+            tail[kind](which, k)
     for copy in started:
         copy.wait_send()
-    enew_copy.wait()
-    egrad_copy.wait()
 
 
 def update_kernel(*refs):
-    (
-        enew,
-        egrad,
-        nnew,
-        ngrad,
-        *rest,
-    ) = refs[:24]
-    outs = refs[24:]
+    passed, weights, firsts, seconds = refs[0:9], refs[9:14], refs[14:19], refs[19:24]
+    outs, new_v, new_w, smalls, sem = refs[24:43], refs[43:47], refs[47:51], refs[51:54], refs[54]
+    enew, egrad, nnew, ngrad, *grads = passed
+    copies = []
+
+    def put(src, dst):
+        copies.append(pltpu.make_async_copy(src, dst, sem.at[len(copies)]))
+        copies[-1].start()
+
+    for src, dst in zip((weights[4], firsts[4], seconds[4]), smalls):
+        put(src, dst)
     for src, dst in zip((enew, nnew, egrad, ngrad), outs[:4]):
-        dst[0] = src[...]
-    grads, weights, firsts, seconds = rest[0:5], rest[5:10], rest[10:15], rest[15:20]
-    rates = (0.03, 0.03, 0.03, 0.03, 0.2)
-    for k in range(5):
-        grad = grads[k][...]
-        new_w, new_v = adamw(weights[k][...], grad, firsts[k][...], seconds[k][...], rates[k])
-        outs[4 + k][...] = grad
-        outs[9 + k][...] = new_v
-        outs[14 + k][...] = new_w
+        put(src, dst.at[0])
+    for k in range(4):
+        put(grads[k], outs[4 + k])
+    outs[8][...] = grads[4][...]
+    for k in range(4):
+        new_w[k][...], new_v[k][...] = adamw(
+            weights[k][...], grads[k][...], firsts[k][...], seconds[k][...], 0.03
+        )
+        put(new_v[k], outs[9 + k])
+        put(new_w[k], outs[14 + k])
+    for copy in copies[:3]:
+        copy.wait()
+    small, first, second = (ref[...] for ref in smalls)
+    outs[18][...], outs[13][...] = adamw(small, grads[4][...], first, second, 0.2)
+    for copy in copies[3:]:
+        copy.wait()
 
 
 def on_device(n_edge, n_grp, *args):
@@ -728,22 +881,26 @@
         n_edge % 2 == 0
         and n_grp == 4
         and all(r % 16 == 0 for r in shards)
-        and D % 128 == 0
+        and n_edge // 2 in (2, 4)
+        and D % (128 * (n_edge // 2)) == 0
+        and D % 256 == 0
         and N % 128 == 0
+        and n % 32 == 0
+        and (shards[0] + shards[1]) % 32 == 0
         and rows % 256 == 0
         and rows * N <= 1024 * 1024
     )
     if not fits:
         return native(*args)
     Z, Y, X, C = n_edge // 2, 2, 2, 2
-    n_sem = 200
+    n_sem = 240
 
     def vm(shape, dtype=bf16):
         return pltpu.VMEM(shape, dtype)
 
+    ins = [edge_lat[0], edge_cot[0], node_lat[0], node_cot[0], senders, receivers, edge_count, *weights]
     scratch = [
-        vm((rows, D)),
-        vm((rows, D)),
+        *[vm(a.shape, a.dtype) for a in ins if a is not edge_count],
         vm((Z, Y, n, D)),
         vm((Z, Y, n, D)),
         *[vm((r * n_dev, D)) for r in shards],
@@ -757,72 +914,61 @@
         vm((rows, D), f32),
         vm((rows, 128), f32),
         vm((rows, D)),
-        vm((rows, D)),
         vm((rows, D), f32),
         vm((rows, D)),
         vm((rows, D)),
-        vm((rows, D)),
         vm((4, 8, D), f32),
-        vm((Z, Y, n, D), f32),
-        vm((Z, Y, n, D)),
-        vm((Z, Y, n, D)),
-        vm((Z, n, D)),
-        vm((Z, n, D)),
-        vm((Z - 1, n, D)),
-        vm((Z - 1, n, D)),
-        vm((Z - 1, n, D)),
-        vm((Z - 1, n, D)),
+        vm((Z, Y, 2, n // 2, D), f32),
+        vm((Z, Y, 2, n // 2, D)),
+        vm((Z, Y, 2, n // 2, D)),
+        vm((Z, 2, n // 2, D)),
+        vm((Z, 2, n // 2, D)),
+        *[vm((Z - 1, 2, n // 2, D))] * 4,
         vm((2 * N, D)),
-        vm((5, 8, D), f32),
-        vm((Z + 2, 8, D), f32),
-        vm((5, 8, D), f32),
-        vm((Z + 2, 8, D), f32),
+        vm((4, 8, D // Z), f32),
+        vm((3, 8, D // Z), f32),
+        vm((Z, 8, D // Z), f32),
+        vm((8, D), f32),
+        vm((4, 8, D // Z), f32),
+        vm((3, 8, D // Z), f32),
+        vm((2 * Z - 1, 8, D // Z), f32),
         vm((8, D), f32),
     ]
-    for r in (shards[0], shards[1], shards[2] + shards[3]):
+    blocks = ((shards[0], D // 2), (shards[0], D // 2), (shards[1], D), (shards[2] + shards[3], D))
+    for r, cols in blocks:
         scratch += [
-            vm((Z, Y, X, C, r, D)),
-            vm((4, Z, r, D)),
-            vm((2, Z, r, D)),
-            vm((2, Z, r, D)),
-            vm((2, Z, r, D), f32),
-            vm((Z, r, D)),
-            vm((Z, r, D)),
-            vm((Z - 1, r, D)),
-            vm((Z - 1, r, D)),
+            vm((Z, Y, X, C, r, cols)),
+            vm((4, Z, r, cols)),
+            vm((2, Z, r, cols)),
+            vm((2, Z, r, cols)),
+            vm((2, Z, r, cols), f32),
+            vm((Z, r, cols)),
+            vm((Z, r, cols)),
+            vm((Z - 1, r, cols)),
+            vm((Z - 1, r, cols)),
         ]
     scratch += [
-        pltpu.SemaphoreType.DMA((4,)),
+        pltpu.SemaphoreType.DMA((len(ins),)),
         pltpu.SemaphoreType.DMA((n_sem,)),
         pltpu.SemaphoreType.DMA((n_sem,)),
     ]
-    sds = jax.ShapeDtypeStruct
+    hbm = pl.BlockSpec(memory_space=pltpu.HBM)
     anyspace = pl.BlockSpec(memory_space=pl.ANY)
     vmem = pl.BlockSpec(memory_space=pltpu.VMEM)
-    smem = pl.BlockSpec(memory_space=pltpu.SMEM)
-    big = [sds((rows, D), bf16)] * 2 + [sds((n, D), bf16)] * 2
-    grads = [sds(w.shape, f32) for w in weights]
     results = pl.pallas_call(
-        functools.partial(layer_kernel, {"dims": (Z, Y, X, C), "n_sem": n_sem, "chunk": 256}),
-        out_shape=big + grads,
-        in_specs=[anyspace, anyspace] + [vmem] * 4 + [smem] + [vmem] * 5,
-        out_specs=[anyspace, anyspace] + [vmem] * 7,
+        functools.partial(layer_kernel, dict(GEO, dims=(Z, Y, X, C), n_sem=n_sem)),
+        out_shape=[vm((rows, D))] * 2 + [vm((n, D))] * 2 + [vm(w.shape, f32) for w in weights],
+        in_specs=[hbm] * 6 + [pl.BlockSpec(memory_space=pltpu.SMEM)] + [hbm] * 5,
+        out_specs=[vmem] * 9,
         scratch_shapes=scratch,
         compiler_params=pltpu.CompilerParams(
-            collective_id=0, has_side_effects=True, vmem_limit_bytes=56 * 1024 * 1024
+            collective_id=0, has_side_effects=True, vmem_limit_bytes=52 * 1024 * 1024
         ),
         name="layer",
-    )(
-        edge_lat[0],
-        edge_cot[0],
-        node_lat[0],
-        node_cot[0],
-        senders,
-        receivers,
-        edge_count,
-        *weights,
-    )
+    )(*ins)
+    sds = jax.ShapeDtypeStruct
     state_out = [sds(w.shape, f32) for w in weights]
+    kept = [vm(w.shape, f32) for w in weights[:4]]
     return tuple(
         pl.pallas_call(
             update_kernel,
@@ -835,9 +981,15 @@
                 *state_out,
                 *state_out,
             ],
-            in_specs=[vmem] * 24,
-            out_specs=[vmem] * 19,
-            compiler_params=pltpu.CompilerParams(vmem_limit_bytes=60 * 1024 * 1024),
+            in_specs=[vmem] * 9 + ([vmem] * 4 + [hbm]) * 3,
+            out_specs=[anyspace] * 4 + ([anyspace] * 4 + [vmem]) * 3,
+            scratch_shapes=[
+                *kept,
+                *kept,
+                *[vm(weights[4].shape, f32)] * 3,
+                pltpu.SemaphoreType.DMA((19,)),
+            ],
+            compiler_params=pltpu.CompilerParams(vmem_limit_bytes=8 * 1024 * 1024),
             name="update",
         )(*results, *weights, *firsts, *seconds)
     )

time: 97.2 us -> 87.8 us (0.903)
  Pallas kernels: 95.7 us -> 85.5 us
    pallas_call x1, Pallas kernels: 92.1 us -> 83.1 us  [on_device(): pl.pallas_call(functools.partial(layer_kernel, dict(GEO, dims=(Z, Y, X, C...]
    pallas_call x1, Pallas kernels: 3.61 us -> 2.33 us  [on_device(): pl.pallas_call(update_kernel, out_shape=[sds((1, rows, D), bf16), sds((1,...]
where the time goes in v3:
time: 87.8 us; the launch traced here: 87.6 us
  Pallas kernels  85.5 us (97%)
  between operations  1.53 us (2%)
    pallas_call x1, Pallas kernels, on_device(): pl.pallas_call(functools.partial(layer_kernel, dict(GEO, dims=(Z, Y, X, C...  83.1 us
    pallas_call x1, Pallas kernels, on_device(): pl.pallas_call(update_kernel, out_shape=[sds((1, rows, D), bf16), sds((1,...  2.33 us

profile of v3, /device:TPU:0, one launch (start us, length us, event | category | flops | bytes accessed | tf_op | source)
XLA Modules:
  0.0 87.6 jit_solution(13892431538910636347)
XLA Ops:
  1.3 0.0 copy-start
  1.3 0.0 copy-start.1
  1.3 0.0 copy-start.2
  1.3 0.0 copy-start.3
  1.4 83.1 %layer.1 = (bf16[1024,512]{1,0:T(8,128)(2,1)S(1)}, bf16[1024,512]{1,0:T(8,128)(2,1)S(1)}, bf16[64,512]{1,0:T(8,128)(2,1)S(1)}, bf16[64,512]{1,0:T(8,128)(2,1)S(1...) custom-call(bf16[1024,512]{1,0:T(8,128)(2,1)} %bitcast.4, ...), custom_call_target="tpu_custom_call" | custom-call | tf_op jit(solution)/shard_map/layer/pallas_call | solution.py:958
  84.6 0.0 copy-start.14
  84.6 0.0 copy-start.13
  84.6 0.0 copy-start.12
  84.6 0.0 copy-done
  84.6 0.0 copy-done.1
  84.6 0.0 copy-done.2
  84.6 0.0 copy-done.3
  84.6 0.0 copy-done.4
  84.7 0.0 copy-done.5
  84.7 0.0 copy-done.6
  84.7 0.0 copy-done.7
  84.7 0.0 copy-done.8
  84.7 0.0 copy-done.9
  84.7 0.0 copy-done.10
  84.7 0.0 copy-done.11
  84.7 0.5 copy-done.14
  85.3 0.0 copy-done.13
  85.3 0.0 copy-done.12
  85.3 2.3 %update.1 = (bf16[1,1024,512]{2,1,0:T(8,128)(2,1)}, bf16[1,64,512]{2,1,0:T(8,128)(2,1)}, bf16[1,1024,512]{2,1,0:T(8,128)(2,1)}, bf16[1,64,512]{2,1,0:T(8,128)(2,...) custom-call(bf16[1024,512]{1,0:T(8,128)(2,1)S(1)} %get-tuple-element, ...), custom_call_target="tpu_custom_call" | custom-call | tf_op jit(solution)/shard_map/update/pallas_call | solution.py:973
  (8 shorter events, 0.0 us)
Async XLA Ops:
  1.3 83.3 %copy-start = (f32[48,512]{1,0:T(8,128)S(1)}, f32[48,512]{1,0:T(8,128)}, u32[]{:S(2)}) copy-start(f32[48,512]{1,0:T(8,128)} %refs_9_.3) | copy-start | bytes 294916
  1.3 83.3 %copy-start.1 = (f32[32,512]{1,0:T(8,128)S(1)}, f32[32,512]{1,0:T(8,128)}, u32[]{:S(2)}) copy-start(f32[32,512]{1,0:T(8,128)} %refs_11_.3) | copy-start | bytes 196612
  1.3 83.3 %copy-start.2 = (f32[16,512]{1,0:T(8,128)S(1)}, f32[16,512]{1,0:T(8,128)}, u32[]{:S(2)}) copy-start(f32[16,512]{1,0:T(8,128)} %refs_10_.3) | copy-start | bytes 98308
  1.3 83.3 %copy-start.3 = (f32[16,512]{1,0:T(8,128)S(1)}, f32[16,512]{1,0:T(8,128)}, u32[]{:S(2)}) copy-start(f32[16,512]{1,0:T(8,128)} %refs_12_.1) | copy-start | bytes 98308
  1.3 83.3 %copy-start.4 = (f32[48,512]{1,0:T(8,128)S(1)}, f32[48,512]{1,0:T(8,128)}, u32[]{:S(2)}) copy-start(f32[48,512]{1,0:T(8,128)} %refs_14_.1) | copy-start | bytes 294916
  1.4 83.3 %copy-start.5 = (f32[48,512]{1,0:T(8,128)S(1)}, f32[48,512]{1,0:T(8,128)}, u32[]{:S(2)}) copy-start(f32[48,512]{1,0:T(8,128)} %refs_19_.1) | copy-start | bytes 294916
  1.4 83.3 %copy-start.6 = (f32[32,512]{1,0:T(8,128)S(1)}, f32[32,512]{1,0:T(8,128)}, u32[]{:S(2)}) copy-start(f32[32,512]{1,0:T(8,128)} %refs_16_.1) | copy-start | bytes 196612
  1.4 83.3 %copy-start.7 = (f32[32,512]{1,0:T(8,128)S(1)}, f32[32,512]{1,0:T(8,128)}, u32[]{:S(2)}) copy-start(f32[32,512]{1,0:T(8,128)} %refs_21_.1) | copy-start | bytes 196612
  1.4 83.3 %copy-start.8 = (f32[16,512]{1,0:T(8,128)S(1)}, f32[16,512]{1,0:T(8,128)}, u32[]{:S(2)}) copy-start(f32[16,512]{1,0:T(8,128)} %refs_15_.1) | copy-start | bytes 98308
  1.4 83.3 %copy-start.9 = (f32[16,512]{1,0:T(8,128)S(1)}, f32[16,512]{1,0:T(8,128)}, u32[]{:S(2)}) copy-start(f32[16,512]{1,0:T(8,128)} %refs_17_.1) | copy-start | bytes 98308
  1.4 83.3 %copy-start.10 = (f32[16,512]{1,0:T(8,128)S(1)}, f32[16,512]{1,0:T(8,128)}, u32[]{:S(2)}) copy-start(f32[16,512]{1,0:T(8,128)} %refs_20_.1) | copy-start | bytes 98308
  1.4 83.3 %copy-start.11 = (f32[16,512]{1,0:T(8,128)S(1)}, f32[16,512]{1,0:T(8,128)}, u32[]{:S(2)}) copy-start(f32[16,512]{1,0:T(8,128)} %refs_22_.1) | copy-start | bytes 98308
  84.6 0.7 copy-start.14
  84.6 0.7 copy-start.13
  84.6 0.7 copy-start.12

commit v4 on v3

--- a/solution.py
+++ b/solution.py
@@ -195,7 +195,6 @@
 
 
 GEO = {
-    "chunk": 256,
     "gather": (
         "n0", "y0.0", "y0.1", "z1.0", "z2.0", "z1.1", "z2.1", "y1.0", "y2.0", "s0", "z3.0", "s1",
         "y2.1", "z3.1", "y1.1", "n1", "n2", "b0", "y3.0", "n3", "s2", "y3.1"
@@ -206,12 +205,20 @@
     "mid": (
         "b3", "l3"
     ),
+    "agg": (
+        "p3", "p2", "p1", "p0", "b0", "t3.0", "t3.1", "t2.0", "g2.0", "t2.1", "b1", "t1.0", "g2.1",
+        "t1.1", "t0.0", "b2", "t0.1", "b3", "g0.0", "g0.1"
+    ),
+    "back": (
+        "x0", "x1", "d1.0", "d2.0", "d1.1", "d2.1", "d3.0", "d3.1", "x2", "x3"
+    ),
     "tail": (
-        "wa", "zn3", "wb", "xa0", "zn2", "ns", "xb0", "g_0", "xb1", "zn1", "xb3", "wc", "ng3",
-        "xa2", "xa1", "ng2", "ya3", "nh2", "nh3", "xa3", "ng1", "ya2", "xb2", "g_1", "ya1", "nh1",
-        "xc0", "ng0", "yb3", "xc1", "za3", "ya0", "zn0", "yb1", "za2", "yb2", "xc3", "g_2", "za1",
-        "yb0", "xc2", "yc3", "zb3", "e", "yc1", "zb1", "yc2", "zb2", "zb0", "za0", "nh0", "tn",
-        "g_3", "zc3", "zc1", "g_4", "zc2", "yc0", "zc0", "tb", "ta", "tN", "tc"
+        "wa", "wb", "xa0", "zn2", "ns", "xa2", "wc", "xb0", "xb2", "zn1", "xc0", "zn3", "g_0",
+        "xa3", "xa1", "ya3", "ng3", "xb1", "ng2", "zn0", "ya1", "ya2", "nh3", "mn2", "yb3", "ng1",
+        "mn0", "yb0", "nh2", "ng0", "nh1", "xc3", "g_1", "yb1", "xc1", "xc2", "za3", "e", "no2",
+        "nm0", "za2", "yc3", "za1", "yb2", "ya0", "xb3", "yc2", "zb3", "ma2", "zb1", "nh0", "yc1",
+        "g_2", "zc3", "tn", "nm2", "zb2", "zc2", "za0", "mb2", "mc2", "ma0", "g_3", "yc0", "zc1",
+        "zb0", "mb0", "no0", "g_4", "zc0", "tb", "tN", "ta", "mc0", "tc"
     ),
 }
 
@@ -297,7 +304,7 @@
     rows, D = edges.shape
     n = nodes_in.shape[0]
     N = Z * Y * n
-    R = geo["chunk"]
+    R = rows // 2
 
     e_id = lax.axis_index("edge")
     g_id = lax.axis_index("grp")
@@ -518,7 +525,7 @@
     row_id = lax.broadcasted_iota(jnp.int32, (R, D), 0)
 
     def edge_forward(i):
-        at = pl.ds(pl.multiple_of(i * R, R), R)
+        at = slice(i * R, (i + 1) * R)
         live = row_id < count - i * R
         own = edges[at, :]
         pre = mm(own, w1[0:D, :]) + mm(pick[at, :], proj[...]) + par_all[0:1, :]
@@ -534,72 +541,92 @@
         enew[at, :] = new.astype(bf16)
         term[at, :] = jnp.where(live, new, 0.0).astype(bf16)
 
-    half = rows // R // 2
-    pl.loop(0, half)(edge_forward)
+    edge_forward(0)
     for step in geo["mid"]:
         kind, m = step[0], int(step[1:])
         if m < Z:
             steps[kind](m, 0)
-    pl.loop(half, rows // R)(edge_forward)
+    edge_forward(1)
 
     order = tuple(reversed(range(Z)))
 
     class NodeSum:
-        def __init__(self, total, pb, yr, zs, zr):
-            self.yr, self.zs, self.zr = yr, zs, zr
-            pf[...] = total.reshape(Z, Y, 2, n // 2, D)
-            pb[...] = total.astype(bf16).reshape(Z, Y, 2, n // 2, D)
-            self.y = {
-                (m, h): push(pb.at[zx(m), yp, h], yr.at[m, h], y_dev) for m in order for h in range(2)
-            }
-
-            self.z = {}
+        def __init__(self, pb, yr, zs, zr):
+            self.pb, self.yr, self.zs, self.zr = pb, yr, zs, zr
+            self.y, self.z = {}, {}
+
+        def put(self, m, values):
+            pf[zx(m)] = values.reshape(Y, 2, n // 2, D)
+            self.pb[zx(m)] = values.astype(bf16).reshape(Y, 2, n // 2, D)
+            for h in range(2):
+                self.y[m, h] = push(self.pb.at[zx(m), yp, h], self.yr.at[m, h], y_dev)
+
+        def over(self, m, h, low):
+            self.zs[m - 1, h] = pf[zx(m), y, h].astype(bf16)
+            self.z[m, h] = push(self.zs.at[m - 1, h], self.zr.at[m - 1, h], z_dev(low))
 
         def turn(self, m, h):
             self.y[m, h].wait_recv()
-            part = pf[zx(m), y, h] + self.yr[m, h].astype(f32)
-            if m == 0:
-                pf[z, y, h] = part
-            else:
-                self.zs[m - 1, h] = part.astype(bf16)
-                self.z[m, h] = push(self.zs.at[m - 1, h], self.zr.at[m - 1, h], z_dev(m))
+            pf[zx(m), y, h] = pf[zx(m), y, h] + self.yr[m, h].astype(f32)
+            if m % 2:
+                self.over(m, h, 1)
+
+        def merge(self, m, h):
+            self.z[m + 1, h].wait_recv()
+            pf[zx(m), y, h] = pf[zx(m), y, h] + self.zr[m, h].astype(f32)
+            if m:
+                self.over(m, h, 2)
 
         def total(self):
             sums = []
             for h in range(2):
                 part = pf[z, y, h]
-                for m in range(1, Z):
+                for m in range(2, Z, 2):
                     self.z[m, h].wait_recv()
                     part = part + self.zr[m - 1, h].astype(f32)
                 sums.append(part)
             return jnp.concatenate(sums, axis=0)
 
-    agg_sum = NodeSum(mm(spread[N : 2 * N, :], term[...]), pb_a, yr_a, zs_a, zr_a)
-    for copy in b_y:
-        copy.wait_recv()
-    b_x.append(send(wb.at[:, yp, x, c], x_dev))
-    b_c = [send(wb.at[:, yy, x, c], c_dev) for yy in (y, yp)]
-    for m in order:
-        for h in range(2):
-            agg_sum.turn(m, h)
-    for copy in b_x[:-1]:
-        copy.wait_recv()
-    b_c.append(send(wb.at[:, y, xp, c], c_dev))
-    b_x[-1].wait_recv()
-    b_c.append(send(wb.at[:, yp, xp, c], c_dev))
-    for copy in b_c:
-        copy.wait_recv()
-    w3[...] = wb[:, :, :, :, 0:r3, :].reshape(w3.shape)
-    w4[...] = wb[:, :, :, :, r3 : r3 + r4, :].reshape(w4.shape)
+    agg_sum = NodeSum(pb_a, yr_a, zs_a, zr_a)
+    b_c, early = [], {}
+
+    def step_p(m, _):
+        first_row = pl.multiple_of(N + zx(m) * (Y * n), Y * n)
+        agg_sum.put(m, mm(spread[pl.ds(first_row, Y * n), :], term[...]))
+
+    def step_b(k, _):
+        if k == 0:
+            for copy in b_y:
+                copy.wait_recv()
+            b_x.append(send(wb.at[:, yp, x, c], x_dev))
+            b_c.extend(send(wb.at[:, yy, x, c], c_dev) for yy in (y, yp))
+        elif k == 1:
+            for copy in b_x[:-1]:
+                copy.wait_recv()
+            b_c.append(send(wb.at[:, y, xp, c], c_dev))
+        elif k == 2:
+            b_x[-1].wait_recv()
+            b_c.append(send(wb.at[:, yp, xp, c], c_dev))
+        else:
+            for copy in b_c:
+                copy.wait_recv()
+            w3[...] = wb[:, :, :, :, 0:r3, :].reshape(w3.shape)
+            w4[...] = wb[:, :, :, :, r3 : r3 + r4, :].reshape(w4.shape)
+            early["pre"] = mm(nodes_in[...], w3[0:D, :])
+
+    sums_n = {"p": step_p, "b": step_b, "t": agg_sum.turn, "g": agg_sum.merge}
+    for step in geo["agg"]:
+        kind, (m, h) = step[0], ([int(v) for v in step[1:].split(".")] + [0])[:2]
+        if kind == "b" or m < Z:
+            sums_n[kind](m, h)
     own_nodes = nodes_in[...]
-    pre_own = mm(own_nodes, w3[0:D, :])
     agg = agg_sum.total()
 
     def par(k):
         return par_all[k : k + 1, :]
 
     agg_low = agg.astype(bf16)
-    pre_n = pre_own + mm(agg_low, w3[D : 2 * D, :]) + par(4)
+    pre_n = early["pre"] + mm(agg_low, w3[D : 2 * D, :]) + par(4)
     sig_n = jax.nn.sigmoid(pre_n)
     hidden_n = (pre_n * sig_n).astype(bf16)
     out_n = mm(hidden_n, w4[...]) + par(5)
@@ -614,11 +641,16 @@
     def d_part(m, h):
         return dbuf.at[zx(m), y, h * (n // 2) : (h + 1) * (n // 2), :]
 
+    def step_d(m, h):
+        block = d_part(m, h)
+        if m == 0:
+            d_z[h] = along_z(block)
+        else:
+            arrive_z(d_z[h], m, block)
+        d_y.append(send(block, y_dev))
+
     for h in range(2):
-        for m in order[:-1]:
-            d_z[m, h] = send(d_part(0, h), z_dev(m))
-        d_y.append(send(d_part(0, h), y_dev))
-
+        step_d(0, h)
     class WeightSum:
         def __init__(self, grad, crecv, xs, xrecv, ks, ys, yrecv, zs, zrecv):
             self.grad, self.crecv, self.xs, self.xrecv, self.ks = grad, crecv, xs, xrecv, ks
@@ -662,17 +694,28 @@
             self.x[1, m].wait_recv()
             self.y[m].wait_recv()
             part = self.ks[1, m] + self.xrecv[1, m].astype(f32) + self.yrecv[m].astype(f32)
-            if m == 0:
+            if m % 2:
+                self.over(part, m, 1)
+            else:
+                self.ks[1, m] = part
+
+        def over(self, part, m, low):
+            self.zs[m - 1] = part.astype(bf16)
+            self.z[m] = push(self.zs.at[m - 1], self.zrecv.at[m - 1], z_dev(low))
+
+        def merge(self, m):
+            self.z[m + 1].wait_recv()
+            part = self.ks[1, m] + self.zrecv[m].astype(f32)
+            if m:
+                self.over(part, m, 2)
+            else:
                 self.ks[1, 0] = part
-            else:
-                self.zs[m - 1] = part.astype(bf16)
-                self.z[m] = push(self.zs.at[m - 1], self.zrecv.at[m - 1], z_dev(m))
 
         def total(self):
             result = self.ks[1, 0]
-            for o in range(1, Z):
-                self.z[o].wait_recv()
-                result = result + self.zrecv[o - 1].astype(f32)
+            for m in range(2, Z, 2):
+                self.z[m].wait_recv()
+                result = result + self.zrecv[m - 1].astype(f32)
             return result
 
     per = len(grad_refs) // 4
@@ -688,12 +731,11 @@
     gsm[5:6, :] = jnp.sum(d_out_n.astype(f32), axis=0, keepdims=True)
     gsm[6:7, :] = jnp.sum(ncot * normed_n, axis=0, keepdims=True)
     gsm[7:8, :] = jnp.sum(ncot, axis=0, keepdims=True)
-    for h in range(2):
-        for m in range(1, Z):
-            d_z[m, h].wait_recv()
-            d_y.append(send(d_part(m, h), y_dev))
-    for k in range(4):
-        sum_n.cross_x(k)
+    parts_d = {"d": step_d, "x": lambda k, _: sum_n.cross_x(k)}
+    for step in geo["back"]:
+        kind, (m, h) = step[0], ([int(v) for v in step[1:].split(".")] + [0])[:2]
+        if kind == "x" or m < Z:
+            parts_d[kind](m, h)
     loads[10].wait()
     for copy in d_y:
         copy.wait_recv()
@@ -702,7 +744,7 @@
     d_all = dbuf[...].reshape(N, D)
 
     def edge_back(i):
-        at = pl.ds(pl.multiple_of(i * R, R), R)
+        at = slice(i * R, (i + 1) * R)
         live = row_id < count - i * R
         d_edge = cot[at, :].astype(f32) + jnp.where(live, mm(pick[at, N : 2 * N], d_all), 0.0)
         dedge[at, :] = d_edge
@@ -719,10 +761,10 @@
         dpre[at, :] = d_pre
         sums[0] += fold_rows(d_pre.astype(f32))
 
-    pl.loop(0, half)(edge_back)
+    edge_back(0)
     for m in order:
         sum_n.cross_y(m)
-    pl.loop(half, rows // R)(edge_back)
+    edge_back(1)
     edges_all = edges[...]
 
     def edge_grads(k, into):
@@ -737,7 +779,7 @@
 
     sums_w = {"a": sum1a, "b": sum1b, "c": sum2, "n": sum_n}
     gm = []
-    later = {}
+    node_sum = NodeSum(pb_n, yr_n, zs_n, zr_n)
 
     def step_w(which, _):
         if which == "c":
@@ -748,7 +790,7 @@
 
     def step_t(which, _):
         if which == "N":
-            ngrad_out[...] = (node_part + later["N"].total()).astype(bf16)
+            ngrad_out[...] = (node_part + node_sum.total()).astype(bf16)
             return
         result = sums_w[which].total()
         if which == "n":
@@ -762,21 +804,21 @@
 
     def step_n(which, k):
         if which == "s":
-            later["N"] = NodeSum(
-                times_t(seg[0:N, :], w1[D : 2 * D, :])
-                + times_t(seg[N : 2 * N, :], w1[2 * D : 3 * D, :]),
-                pb_n,
-                yr_n,
-                zs_n,
-                zr_n,
-            )
+            total = times_t(seg[0:N, :], w1[D : 2 * D, :])
+            total = total + times_t(seg[N : 2 * N, :], w1[2 * D : 3 * D, :])
+            pf[...] = total.reshape(pf.shape)
+            pb_n[...] = total.astype(bf16).reshape(pf.shape)
+            for m in order:
+                for h in range(2):
+                    node_sum.y[m, h] = push(pb_n.at[zx(m), yp, h], yr_n.at[m, h], y_dev)
+        elif which in "gh":
+            node_sum.turn(k, "gh".index(which))
         else:
-            later["N"].turn(k, "gh".index(which))
+            node_sum.merge(k, "mo".index(which))
 
     def step_e(*_):
-        @pl.loop(0, rows // R)
-        def _(i):
-            at = pl.ds(pl.multiple_of(i * R, R), R)
+        for i in range(2):
+            at = slice(i * R, (i + 1) * R)
             egrad[at, :] = (dedge[at, :] + times_t(dpre[at, :], w1[0:D, :])).astype(bf16)
 
     def step_g(_, k):
@@ -816,6 +858,7 @@
         "x": lambda which, k: sums_w[which].cross_x(k),
         "y": lambda which, m: sums_w[which].cross_y(m),
         "z": lambda which, m: sums_w[which].cross_z(m),
+        "m": lambda which, m: sums_w[which].merge(m),
         "t": step_t,
         "n": step_n,
         "e": step_e,
@@ -823,7 +866,7 @@
     }
     for step in geo["tail"]:
         kind, which, k = step[0], step[1:2], int(step[2:] or 0)
-        if kind not in "yzn" or k < Z:
+        if kind not in "yzmn" or k < Z:
             tail[kind](which, k)
     for copy in started:
         copy.wait_send()

time: 87.8 us -> 84.5 us (0.962)
  Pallas kernels: 85.5 us -> 82.1 us
    pallas_call x1, Pallas kernels: 83.1 us -> 79.8 us  [on_device(): pl.pallas_call(functools.partial(layer_kernel, dict(GEO, dims=(Z, Y, X, C...]
where the time goes in v4:
time: 84.5 us; the launch traced here: 84.3 us
  Pallas kernels  82.1 us (97%)
  between operations  1.53 us (2%)
    pallas_call x1, Pallas kernels, on_device(): pl.pallas_call(functools.partial(layer_kernel, dict(GEO, dims=(Z, Y, X, C...  79.8 us
    pallas_call x1, Pallas kernels, on_device(): pl.pallas_call(update_kernel, out_shape=[sds((1, rows, D), bf16), sds((1,...  2.33 us

profile of v4, /device:TPU:0, one launch (start us, length us, event | category | flops | bytes accessed | tf_op | source)
XLA Modules:
  0.0 84.3 jit_solution(3949507514595582452)
XLA Ops:
  1.3 0.0 copy-start
  1.3 0.0 copy-start.1
  1.3 0.0 copy-start.2
  1.3 0.0 copy-start.3
  1.3 0.0 copy-start.4
  1.4 0.0 copy-start.5
  1.4 0.0 copy-start.6
  1.4 0.0 copy-start.7
  1.4 0.0 copy-start.8
  1.4 0.0 copy-start.9
  1.4 0.0 copy-start.10
  1.4 0.0 copy-start.11
  1.4 79.8 %layer.1 = (bf16[1024,512]{1,0:T(8,128)(2,1)S(1)}, bf16[1024,512]{1,0:T(8,128)(2,1)S(1)}, bf16[64,512]{1,0:T(8,128)(2,1)S(1)}, bf16[64,512]{1,0:T(8,128)(2,1)S(1...) custom-call(bf16[1024,512]{1,0:T(8,128)(2,1)} %bitcast.4, ...), custom_call_target="tpu_custom_call" | custom-call | tf_op jit(solution)/shard_map/layer/pallas_call | solution.py:1001
  81.2 0.0 copy-start.14
  81.2 0.0 copy-start.13
  81.2 0.0 copy-start.12
  81.2 0.0 copy-done
  81.2 0.0 copy-done.1
  81.3 0.0 copy-done.2
  81.3 0.0 copy-done.3
  81.4 0.5 copy-done.14
  81.9 0.0 copy-done.13
  81.9 0.0 copy-done.12
  81.9 2.3 %update.1 = (bf16[1,1024,512]{2,1,0:T(8,128)(2,1)}, bf16[1,64,512]{2,1,0:T(8,128)(2,1)}, bf16[1,1024,512]{2,1,0:T(8,128)(2,1)}, bf16[1,64,512]{2,1,0:T(8,128)(2,...) custom-call(bf16[1024,512]{1,0:T(8,128)(2,1)S(1)} %get-tuple-element, ...), custom_call_target="tpu_custom_call" | custom-call | tf_op jit(solution)/shard_map/update/pallas_call | solution.py:1016
  (8 shorter events, 0.0 us)
Async XLA Ops:
  1.3 79.9 %copy-start = (f32[48,512]{1,0:T(8,128)S(1)}, f32[48,512]{1,0:T(8,128)}, u32[]{:S(2)}) copy-start(f32[48,512]{1,0:T(8,128)} %refs_9_.3) | copy-start | bytes 294916
  1.3 79.9 %copy-start.1 = (f32[32,512]{1,0:T(8,128)S(1)}, f32[32,512]{1,0:T(8,128)}, u32[]{:S(2)}) copy-start(f32[32,512]{1,0:T(8,128)} %refs_11_.3) | copy-start | bytes 196612
  1.3 79.9 %copy-start.2 = (f32[16,512]{1,0:T(8,128)S(1)}, f32[16,512]{1,0:T(8,128)}, u32[]{:S(2)}) copy-start(f32[16,512]{1,0:T(8,128)} %refs_10_.3) | copy-start | bytes 98308
  1.3 79.9 %copy-start.3 = (f32[16,512]{1,0:T(8,128)S(1)}, f32[16,512]{1,0:T(8,128)}, u32[]{:S(2)}) copy-start(f32[16,512]{1,0:T(8,128)} %refs_12_.1) | copy-start | bytes 98308
  1.3 79.9 %copy-start.4 = (f32[48,512]{1,0:T(8,128)S(1)}, f32[48,512]{1,0:T(8,128)}, u32[]{:S(2)}) copy-start(f32[48,512]{1,0:T(8,128)} %refs_14_.1) | copy-start | bytes 294916
  1.4 79.9 %copy-start.5 = (f32[48,512]{1,0:T(8,128)S(1)}, f32[48,512]{1,0:T(8,128)}, u32[]{:S(2)}) copy-start(f32[48,512]{1,0:T(8,128)} %refs_19_.1) | copy-start | bytes 294916
  1.4 79.9 %copy-start.6 = (f32[32,512]{1,0:T(8,128)S(1)}, f32[32,512]{1,0:T(8,128)}, u32[]{:S(2)}) copy-start(f32[32,512]{1,0:T(8,128)} %refs_16_.1) | copy-start | bytes 196612
  1.4 79.9 %copy-start.7 = (f32[32,512]{1,0:T(8,128)S(1)}, f32[32,512]{1,0:T(8,128)}, u32[]{:S(2)}) copy-start(f32[32,512]{1,0:T(8,128)} %refs_21_.1) | copy-start | bytes 196612
  1.4 79.9 %copy-start.8 = (f32[16,512]{1,0:T(8,128)S(1)}, f32[16,512]{1,0:T(8,128)}, u32[]{:S(2)}) copy-start(f32[16,512]{1,0:T(8,128)} %refs_15_.1) | copy-start | bytes 98308
  1.4 79.9 %copy-start.9 = (f32[16,512]{1,0:T(8,128)S(1)}, f32[16,512]{1,0:T(8,128)}, u32[]{:S(2)}) copy-start(f32[16,512]{1,0:T(8,128)} %refs_17_.1) | copy-start | bytes 98308
  1.4 79.9 %copy-start.10 = (f32[16,512]{1,0:T(8,128)S(1)}, f32[16,512]{1,0:T(8,128)}, u32[]{:S(2)}) copy-start(f32[16,512]{1,0:T(8,128)} %refs_20_.1) | copy-start | bytes 98308
  1.4 79.9 %copy-start.11 = (f32[16,512]{1,0:T(8,128)S(1)}, f32[16,512]{1,0:T(8,128)}, u32[]{:S(2)}) copy-start(f32[16,512]{1,0:T(8,128)} %refs_22_.1) | copy-start | bytes 98308
  81.2 0.7 copy-start.14
  81.2 0.7 copy-start.13
  81.2 0.7 copy-start.12

commit v5 on v4

--- a/solution.py
+++ b/solution.py
@@ -195,32 +195,44 @@
 
 
 GEO = {
+    "x_first": (True, True, False, True),
+    "diagonal": (),
+    "bits_a": True,
+    "bits_n": True,
+    "bits_b": True,
+    "bits_d": True,
+    "bits_agg": True,
+    "bits_node": False,
+    "bits_w": False,
     "gather": (
-        "n0", "y0.0", "y0.1", "z1.0", "z2.0", "z1.1", "z2.1", "y1.0", "y2.0", "s0", "z3.0", "s1",
-        "y2.1", "z3.1", "y1.1", "n1", "n2", "b0", "y3.0", "n3", "s2", "y3.1"
+        200, 700, 100, 10, 101, 20, 11, 21, 120, 110, 600, 30, 111, 31, 610, 220, 121, 210, 130,
+        300, 131, 230, 620
     ),
     "late": (
-        "b1", "b2", "l0", "l1", "l2"
+        310, 320, 400, 410, 420
     ),
     "mid": (
-        "b3", "l3"
+        330, 430
     ),
     "agg": (
-        "p3", "p2", "p1", "p0", "b0", "t3.0", "t3.1", "t2.0", "g2.0", "t2.1", "b1", "t1.0", "g2.1",
-        "t1.1", "t0.0", "b2", "t0.1", "b3", "g0.0", "g0.1"
+        30, 300, 20, 10, 0, 130, 131, 121, 310, 120, 110, 220, 221, 320, 100, 111, 101, 330, 200,
+        201
     ),
     "back": (
-        "x0", "x1", "d1.0", "d2.0", "d1.1", "d2.1", "d3.0", "d3.1", "x2", "x3"
+        100, 110, 10, 20, 21, 11, 30, 120, 130, 31
     ),
     "tail": (
-        "wa", "wb", "xa0", "zn2", "ns", "xa2", "wc", "xb0", "xb2", "zn1", "xc0", "zn3", "g_0",
-        "xa3", "xa1", "ya3", "ng3", "xb1", "ng2", "zn0", "ya1", "ya2", "nh3", "mn2", "yb3", "ng1",
-        "mn0", "yb0", "nh2", "ng0", "nh1", "xc3", "g_1", "yb1", "xc1", "xc2", "za3", "e", "no2",
-        "nm0", "za2", "yc3", "za1", "yb2", "ya0", "xb3", "yc2", "zb3", "ma2", "zb1", "nh0", "yc1",
-        "g_2", "zc3", "tn", "nm2", "zb2", "zc2", "za0", "mb2", "mc2", "ma0", "g_3", "yc0", "zc1",
-        "zb0", "mb0", "no0", "g_4", "zc0", "tb", "tN", "ta", "mc0", "tc"
+        0, 8050, 10, 3032, 5060, 3033, 1000, 1012, 1010, 1002, 1001, 3030, 4032, 5073, 20, 5083,
+        2002, 1011, 1022, 5082, 1013, 1003, 3031, 2003, 5081, 1020, 2012, 8051, 2001, 5072, 3003,
+        2013, 4030, 5070, 5092, 2023, 1023, 3002, 2011, 5080, 1021, 2020, 2021, 2000, 2010, 2022,
+        5071, 3012, 3013, 5090, 4002, 3001, 3011, 5100, 7050, 3023, 8052, 3022, 4012, 3021, 5102,
+        3020, 8053, 8054, 3010, 6040, 4010, 3000, 6030, 4000, 6000, 4022, 6010, 4020, 6020
     ),
 }
+
+
+def decode(step, unit):
+    return step // (10 * unit), step // 10 % unit, step % 10
 
 
 def layer_kernel(geo, *refs):
@@ -239,15 +251,14 @@
         w3_hbm,
         w4_hbm,
         small_hbm,
-        enew,
-        egrad,
-        nnew_out,
-        ngrad_out,
-        g1_out,
-        g2_out,
-        g3_out,
-        g4_out,
-        gs_out,
+        *rest,
+    ) = refs
+    moments_hbm, rest = rest[:10], rest[10:]
+    enew, nnew_out, egrad, ngrad_out, *rest = rest
+    grads_out, seconds_out, weights_out, rest = rest[0:5], rest[5:10], rest[10:15], rest[15:]
+    g1_out, g2_out, g3_out, g4_out, gs_out = grads_out
+    moments_in, rest = rest[:10], rest[10:]
+    (
         edges,
         cot,
         nodes_in,
@@ -298,7 +309,7 @@
         gm_tile,
         gsm,
         *grad_refs,
-    ) = refs
+    ) = rest
     local_sem, ssem, rsem = grad_refs[-3:]
     grad_refs = grad_refs[:-3]
     rows, D = edges.shape
@@ -317,6 +328,7 @@
     y_dev = (z * Y + yp, g_id)
     x_dev = (e_id, xp * C + c)
     c_dev = (e_id, x * C + cp)
+    xy_dev = (z * Y + yp, xp * C + c)
 
     def zx(m):
         place = z
@@ -346,7 +358,7 @@
         return copy
 
     barrier = pltpu.get_barrier_semaphore()
-    peers = [z_dev(m) for m in range(1, Z)] + [y_dev, x_dev, c_dev]
+    peers = [z_dev(m) for m in range(1, Z)] + [y_dev, x_dev, c_dev, xy_dev]
     for dev in peers:
         pl.semaphore_signal(barrier, inc=1, device_id=dev, device_id_type=MESH)
     loads = [
@@ -361,6 +373,7 @@
         (ncot_hbm, ncot_in),
         (edges_hbm, edges),
         (cot_hbm, cot),
+        *zip(moments_hbm, moments_in),
     ]
     loads = [pltpu.make_async_copy(*pair, local_sem.at[k]) for k, pair in enumerate(loads)]
     for load in loads:
@@ -383,30 +396,26 @@
     )
     sm_src[0] = mm(small_in[...].astype(bf16), jnp.where(place, 1.0, 0.0).astype(bf16))
 
-    for load in loads[6:9]:
-        load.wait()
-    lane = lax.broadcasted_iota(jnp.int32, (128, N), 1)
-    sub = lax.broadcasted_iota(jnp.int32, (N, 128), 0)
-
-    @pl.loop(0, rows // 128)
-    def _(k):
-        at = pl.ds(pl.multiple_of(k * 128, 128), 128)
-        for half, ids in enumerate((send_in, recv_in)):
-            row = jnp.broadcast_to(ids[0:1, at], (128, 128))
-            col = jnp.tile(row.T, (1, N // 128))
-            pick[at, half * N : (half + 1) * N] = jnp.where(lane == col, 1.0, 0.0).astype(bf16)
-            flat = jnp.broadcast_to(ids[0:1, at], (N, 128))
-            spread[half * N : (half + 1) * N, at] = jnp.where(sub == flat, 1.0, 0.0).astype(bf16)
+    def update(k):
+        weight = (w1_in, w2_in, w3_in, w4_in, small_in)[k]
+        weights_out[k][...], seconds_out[k][...] = adamw(
+            weight[...],
+            grads_out[k][...],
+            moments_in[k][...],
+            moments_in[5 + k][...],
+            0.2 if k == 4 else 0.03,
+        )
 
     pl.semaphore_wait(barrier, len(peers))
 
-    def along_z(own):
-        return {1 << j: push(own, own, z_dev(1 << j)) for j in reversed(range((Z - 1).bit_length()))}
+    def along_z(own, by_bits):
+        to = [1 << j for j in range((Z - 1).bit_length())] if by_bits else range(1, Z)
+        return {m: push(own, own, z_dev(m)) for m in reversed(to)}
 
     def arrive_z(copies, m, block):
         copies[m].wait_recv()
-        j = 0
-        while not m >> j & 1:
+        j = 0 if len(copies) < Z - 1 else Z
+        while not m >> j & 1 and j < Z:
             copies[m | 1 << j] = push(block, block, z_dev(1 << j))
             j += 1
 
@@ -432,7 +441,7 @@
     n_z, n_y, b_z, b_y, b_x = {}, [], {}, [], []
     for h in range(2):
         own = part(z, y, x, h)
-        a_z[h].update(along_z(own))
+        a_z[h].update(along_z(own, geo["bits_a"]))
         a_y[0, h] = send(own, y_dev)
         a_x.append(send(own, x_dev))
         x_order.append((0, 0, h))
@@ -440,8 +449,13 @@
 
     def across(m, flip, h):
         yy = yp if flip else y
-        a_x.append(send(part(zx(m), yy, x, h), x_dev))
-        x_order.append((m, flip, h))
+        straight = m in geo["diagonal"]
+        if not (flip and straight):
+            a_x.append(send(part(zx(m), yy, x, h), x_dev))
+            x_order.append((m, flip, h))
+        if straight and not flip:
+            a_x.append(send(part(zx(m), yy, x, h), xy_dev))
+            x_order.append((m, 1, h))
         if h == 1:
             a_c.append(send(wa.at[zx(m), yy, x, c], c_dev))
             settle(zx(m), yy, x, c)
@@ -459,7 +473,7 @@
     def on_n(m, _):
         block = nbuf.at[zx(m), y]
         if m == 0:
-            n_z.update(along_z(block))
+            n_z.update(along_z(block, geo["bits_n"]))
         else:
             arrive_z(n_z, m, block)
         n_y.append(send(block, y_dev))
@@ -467,7 +481,7 @@
     def on_b(m, _):
         block = wb.at[zx(m), y, x, c]
         if m == 0:
-            b_z.update(along_z(block))
+            b_z.update(along_z(block, geo["bits_b"]))
         else:
             arrive_z(b_z, m, block)
 
@@ -494,21 +508,38 @@
             small.extend(push(sm_src.at[3], sm_tile.at[z], z_dev(m)) for m in range(1, Z))
 
     settle(z, y, x, c)
-    steps = {"z": on_z, "y": on_y, "n": on_n, "b": on_b, "l": line_b, "x": on_x, "s": on_small}
-    for step in geo["gather"]:
-        kind, (m, h) = step[0], ([int(v) for v in step[1:].split(".")] + [0])[:2]
-        if kind in "xs" or m < Z:
-            steps[kind](m, h)
+    def on_hot(*_):
+        for load in loads[6:9]:
+            load.wait()
+        lane = lax.broadcasted_iota(jnp.int32, (128, N), 1)
+        sub = lax.broadcasted_iota(jnp.int32, (N, 128), 0)
+
+        @pl.loop(0, rows // 128)
+        def _(k):
+            at = pl.ds(pl.multiple_of(k * 128, 128), 128)
+            for half, ids in enumerate((send_in, recv_in)):
+                row = jnp.broadcast_to(ids[0:1, at], (128, 128))
+                col = jnp.tile(row.T, (1, N // 128))
+                pick[at, half * N : (half + 1) * N] = jnp.where(lane == col, 1.0, 0.0).astype(bf16)
+                flat = jnp.broadcast_to(ids[0:1, at], (N, 128))
+                spread[half * N : (half + 1) * N, at] = jnp.where(sub == flat, 1.0, 0.0).astype(bf16)
+
+    steps = (on_z, on_y, on_n, on_b, line_b, on_x, on_small, on_hot)
+
+    def gather(name):
+        for step in geo[name]:
+            kind, m, h = decode(step, 10)
+            if kind > 5 or m < Z:
+                steps[kind](m, h)
+
+    gather("gather")
     on_x(0, len(x_order))
     for copy in n_y:
         copy.wait_recv()
     loads[9].wait()
     for copy in a_c:
         copy.wait_recv()
-    for step in geo["late"]:
-        kind, m = step[0], int(step[1:])
-        if m < Z:
-            steps[kind](m, 0)
+    gather("late")
     for zz in range(Z):
         for yy in range(Y):
             for xx in range(X):
@@ -542,16 +573,14 @@
         term[at, :] = jnp.where(live, new, 0.0).astype(bf16)
 
     edge_forward(0)
-    for step in geo["mid"]:
-        kind, m = step[0], int(step[1:])
-        if m < Z:
-            steps[kind](m, 0)
+    gather("mid")
     edge_forward(1)
 
     order = tuple(reversed(range(Z)))
 
     class NodeSum:
-        def __init__(self, pb, yr, zs, zr):
+        def __init__(self, by_bits, pb, yr, zs, zr):
+            self.by_bits = by_bits
             self.pb, self.yr, self.zs, self.zr = pb, yr, zs, zr
             self.y, self.z = {}, {}
 
@@ -568,10 +597,14 @@
         def turn(self, m, h):
             self.y[m, h].wait_recv()
             pf[zx(m), y, h] = pf[zx(m), y, h] + self.yr[m, h].astype(f32)
-            if m % 2:
+            if not self.by_bits and m:
+                self.over(m, h, m)
+            elif m % 2:
                 self.over(m, h, 1)
 
         def merge(self, m, h):
+            if not self.by_bits:
+                return
             self.z[m + 1, h].wait_recv()
             pf[zx(m), y, h] = pf[zx(m), y, h] + self.zr[m, h].astype(f32)
             if m:
@@ -581,13 +614,13 @@
             sums = []
             for h in range(2):
                 part = pf[z, y, h]
-                for m in range(2, Z, 2):
+                for m in range(2, Z, 2) if self.by_bits else range(1, Z):
                     self.z[m, h].wait_recv()
                     part = part + self.zr[m - 1, h].astype(f32)
                 sums.append(part)
             return jnp.concatenate(sums, axis=0)
 
-    agg_sum = NodeSum(pb_a, yr_a, zs_a, zr_a)
+    agg_sum = NodeSum(geo["bits_agg"], pb_a, yr_a, zs_a, zr_a)
     b_c, early = [], {}
 
     def step_p(m, _):
@@ -614,11 +647,10 @@
             w4[...] = wb[:, :, :, :, r3 : r3 + r4, :].reshape(w4.shape)
             early["pre"] = mm(nodes_in[...], w3[0:D, :])
 
-    sums_n = {"p": step_p, "b": step_b, "t": agg_sum.turn, "g": agg_sum.merge}
     for step in geo["agg"]:
-        kind, (m, h) = step[0], ([int(v) for v in step[1:].split(".")] + [0])[:2]
-        if kind == "b" or m < Z:
-            sums_n[kind](m, h)
+        kind, m, h = decode(step, 10)
+        if kind == 3 or m < Z:
+            (step_p, agg_sum.turn, agg_sum.merge, step_b)[kind](m, h)
     own_nodes = nodes_in[...]
     agg = agg_sum.total()
 
@@ -644,7 +676,7 @@
     def step_d(m, h):
         block = d_part(m, h)
         if m == 0:
-            d_z[h] = along_z(block)
+            d_z[h] = along_z(block, geo["bits_d"])
         else:
             arrive_z(d_z[h], m, block)
         d_y.append(send(block, y_dev))
@@ -652,7 +684,10 @@
     for h in range(2):
         step_d(0, h)
     class WeightSum:
-        def __init__(self, grad, crecv, xs, xrecv, ks, ys, yrecv, zs, zrecv):
+        def __init__(self, x_first, grad, crecv, xs, xrecv, ks, ys, yrecv, zs, zrecv):
+            self.first, self.second = (x_dev, y_dev) if x_first else (y_dev, x_dev)
+            side = ((y, xp), (yp, x)) if x_first else ((yp, x), (y, xp))
+            self.groups = ((yp, xp), side[0], side[1], (y, x))
             self.grad, self.crecv, self.xs, self.xrecv, self.ks = grad, crecv, xs, xrecv, ks
             self.ys, self.yrecv, self.zs, self.zrecv = ys, yrecv, zs, zrecv
 
@@ -669,7 +704,7 @@
         def start(self):
             self.c = [
                 push(self.grad.at[:, yy, xx, cp], self.crecv.at[k], c_dev)
-                for k, (yy, xx) in enumerate(((yp, xp), (y, xp), (yp, x), (y, x)))
+                for k, (yy, xx) in enumerate(self.groups)
             ]
 
             self.x, self.y, self.z = {}, {}, {}
@@ -677,24 +712,26 @@
         def cross_x(self, k):
             self.c[k].wait_recv()
             for m in order:
-                part = self.grad[zx(m), (yp, y)[k % 2], (xp, x)[k // 2], c].astype(f32)
+                part = self.grad[(zx(m), *self.groups[k], c)].astype(f32)
                 part = part + self.crecv[k, zx(m)].astype(f32)
                 if k < 2:
                     self.xs[k, m] = part.astype(bf16)
-                    self.x[k, m] = push(self.xs.at[k, m], self.xrecv.at[k, m], x_dev)
+                    self.x[k, m] = push(self.xs.at[k, m], self.xrecv.at[k, m], self.first)
                 else:
                     self.ks[k - 2, m] = part
 
         def cross_y(self, m):
             self.x[0, m].wait_recv()
             self.ys[m] = (self.ks[0, m] + self.xrecv[0, m].astype(f32)).astype(bf16)
-            self.y[m] = push(self.ys.at[m], self.yrecv.at[m], y_dev)
+            self.y[m] = push(self.ys.at[m], self.yrecv.at[m], self.second)
 
         def cross_z(self, m):
             self.x[1, m].wait_recv()
             self.y[m].wait_recv()
             part = self.ks[1, m] + self.xrecv[1, m].astype(f32) + self.yrecv[m].astype(f32)
-            if m % 2:
+            if not geo["bits_w"] and m:
+                self.over(part, m, m)
+            elif m % 2:
                 self.over(part, m, 1)
             else:
                 self.ks[1, m] = part
@@ -704,6 +741,8 @@
             self.z[m] = push(self.zs.at[m - 1], self.zrecv.at[m - 1], z_dev(low))
 
         def merge(self, m):
+            if not geo["bits_w"]:
+                return
             self.z[m + 1].wait_recv()
             part = self.ks[1, m] + self.zrecv[m].astype(f32)
             if m:
@@ -713,13 +752,15 @@
 
         def total(self):
             result = self.ks[1, 0]
-            for m in range(2, Z, 2):
+            for m in range(2, Z, 2) if geo["bits_w"] else range(1, Z):
                 self.z[m].wait_recv()
                 result = result + self.zrecv[m - 1].astype(f32)
             return result
 
     per = len(grad_refs) // 4
-    sum1a, sum1b, sum2, sum_n = [WeightSum(*grad_refs[k * per : (k + 1) * per]) for k in range(4)]
+    sum1a, sum1b, sum2, sum_n = [
+        WeightSum(geo["x_first"][k], *grad_refs[k * per : (k + 1) * per]) for k in range(4)
+    ]
 
     sum_n.put(0, inner(own_nodes, d_pre_n), r3)
     sum_n.put(D, inner(agg_low, d_pre_n), r3)
@@ -731,12 +772,14 @@
     gsm[5:6, :] = jnp.sum(d_out_n.astype(f32), axis=0, keepdims=True)
     gsm[6:7, :] = jnp.sum(ncot * normed_n, axis=0, keepdims=True)
     gsm[7:8, :] = jnp.sum(ncot, axis=0, keepdims=True)
-    parts_d = {"d": step_d, "x": lambda k, _: sum_n.cross_x(k)}
     for step in geo["back"]:
-        kind, (m, h) = step[0], ([int(v) for v in step[1:].split(".")] + [0])[:2]
-        if kind == "x" or m < Z:
-            parts_d[kind](m, h)
-    loads[10].wait()
+        kind, m, h = decode(step, 10)
+        if kind == 1:
+            sum_n.cross_x(m)
+        elif m < Z:
+            step_d(m, h)
+    for load in loads[10:]:
+        load.wait()
     for copy in d_y:
         copy.wait_recv()
 
@@ -777,33 +820,35 @@
             into.put((1 + half) * D, inner(nodes_all, seg[nodes_at, at]))
         into.start()
 
-    sums_w = {"a": sum1a, "b": sum1b, "c": sum2, "n": sum_n}
+    sums_w = (sum1a, sum1b, sum2, sum_n)
     gm = []
-    node_sum = NodeSum(pb_n, yr_n, zs_n, zr_n)
+    node_sum = NodeSum(geo["bits_node"], pb_n, yr_n, zs_n, zr_n)
 
     def step_w(which, _):
-        if which == "c":
+        if which == 2:
             sum2.put(0, inner(hidden[...], dout[...]))
             sum2.start()
         else:
-            edge_grads("ab".index(which), sums_w[which])
+            edge_grads(which, sums_w[which])
 
     def step_t(which, _):
-        if which == "N":
+        if which == 4:
             ngrad_out[...] = (node_part + node_sum.total()).astype(bf16)
             return
         result = sums_w[which].total()
-        if which == "n":
+        if which == 3:
             g3_out[...] = result[0:r3]
             g4_out[...] = result[r3 : r3 + r4]
-        elif which == "c":
+            update(2)
+            update(3)
+        elif which == 2:
             g2_out[...] = result
+            update(1)
         else:
-            k = "ab".index(which)
-            g1_out[:, k * (D // 2) : (k + 1) * (D // 2)] = result
+            g1_out[:, which * (D // 2) : (which + 1) * (D // 2)] = result
 
     def step_n(which, k):
-        if which == "s":
+        if which == 6:
             total = times_t(seg[0:N, :], w1[D : 2 * D, :])
             total = total + times_t(seg[N : 2 * N, :], w1[2 * D : 3 * D, :])
             pf[...] = total.reshape(pf.shape)
@@ -811,10 +856,10 @@
             for m in order:
                 for h in range(2):
                     node_sum.y[m, h] = push(pb_n.at[zx(m), yp, h], yr_n.at[m, h], y_dev)
-        elif which in "gh":
-            node_sum.turn(k, "gh".index(which))
+        elif which < 9:
+            node_sum.turn(k, which - 7)
         else:
-            node_sum.merge(k, "mo".index(which))
+            node_sum.merge(k, which - 9)
 
     def step_e(*_):
         for i in range(2):
@@ -852,54 +897,38 @@
                 preferred_element_type=f32,
                 precision=lax.Precision.HIGHEST,
             )
-
-    tail = {
-        "w": step_w,
-        "x": lambda which, k: sums_w[which].cross_x(k),
-        "y": lambda which, m: sums_w[which].cross_y(m),
-        "z": lambda which, m: sums_w[which].cross_z(m),
-        "m": lambda which, m: sums_w[which].merge(m),
-        "t": step_t,
-        "n": step_n,
-        "e": step_e,
-        "g": step_g,
-    }
+            update(4)
+
+    tail = (
+        step_w,
+        lambda which, k: sums_w[which].cross_x(k),
+        lambda which, m: sums_w[which].cross_y(m),
+        lambda which, m: sums_w[which].cross_z(m),
+        lambda which, m: sums_w[which].merge(m),
+        step_n,
+        step_t,
+        step_e,
+        step_g,
+    )
     for step in geo["tail"]:
-        kind, which, k = step[0], step[1:2], int(step[2:] or 0)
-        if kind not in "yzmn" or k < Z:
+        kind, which, k = decode(step, 100)
+        if not 2 <= kind <= 5 or k < Z:
             tail[kind](which, k)
+    update(0)
     for copy in started:
         copy.wait_send()
 
 
-def update_kernel(*refs):
-    passed, weights, firsts, seconds = refs[0:9], refs[9:14], refs[14:19], refs[19:24]
-    outs, new_v, new_w, smalls, sem = refs[24:43], refs[43:47], refs[47:51], refs[51:54], refs[54]
-    enew, egrad, nnew, ngrad, *grads = passed
+def deliver_kernel(*refs):
+    count = len(refs) // 2
     copies = []
-
-    def put(src, dst):
-        copies.append(pltpu.make_async_copy(src, dst, sem.at[len(copies)]))
-        copies[-1].start()
-
-    for src, dst in zip((weights[4], firsts[4], seconds[4]), smalls):
-        put(src, dst)
-    for src, dst in zip((enew, nnew, egrad, ngrad), outs[:4]):
-        put(src, dst.at[0])
-    for k in range(4):
-        put(grads[k], outs[4 + k])
-    outs[8][...] = grads[4][...]
-    for k in range(4):
-        new_w[k][...], new_v[k][...] = adamw(
-            weights[k][...], grads[k][...], firsts[k][...], seconds[k][...], 0.03
-        )
-        put(new_v[k], outs[9 + k])
-        put(new_w[k], outs[14 + k])
-    for copy in copies[:3]:
-        copy.wait()
-    small, first, second = (ref[...] for ref in smalls)
-    outs[18][...], outs[13][...] = adamw(small, grads[4][...], first, second, 0.2)
-    for copy in copies[3:]:
+    for k in range(count):
+        dst = refs[count + k]
+        dst = dst.at[0] if k < 4 else dst
+        copies.append(pltpu.make_async_copy(refs[k], dst, refs[-1].at[k]))
+    for copy in copies:
+        copy.start()
+    for copy in copies:
         copy.wait()
 
 
@@ -941,9 +970,12 @@
     def vm(shape, dtype=bf16):
         return pltpu.VMEM(shape, dtype)
 
-    ins = [edge_lat[0], edge_cot[0], node_lat[0], node_cot[0], senders, receivers, edge_count, *weights]
+    ins = [edge_lat[0], edge_cot[0], node_lat[0], node_cot[0], senders, receivers, edge_count]
+    ins += [*weights, *firsts, *seconds]
+    moments = [vm(m.shape, f32) for m in (*firsts, *seconds)]
     scratch = [
-        *[vm(a.shape, a.dtype) for a in ins if a is not edge_count],
+        *moments,
+        *[vm(a.shape, a.dtype) for a in ins[:12] if a is not edge_count],
         vm((Z, Y, n, D)),
         vm((Z, Y, n, D)),
         *[vm((r * n_dev, D)) for r in shards],
@@ -998,11 +1030,12 @@
     hbm = pl.BlockSpec(memory_space=pltpu.HBM)
     anyspace = pl.BlockSpec(memory_space=pl.ANY)
     vmem = pl.BlockSpec(memory_space=pltpu.VMEM)
+    state_out = [vm(w.shape, f32) for w in weights]
     results = pl.pallas_call(
         functools.partial(layer_kernel, dict(GEO, dims=(Z, Y, X, C), n_sem=n_sem)),
-        out_shape=[vm((rows, D))] * 2 + [vm((n, D))] * 2 + [vm(w.shape, f32) for w in weights],
-        in_specs=[hbm] * 6 + [pl.BlockSpec(memory_space=pltpu.SMEM)] + [hbm] * 5,
-        out_specs=[vmem] * 9,
+        out_shape=[vm((rows, D)), vm((n, D))] * 2 + state_out * 3,
+        in_specs=[hbm] * 6 + [pl.BlockSpec(memory_space=pltpu.SMEM)] + [hbm] * 15,
+        out_specs=[vmem] * 19,
         scratch_shapes=scratch,
         compiler_params=pltpu.CompilerParams(
             collective_id=0, has_side_effects=True, vmem_limit_bytes=52 * 1024 * 1024
@@ -1010,31 +1043,17 @@
         name="layer",
     )(*ins)
     sds = jax.ShapeDtypeStruct
-    state_out = [sds(w.shape, f32) for w in weights]
-    kept = [vm(w.shape, f32) for w in weights[:4]]
+    shapes = [sds((1, *r.shape) if k < 4 else r.shape, r.dtype) for k, r in enumerate(results)]
     return tuple(
         pl.pallas_call(
-            update_kernel,
-            out_shape=[
-                sds((1, rows, D), bf16),
-                sds((1, n, D), bf16),
-                sds((1, rows, D), bf16),
-                sds((1, n, D), bf16),
-                *state_out,
-                *state_out,
-                *state_out,
-            ],
-            in_specs=[vmem] * 9 + ([vmem] * 4 + [hbm]) * 3,
-            out_specs=[anyspace] * 4 + ([anyspace] * 4 + [vmem]) * 3,
-            scratch_shapes=[
-                *kept,
-                *kept,
-                *[vm(weights[4].shape, f32)] * 3,
-                pltpu.SemaphoreType.DMA((19,)),
-            ],
+            deliver_kernel,
+            out_shape=shapes,
+            in_specs=[vmem] * 19,
+            out_specs=[anyspace] * 19,
+            scratch_shapes=[pltpu.SemaphoreType.DMA((19,))],
             compiler_params=pltpu.CompilerParams(vmem_limit_bytes=8 * 1024 * 1024),
-            name="update",
-        )(*results, *weights, *firsts, *seconds)
+            name="deliver",
+        )(*results)
     )
 
 

time: 84.5 us -> 80.5 us (0.953)
  Pallas kernels: 82.1 us -> 78.9 us
    pallas_call x1, Pallas kernels: 79.8 us -> 77.1 us  [on_device(): pl.pallas_call(functools.partial(layer_kernel, dict(GEO, dims=(Z, Y, X, C...]
where the time goes in v5:
time: 80.5 us; the launch traced here: 80.4 us
  Pallas kernels  78.9 us (98%)
  between operations  1.48 us (2%)
    pallas_call x1, Pallas kernels, on_device(): pl.pallas_call(functools.partial(layer_kernel, dict(GEO, dims=(Z, Y, X, C...  77.1 us
    pallas_call x1, Pallas kernels, on_device(): pl.pallas_call(deliver_kernel, out_shape=shapes, in_specs=[vmem] * 19, ou...  1.77 us

profile of v5, /device:TPU:0, one launch (start us, length us, event | category | flops | bytes accessed | tf_op | source)
XLA Modules:
  0.0 80.4 jit_solution(17290533695511464292)
XLA Ops:
  1.3 77.1 %layer.1 = (bf16[1024,512]{1,0:T(8,128)(2,1)S(1)}, bf16[64,512]{1,0:T(8,128)(2,1)S(1)}, bf16[1024,512]{1,0:T(8,128)(2,1)S(1)}, bf16[64,512]{1,0:T(8,128)(2,1)S(1...) custom-call(bf16[1024,512]{1,0:T(8,128)(2,1)} %bitcast.4, ...), custom_call_target="tpu_custom_call" | custom-call | tf_op jit(solution)/shard_map/layer/pallas_call | solution.py:1034
  78.4 1.8 %deliver.1 = (bf16[1,1024,512]{2,1,0:T(8,128)(2,1)}, bf16[1,64,512]{2,1,0:T(8,128)(2,1)}, bf16[1,1024,512]{2,1,0:T(8,128)(2,1)}, bf16[1,64,512]{2,1,0:T(8,128)(2...) custom-call(bf16[1024,512]{1,0:T(8,128)(2,1)S(1)} %get-tuple-element, ...), custom_call_target="tpu_custom_call" | custom-call | tf_op jit(solution)/shard_map/deliver/pallas_call | solution.py:1048

commit v6 on v5

--- a/solution.py
+++ b/solution.py
@@ -201,9 +201,9 @@
     "bits_n": True,
     "bits_b": True,
     "bits_d": True,
-    "bits_agg": True,
+    "bits_agg": False,
     "bits_node": False,
-    "bits_w": False,
+    "bits_w": (False, False, False, False),
     "gather": (
         200, 700, 100, 10, 101, 20, 11, 21, 120, 110, 600, 30, 111, 31, 610, 220, 121, 210, 130,
         300, 131, 230, 620
@@ -215,18 +215,16 @@
         330, 430
     ),
     "agg": (
-        30, 300, 20, 10, 0, 130, 131, 121, 310, 120, 110, 220, 221, 320, 100, 111, 101, 330, 200,
-        201
-    ),
-    "back": (
-        100, 110, 10, 20, 21, 11, 30, 120, 130, 31
+        30, 600, 10, 20, 111, 121, 131, 230, 0, 210, 101, 220, 221, 610, 620, 231, 211, 200, 630,
+        201, 300, 301, 700, 701, 320, 800, 420, 410, 321, 421, 500, 411, 510, 520, 430, 530, 431
     ),
     "tail": (
-        0, 8050, 10, 3032, 5060, 3033, 1000, 1012, 1010, 1002, 1001, 3030, 4032, 5073, 20, 5083,
-        2002, 1011, 1022, 5082, 1013, 1003, 3031, 2003, 5081, 1020, 2012, 8051, 2001, 5072, 3003,
-        2013, 4030, 5070, 5092, 2023, 1023, 3002, 2011, 5080, 1021, 2020, 2021, 2000, 2010, 2022,
-        5071, 3012, 3013, 5090, 4002, 3001, 3011, 5100, 7050, 3023, 8052, 3022, 4012, 3021, 5102,
-        3020, 8053, 8054, 3010, 6040, 4010, 3000, 6030, 4000, 6000, 4022, 6010, 4020, 6020
+        2032, 9050, 2031, 2033, 9051, 10051, 10050, 0, 3032, 2030, 10, 5060, 8050, 1000, 1010, 3033,
+        3030, 1012, 1001, 1002, 20, 5073, 5083, 1022, 3031, 8051, 1003, 5082, 2003, 2002, 2013,
+        1020, 5072, 5081, 2011, 5071, 1011, 1013, 2012, 2001, 7050, 5070, 1021, 1023, 5080, 5102,
+        3003, 2023, 3013, 2021, 3002, 5090, 5092, 4030, 2022, 8052, 4002, 3011, 3012, 2010, 3001,
+        2000, 4032, 2020, 4012, 3023, 5100, 3022, 3021, 3020, 8053, 3010, 6040, 4010, 3000, 8054,
+        6030, 4000, 6000, 4020, 6010, 4022, 6020
     ),
 }
 
@@ -300,6 +298,13 @@
         zr_a,
         zr_n,
         seg,
+        pre_own,
+        norm_n,
+        node_part,
+        agg_low,
+        hidden_n,
+        dout_n,
+        dpre_n,
         sm_src,
         sm_rcv,
         sm_tile,
@@ -587,8 +592,9 @@
         def put(self, m, values):
             pf[zx(m)] = values.reshape(Y, 2, n // 2, D)
             self.pb[zx(m)] = values.astype(bf16).reshape(Y, 2, n // 2, D)
-            for h in range(2):
-                self.y[m, h] = push(self.pb.at[zx(m), yp, h], self.yr.at[m, h], y_dev)
+
+        def go(self, m, h):
+            self.y[m, h] = push(self.pb.at[zx(m), yp, h], self.yr.at[m, h], y_dev)
 
         def over(self, m, h, low):
             self.zs[m - 1, h] = pf[zx(m), y, h].astype(bf16)
@@ -610,22 +616,100 @@
             if m:
                 self.over(m, h, 2)
 
+        def total(self, h):
+            part = pf[z, y, h]
+            for m in range(2, Z, 2) if self.by_bits else range(1, Z):
+                self.z[m, h].wait_recv()
+                part = part + self.zr[m - 1, h].astype(f32)
+            return part
+
+    class WeightSum:
+        def __init__(self, x_first, by_bits, grad, crecv, xs, xrecv, ks, ys, yrecv, zs, zrecv):
+            self.by_bits = by_bits
+            self.first, self.second = (x_dev, y_dev) if x_first else (y_dev, x_dev)
+            side = ((y, xp), (yp, x)) if x_first else ((yp, x), (y, xp))
+            self.groups = ((yp, xp), side[0], side[1], (y, x))
+            self.grad, self.crecv, self.xs, self.xrecv, self.ks = grad, crecv, xs, xrecv, ks
+            self.ys, self.yrecv, self.zs, self.zrecv = ys, yrecv, zs, zrecv
+
+        def put(self, first, values, lane_rows=None, base=0):
+            low, r = values.astype(bf16), lane_rows or self.grad.shape[4]
+            row = 0
+            while row < values.shape[0]:
+                k, off = divmod(first + row, r)
+                size = min(r - off, values.shape[0] - row)
+                at = (k // (Y * X * C), k // (X * C) % Y, k // C % X, k % C)
+                self.grad[(*at, slice(base + off, base + off + size))] = low[row : row + size]
+                row += size
+
+        def start(self):
+            self.c = [
+                push(self.grad.at[:, yy, xx, cp], self.crecv.at[k], c_dev)
+                for k, (yy, xx) in enumerate(self.groups)
+            ]
+
+            self.x, self.y, self.z = {}, {}, {}
+
+        def cross_x(self, k):
+            self.c[k].wait_recv()
+            for m in order:
+                part = self.grad[(zx(m), *self.groups[k], c)].astype(f32)
+                part = part + self.crecv[k, zx(m)].astype(f32)
+                if k < 2:
+                    self.xs[k, m] = part.astype(bf16)
+                    self.x[k, m] = push(self.xs.at[k, m], self.xrecv.at[k, m], self.first)
+                else:
+                    self.ks[k - 2, m] = part
+
+        def cross_y(self, m):
+            self.x[0, m].wait_recv()
+            self.ys[m] = (self.ks[0, m] + self.xrecv[0, m].astype(f32)).astype(bf16)
+            self.y[m] = push(self.ys.at[m], self.yrecv.at[m], self.second)
+
+        def cross_z(self, m):
+            self.x[1, m].wait_recv()
+            self.y[m].wait_recv()
+            part = self.ks[1, m] + self.xrecv[1, m].astype(f32) + self.yrecv[m].astype(f32)
+            if not self.by_bits and m:
+                self.over(part, m, m)
+            elif m % 2:
+                self.over(part, m, 1)
+            else:
+                self.ks[1, m] = part
+
+        def over(self, part, m, low):
+            self.zs[m - 1] = part.astype(bf16)
+            self.z[m] = push(self.zs.at[m - 1], self.zrecv.at[m - 1], z_dev(low))
+
+        def merge(self, m):
+            if not self.by_bits:
+                return
+            self.z[m + 1].wait_recv()
+            part = self.ks[1, m] + self.zrecv[m].astype(f32)
+            if m:
+                self.over(part, m, 2)
+            else:
+                self.ks[1, 0] = part
+
         def total(self):
-            sums = []
-            for h in range(2):
-                part = pf[z, y, h]
-                for m in range(2, Z, 2) if self.by_bits else range(1, Z):
-                    self.z[m, h].wait_recv()
-                    part = part + self.zr[m - 1, h].astype(f32)
-                sums.append(part)
-            return jnp.concatenate(sums, axis=0)
+            result = self.ks[1, 0]
+            for m in range(2, Z, 2) if self.by_bits else range(1, Z):
+                self.z[m].wait_recv()
+                result = result + self.zrecv[m - 1].astype(f32)
+            return result
+
+    per = len(grad_refs) // 4
+    sum1a, sum1b, sum2, sum_n = [
+        WeightSum(geo["x_first"][k], geo["bits_w"][k], *grad_refs[k * per : (k + 1) * per]) for k in range(4)
+    ]
 
     agg_sum = NodeSum(geo["bits_agg"], pb_a, yr_a, zs_a, zr_a)
-    b_c, early = [], {}
+    b_c = []
 
     def step_p(m, _):
         first_row = pl.multiple_of(N + zx(m) * (Y * n), Y * n)
         agg_sum.put(m, mm(spread[pl.ds(first_row, Y * n), :], term[...]))
+        agg_sum.go(m, 0)
 
     def step_b(k, _):
         if k == 0:
@@ -645,29 +729,30 @@
                 copy.wait_recv()
             w3[...] = wb[:, :, :, :, 0:r3, :].reshape(w3.shape)
             w4[...] = wb[:, :, :, :, r3 : r3 + r4, :].reshape(w4.shape)
-            early["pre"] = mm(nodes_in[...], w3[0:D, :])
-
-    for step in geo["agg"]:
-        kind, m, h = decode(step, 10)
-        if kind == 3 or m < Z:
-            (step_p, agg_sum.turn, agg_sum.merge, step_b)[kind](m, h)
-    own_nodes = nodes_in[...]
-    agg = agg_sum.total()
+            pre_own[...] = mm(nodes_in[...], w3[0:D, :])
 
     def par(k):
         return par_all[k : k + 1, :]
 
-    agg_low = agg.astype(bf16)
-    pre_n = early["pre"] + mm(agg_low, w3[D : 2 * D, :]) + par(4)
-    sig_n = jax.nn.sigmoid(pre_n)
-    hidden_n = (pre_n * sig_n).astype(bf16)
-    out_n = mm(hidden_n, w4[...]) + par(5)
-    normed_n, rstd_n = norm_stats(out_n)
-    ncot = ncot_in[...].astype(f32)
-    d_out_n = norm_back(ncot, normed_n, rstd_n, par(6)).astype(bf16)
-    slope_n = sig_n * (1.0 + pre_n * (1.0 - sig_n))
-    d_pre_n = (times_t(d_out_n, w4[...]) * slope_n).astype(bf16)
-    dbuf[z, y] = times_t(d_pre_n, w3[D : 2 * D, :]).astype(bf16)
+    def step_node(_, h):
+        at = slice(h * (n // 2), (h + 1) * (n // 2))
+        low = agg_sum.total(h).astype(bf16)
+        agg_low[at, :] = low
+        pre_n = pre_own[at, :] + mm(low, w3[D : 2 * D, :]) + par(4)
+        sig_n = jax.nn.sigmoid(pre_n)
+        act_n = (pre_n * sig_n).astype(bf16)
+        hidden_n[at, :] = act_n
+        normed_n, rstd_n = norm_stats(mm(act_n, w4[...]) + par(5))
+        ncot = ncot_in[at, :].astype(f32)
+        d_out_n = norm_back(ncot, normed_n, rstd_n, par(6)).astype(bf16)
+        dout_n[at, :] = d_out_n
+        slope_n = sig_n * (1.0 + pre_n * (1.0 - sig_n))
+        d_pre_n = (times_t(d_out_n, w4[...]) * slope_n).astype(bf16)
+        dpre_n[at, :] = d_pre_n
+        dbuf[z, y, at, :] = times_t(d_pre_n, w3[D : 2 * D, :]).astype(bf16)
+        step_d(0, h)
+        norm_n[at, :] = normed_n
+
     d_z, d_y = {}, []
 
     def d_part(m, h):
@@ -681,112 +766,48 @@
             arrive_z(d_z[h], m, block)
         d_y.append(send(block, y_dev))
 
-    for h in range(2):
-        step_d(0, h)
-    class WeightSum:
-        def __init__(self, x_first, grad, crecv, xs, xrecv, ks, ys, yrecv, zs, zrecv):
-            self.first, self.second = (x_dev, y_dev) if x_first else (y_dev, x_dev)
-            side = ((y, xp), (yp, x)) if x_first else ((yp, x), (y, xp))
-            self.groups = ((yp, xp), side[0], side[1], (y, x))
-            self.grad, self.crecv, self.xs, self.xrecv, self.ks = grad, crecv, xs, xrecv, ks
-            self.ys, self.yrecv, self.zs, self.zrecv = ys, yrecv, zs, zrecv
-
-        def put(self, first, values, lane_rows=None, base=0):
-            low, r = values.astype(bf16), lane_rows or self.grad.shape[4]
-            row = 0
-            while row < values.shape[0]:
-                k, off = divmod(first + row, r)
-                size = min(r - off, values.shape[0] - row)
-                at = (k // (Y * X * C), k // (X * C) % Y, k // C % X, k % C)
-                self.grad[(*at, slice(base + off, base + off + size))] = low[row : row + size]
-                row += size
-
-        def start(self):
-            self.c = [
-                push(self.grad.at[:, yy, xx, cp], self.crecv.at[k], c_dev)
-                for k, (yy, xx) in enumerate(self.groups)
-            ]
-
-            self.x, self.y, self.z = {}, {}, {}
-
-        def cross_x(self, k):
-            self.c[k].wait_recv()
-            for m in order:
-                part = self.grad[(zx(m), *self.groups[k], c)].astype(f32)
-                part = part + self.crecv[k, zx(m)].astype(f32)
-                if k < 2:
-                    self.xs[k, m] = part.astype(bf16)
-                    self.x[k, m] = push(self.xs.at[k, m], self.xrecv.at[k, m], self.first)
-                else:
-                    self.ks[k - 2, m] = part
-
-        def cross_y(self, m):
-            self.x[0, m].wait_recv()
-            self.ys[m] = (self.ks[0, m] + self.xrecv[0, m].astype(f32)).astype(bf16)
-            self.y[m] = push(self.ys.at[m], self.yrecv.at[m], self.second)
-
-        def cross_z(self, m):
-            self.x[1, m].wait_recv()
-            self.y[m].wait_recv()
-            part = self.ks[1, m] + self.xrecv[1, m].astype(f32) + self.yrecv[m].astype(f32)
-            if not geo["bits_w"] and m:
-                self.over(part, m, m)
-            elif m % 2:
-                self.over(part, m, 1)
-            else:
-                self.ks[1, m] = part
-
-        def over(self, part, m, low):
-            self.zs[m - 1] = part.astype(bf16)
-            self.z[m] = push(self.zs.at[m - 1], self.zrecv.at[m - 1], z_dev(low))
-
-        def merge(self, m):
-            if not geo["bits_w"]:
-                return
-            self.z[m + 1].wait_recv()
-            part = self.ks[1, m] + self.zrecv[m].astype(f32)
-            if m:
-                self.over(part, m, 2)
-            else:
-                self.ks[1, 0] = part
-
-        def total(self):
-            result = self.ks[1, 0]
-            for m in range(2, Z, 2) if geo["bits_w"] else range(1, Z):
-                self.z[m].wait_recv()
-                result = result + self.zrecv[m - 1].astype(f32)
-            return result
-
-    per = len(grad_refs) // 4
-    sum1a, sum1b, sum2, sum_n = [
-        WeightSum(geo["x_first"][k], *grad_refs[k * per : (k + 1) * per]) for k in range(4)
-    ]
-
-    sum_n.put(0, inner(own_nodes, d_pre_n), r3)
-    sum_n.put(D, inner(agg_low, d_pre_n), r3)
-    sum_n.put(0, inner(hidden_n, d_out_n), r4, r3)
-    sum_n.start()
-    nnew_out[...] = (own_nodes.astype(f32) + normed_n * par(6) + par(7)).astype(bf16)
-    node_part = ncot + times_t(d_pre_n, w3[0:D, :])
-    gsm[4:5, :] = jnp.sum(d_pre_n.astype(f32), axis=0, keepdims=True)
-    gsm[5:6, :] = jnp.sum(d_out_n.astype(f32), axis=0, keepdims=True)
-    gsm[6:7, :] = jnp.sum(ncot * normed_n, axis=0, keepdims=True)
-    gsm[7:8, :] = jnp.sum(ncot, axis=0, keepdims=True)
-    for step in geo["back"]:
+    def step_wn(*_):
+        own_nodes, ncot = nodes_in[...], ncot_in[...].astype(f32)
+        normed_n, d_pre_n, d_out_n = norm_n[...], dpre_n[...], dout_n[...]
+        sum_n.put(0, inner(own_nodes, d_pre_n), r3)
+        sum_n.put(D, inner(agg_low[...], d_pre_n), r3)
+        sum_n.put(0, inner(hidden_n[...], d_out_n), r4, r3)
+        sum_n.start()
+        nnew_out[...] = (own_nodes.astype(f32) + normed_n * par(6) + par(7)).astype(bf16)
+        node_part[...] = ncot + times_t(d_pre_n, w3[0:D, :])
+        gsm[4:5, :] = jnp.sum(d_pre_n.astype(f32), axis=0, keepdims=True)
+        gsm[5:6, :] = jnp.sum(d_out_n.astype(f32), axis=0, keepdims=True)
+        gsm[6:7, :] = jnp.sum(ncot * normed_n, axis=0, keepdims=True)
+        gsm[7:8, :] = jnp.sum(ncot, axis=0, keepdims=True)
+
+    steps_n = (
+        step_p,
+        agg_sum.go,
+        agg_sum.turn,
+        agg_sum.merge,
+        step_d,
+        lambda k, _: sum_n.cross_x(k),
+        step_b,
+        step_node,
+        step_wn,
+    )
+    for step in geo["agg"]:
         kind, m, h = decode(step, 10)
-        if kind == 1:
-            sum_n.cross_x(m)
-        elif m < Z:
-            step_d(m, h)
+        if kind > 4 or m < Z:
+            steps_n[kind](m, h)
     for load in loads[10:]:
         load.wait()
     for copy in d_y:
         copy.wait_recv()
 
     sums[...] = jnp.zeros_like(sums)
+
+    def add_sums(k, at, values):
+        sums[k, :, at] += fold_rows(values)
+
     d_all = dbuf[...].reshape(N, D)
 
-    def edge_back(i):
+    def step_v(_, i):
         at = slice(i * R, (i + 1) * R)
         live = row_id < count - i * R
         d_edge = cot[at, :].astype(f32) + jnp.where(live, mm(pick[at, N : 2 * N], d_all), 0.0)
@@ -795,19 +816,18 @@
         norm = normed[at, :]
         inv = rstd[at, 0:1]
         weighted = masked * norm
-        sums[2] += fold_rows(weighted)
-        sums[3] += fold_rows(masked)
+        add_sums(2, slice(0, D), weighted)
+        add_sums(3, slice(0, D), masked)
         d_out = norm_back(masked, norm, inv, par(2)).astype(bf16)
         dout[at, :] = d_out
-        sums[1] += fold_rows(d_out.astype(f32))
-        d_pre = (times_t(d_out, w2[...]) * slope[at, :]).astype(bf16)
-        dpre[at, :] = d_pre
-        sums[0] += fold_rows(d_pre.astype(f32))
-
-    edge_back(0)
-    for m in order:
-        sum_n.cross_y(m)
-    edge_back(1)
+        add_sums(1, slice(0, D), d_out.astype(f32))
+
+    def step_d(_, k):
+        at = slice(k * (D // 2), (k + 1) * (D // 2))
+        d_pre = (times_t(dout[...], w2[at, :]) * slope[:, at]).astype(bf16)
+        dpre[:, at] = d_pre
+        add_sums(0, at, d_pre.astype(f32))
+
     edges_all = edges[...]
 
     def edge_grads(k, into):
@@ -833,7 +853,9 @@
 
     def step_t(which, _):
         if which == 4:
-            ngrad_out[...] = (node_part + node_sum.total()).astype(bf16)
+            for h in range(2):
+                at = slice(h * (n // 2), (h + 1) * (n // 2))
+                ngrad_out[at, :] = (node_part[at, :] + node_sum.total(h)).astype(bf16)
             return
         result = sums_w[which].total()
         if which == 3:
@@ -855,7 +877,7 @@
             pb_n[...] = total.astype(bf16).reshape(pf.shape)
             for m in order:
                 for h in range(2):
-                    node_sum.y[m, h] = push(pb_n.at[zx(m), yp, h], yr_n.at[m, h], y_dev)
+                    node_sum.go(m, h)
         elif which < 9:
             node_sum.turn(k, which - 7)
         else:
@@ -909,6 +931,8 @@
         step_t,
         step_e,
         step_g,
+        step_v,
+        step_d,
     )
     for step in geo["tail"]:
         kind, which, k = decode(step, 100)
@@ -1000,6 +1024,8 @@
         vm((Z, 2, n // 2, D)),
         *[vm((Z - 1, 2, n // 2, D))] * 4,
         vm((2 * N, D)),
+        *[vm((n, D), f32)] * 3,
+        *[vm((n, D))] * 4,
         vm((4, 8, D // Z), f32),
         vm((3, 8, D // Z), f32),
         vm((Z, 8, D // Z), f32),

time: 80.5 us -> 78.6 us (0.976)
  Pallas kernels: 78.9 us -> 77.1 us
    pallas_call x1, Pallas kernels: 77.1 us -> 75.3 us  [on_device(): pl.pallas_call(functools.partial(layer_kernel, dict(GEO, dims=(Z, Y, X, C...]
where the time goes in v6:
time: 78.6 us; the launch traced here: 78.4 us
  Pallas kernels  77.1 us (98%)
  between operations  1.32 us (2%)
    pallas_call x1, Pallas kernels, on_device(): pl.pallas_call(functools.partial(layer_kernel, dict(GEO, dims=(Z, Y, X, C...  75.3 us
    pallas_call x1, Pallas kernels, on_device(): pl.pallas_call(deliver_kernel, out_shape=shapes, in_specs=[vmem] * 19, ou...  1.77 us

profile of v6, /device:TPU:0, one launch (start us, length us, event | category | flops | bytes accessed | tf_op | source)
XLA Modules:
  0.0 78.4 jit_solution(3448472471639329556)
XLA Ops:
  1.3 75.3 %layer.1 = (bf16[1024,512]{1,0:T(8,128)(2,1)S(1)}, bf16[64,512]{1,0:T(8,128)(2,1)S(1)}, bf16[1024,512]{1,0:T(8,128)(2,1)S(1)}, bf16[64,512]{1,0:T(8,128)(2,1)S(1...) custom-call(bf16[1024,512]{1,0:T(8,128)(2,1)} %bitcast.4, ...), custom_call_target="tpu_custom_call" | custom-call | tf_op jit(solution)/shard_map/layer/pallas_call | solution.py:1060
  76.6 1.8 %deliver.1 = (bf16[1,1024,512]{2,1,0:T(8,128)(2,1)}, bf16[1,64,512]{2,1,0:T(8,128)(2,1)}, bf16[1,1024,512]{2,1,0:T(8,128)(2,1)}, bf16[1,64,512]{2,1,0:T(8,128)(2...) custom-call(bf16[1024,512]{1,0:T(8,128)(2,1)S(1)} %get-tuple-element, ...), custom_call_target="tpu_custom_call" | custom-call | tf_op jit(solution)/shard_map/deliver/pallas_call | solution.py:1074

commit v7 on v6

--- a/solution.py
+++ b/solution.py
@@ -199,7 +199,7 @@
     "diagonal": (),
     "bits_a": True,
     "bits_n": True,
-    "bits_b": True,
+    "bits_b": False,
     "bits_d": True,
     "bits_agg": False,
     "bits_node": False,

time: 78.6 us -> 78.4 us (level)
  no operation moved by 1% of the time
where the time goes in v7:
time: 78.4 us; the launch traced here: 78.2 us
  Pallas kernels  76.9 us (98%)
  between operations  1.32 us (2%)
    pallas_call x1, Pallas kernels, on_device(): pl.pallas_call(functools.partial(layer_kernel, dict(GEO, dims=(Z, Y, X, C...  75.1 us
    pallas_call x1, Pallas kernels, on_device(): pl.pallas_call(deliver_kernel, out_shape=shapes, in_specs=[vmem] * 19, ou...  1.77 us

profile of v7, /device:TPU:0, one launch (start us, length us, event | category | flops | bytes accessed | tf_op | source)
XLA Modules:
  0.0 78.2 jit_solution(9172131626077908076)
XLA Ops:
  1.3 75.1 %layer.1 = (bf16[1024,512]{1,0:T(8,128)(2,1)S(1)}, bf16[64,512]{1,0:T(8,128)(2,1)S(1)}, bf16[1024,512]{1,0:T(8,128)(2,1)S(1)}, bf16[64,512]{1,0:T(8,128)(2,1)S(1...) custom-call(bf16[1024,512]{1,0:T(8,128)(2,1)} %bitcast.4, ...), custom_call_target="tpu_custom_call" | custom-call | tf_op jit(solution)/shard_map/layer/pallas_call | solution.py:1060
  76.4 1.8 %deliver.1 = (bf16[1,1024,512]{2,1,0:T(8,128)(2,1)}, bf16[1,64,512]{2,1,0:T(8,128)(2,1)}, bf16[1,1024,512]{2,1,0:T(8,128)(2,1)}, bf16[1,64,512]{2,1,0:T(8,128)(2...) custom-call(bf16[1024,512]{1,0:T(8,128)(2,1)S(1)} %get-tuple-element, ...), custom_call_target="tpu_custom_call" | custom-call | tf_op jit(solution)/shard_map/deliver/pallas_call | solution.py:1074
